TPU v7x, 32 devices: a whole 2x2x4 slice. The times are simulated.
32 devices in a mesh: sub: 8 (over z, x), blk: 4 (over y, core).
Axes of the slice: x: 2, y: 2, z: 4, core: 2. Of those that a mesh axis runs over, the one named last changes fastest.
Arguments:
- a_tiles: bfloat16 [768, 12, 128, 128], P(('sub', 'blk'))
- modes: bfloat16 [768, 16, 128], P(('sub', 'blk')), may hold values from -6 to 6
- col_tiles: int32 [768, 12], P(('sub', 'blk')), may hold values from 0 to 221, as said below
- fetch_list: int32 [32, 126], P(('sub', 'blk')), may hold values from 0 to 767, as said below
Outputs:
- prolong: bfloat16 [768, 12, 16, 128], P(('sub', 'blk'))
- coarse_diag: float32 [768, 256], P('sub')
Inputs may be any that keep to these rules, and one draw needn't show every extreme that they name: `col_tiles`: slot 0 of row tile t names t itself (its index within its group); the other slots name other tiles of the same group (values below 96) or 96 + h for entry h of the device's fetch list; every entry of a device's fetch list is named by some slot of that device's rows. `fetch_list`: A device's list is 7 blocks of 18 entries; each block names distinct tiles of one group other than the device's own, different blocks name different groups; tile i of group g has number g * 96 + i.
All inputs are finite; a program needn't handle non-finite values.
Results may differ from a plain program's by a relative error of at most 0.008.
Values may be sent and summed in bfloat16 or wider, within the bound.
No kernel may reach another device: no remote copies, remote signals or barrier semaphores. Data moves between devices by JAX's collectives and lax.ppermute only.
A program may use at most 64 MiB of HBM per device.

v0:
```python
import jax
import jax.numpy as jnp
from jax import lax
from jax.sharding import PartitionSpec as P

NEIGHBOURS = 26


damping = 2.0 / 3.0


def shards(a_tiles, modes, col_tiles, fetch_list):
    blk_count = lax.axis_size("blk")
    sub_count = lax.axis_size("sub")
    tile_dev = a_tiles.shape[0]
    slot_count = a_tiles.shape[1]
    tile_rows = a_tiles.shape[2]
    mode_count = modes.shape[1]
    group_size = tile_dev * blk_count
    ghost_count = fetch_list.shape[1]
    peer_count = min(NEIGHBOURS, sub_count - 1)
    per_peer = ghost_count // peer_count
    group_modes = lax.all_gather(modes, "blk", axis=0, tiled=True)
    wanted = fetch_list[0].reshape(peer_count, per_peer)
    owners = wanted[:, 0] // group_size
    within = wanted % group_size
    selector = (owners[:, None] == jnp.arange(sub_count, dtype=jnp.int32)[None, :]).astype(
        jnp.int32
    )
    requests = jnp.sum(selector[:, :, None] * (within + 1)[:, None, :], axis=0)
    received = lax.all_to_all(requests, "sub", split_axis=0, concat_axis=0, tiled=True)
    present = received > 0
    picked = group_modes[jnp.maximum(received - 1, 0)]
    picked = jnp.where(present[:, :, None, None], picked, jnp.zeros_like(picked))
    returned = lax.all_to_all(picked, "sub", split_axis=0, concat_axis=0, tiled=True)
    returned, received = (returned, received)
    ghosts = returned[owners].reshape(ghost_count, mode_count, tile_rows)
    lookup = jnp.concatenate([group_modes, ghosts], axis=0)
    gathered = lookup[col_tiles]
    product = jnp.einsum("tkrc,tkmc->tkmr", a_tiles, gathered, preferred_element_type=jnp.float32)
    inverse = 1.0 / jnp.diagonal(a_tiles[:, 0], axis1=1, axis2=2).astype(jnp.float32)
    leading = (jnp.arange(slot_count) == 0).astype(jnp.float32)
    prolong = (
        leading[None, :, None, None] * modes.astype(jnp.float32)[:, None]
        - damping * inverse[:, None, None, :] * product
    ).astype(jnp.bfloat16)
    partial_value = (
        jnp.einsum(
            "tkmr,tknr->tkmn", prolong.astype(jnp.float32), product, precision=lax.Precision.HIGHEST
        )
        / tile_rows
    )
    partial_value = partial_value.reshape(tile_dev * slot_count, mode_count * mode_count)
    segment = (
        col_tiles.reshape(-1)[:, None]
        == jnp.arange(group_size + ghost_count, dtype=jnp.int32)[None, :]
    ).astype(jnp.float32)
    slot_sums = jnp.dot(
        segment.T,
        partial_value,
        precision=lax.Precision.HIGHEST,
        preferred_element_type=jnp.float32,
    )
    ghost_sums = slot_sums[group_size:].reshape(peer_count, per_peer, mode_count * mode_count)
    outgoing = jnp.einsum(
        "jp,jmv->pmv", selector.astype(jnp.float32), ghost_sums, precision=lax.Precision.HIGHEST
    )
    incoming = lax.all_to_all(
        outgoing.astype(jnp.bfloat16), "sub", split_axis=0, concat_axis=0, tiled=True
    ).astype(outgoing.dtype)
    target = (
        received[:, :, None] == jnp.arange(1, group_size + 1, dtype=jnp.int32)[None, None, :]
    ).astype(jnp.float32)
    local_sum = slot_sums[:group_size] + jnp.einsum(
        "pmg,pmv->gv", target, incoming, precision=lax.Precision.HIGHEST
    )
    coarse_diag = lax.psum(local_sum.astype(jnp.bfloat16), "blk").astype(jnp.float32)
    return (prolong, coarse_diag)


def solution(mesh):
    in_specs = (
        P(("sub", "blk"), None, None, None),
        P(("sub", "blk"), None, None),
        P(("sub", "blk"), None),
        P(("sub", "blk"), None),
    )
    out_specs = (P(("sub", "blk"), None, None, None), P("sub", None))
    return jax.shard_map(shards, mesh=mesh, in_specs=in_specs, out_specs=out_specs, check_vma=False)
```

profile of v0, /device:TPU:0, one launch (start us, length us, event | category | flops | bytes accessed | tf_op | source)
XLA Modules:
  0.0 80.3 jit_solution(5689057946343639641)
XLA Ops:
  0.6 0.5 broadcast.175
  1.2 1.3 %reduce.11 = s32[126]{0:T(128)S(1)} reduce(s32[1,126]{1,0:T(1,128)} %param.7, s32[]{:T(128)} %broadcast.175), dimensions={0}, to_apply=%param.7.reduce_sub_computation.3 | reduce | bytes 1012 | tf_op args[3]
  2.8 0.7 multiply_reduce_fusion
  3.5 7.3 %all-to-all-start = ((s32[8,1,18]{2,1,0:T(1,128)}), s32[8,1,18]{2,1,0:T(1,128)S(1)}, u32[]{:S(2)}, u32[]{:S(2)}) async-start(s32[8,1,18]{2,1,0:T(1,128)} %bitcast.4), calls=%async_computation | async-start | bytes 8192 | tf_op jit(solution)/shard_map/all_to_all | solution.py:31
  10.8 6.7 %all_gather.3 = bf16[96,16,128]{2,1,0:T(8,128)(2,1)S(1)} all-gather(bf16[24,16,128]{2,1,0:T(8,128)(2,1)} %param.5), channel_id=1, replica_groups=mesh['sub'=8,'blk'=4] {'blk'}, dimensions={0}, use_global_device_ids=true | all-gather | bytes 491520 | tf_op jit(solution)/shard_map/all_gather | solution.py:23
  17.6 0.7 gather_fusion.1
  18.3 1.0 %broadcast_select_fusion = bf16[8,18,16,128]{3,2,1,0:T(8,128)(2,1)} fusion(bf16[8,18,16,128]{3,2,1,0:T(8,128)(2,1)S(1)} %bitcast.31, pred[8,18]{1,0:T(8,128)(4,1)S(1)} %broadcast_compare_fusion), kind=kLoop, calls=%fused_computation.11 | loop fusion | flops 294912 | bytes 1179792 | tf_op jit(solution)/shard_map/jit(_where)/select_n | solution.py:34
  19.4 6.0 %all-to-all-start.1 = ((bf16[8,18,16,128]{3,2,1,0:T(8,128)(2,1)}), bf16[8,18,16,128]{3,2,1,0:T(8,128)(2,1)S(1)}, u32[]{:S(2)}, u32[]{:S(2)}) async-start(bf16[8,18,16,128]{3,2,1,0:T(8,128)(2,1)} %broadcast_select_fusion), calls=%async_computation.1 | async-start | bytes 1179648 | tf_op jit(solution)/shard_map/all_to_all | solution.py:35
  25.4 3.2 %copy.42 = bf16[24,1,128,128]{0,3,2,1:T(8,128)(2,1)} copy(bf16[24,1,128,128]{3,2,1,0:T(8,128)(2,1)S(1)} %slice-done) | data formatting | bytes 1572864
  28.7 1.9 %gather_fusion = bf16[128,24]{1,0:T(8,128)(2,1)S(1)} fusion(bf16[24,128,128]{0,2,1:T(8,128)(2,1)} %bitcast.30, s32[128]{0:T(128)S(1)} %or_bitcast_fusion), kind=kCustom, calls=%fused_computation | custom fusion | bytes 13312 | tf_op jit(solution)/shard_map/jit(diagonal)/gather | solution.py:41
  31.1 10.7 %all-to-all-done.1 = bf16[8,18,16,128]{3,2,1,0:T(8,128)(2,1)S(1)} async-done(((bf16[8,18,16,128]{3,2,1,0:T(8,128)(2,1)}), bf16[8,18,16,128]{3,2,1,0:T(8,128)(2,1)S(1)}, u32[]{:S(2)}, u32[]{:S(2)}) %all-to-all-start.1) | async-done | bytes 589856 | tf_op jit(solution)/shard_map/all_to_all | solution.py:35
  41.8 0.6 gather_fusion.2
  42.5 1.8 %gather_fusion.3 = bf16[288,16,128]{2,1,0:T(8,128)(2,1)S(1)} fusion(bf16[222,16,128]{2,1,0:T(8,128)(2,1)S(1)} %pad_maximum_fusion, s32[1024]{0:T(1024)S(1)} %pad_clamp_fusion), kind=kCustom, calls=%fused_computation.3 | custom fusion | bytes 2360448 | tf_op jit(solution)/shard_map/gather | solution.py:39
  44.4 7.5 %subtract_convert_fusion = (bf16[24,12,16,128]{3,2,1,0:T(8,128)(2,1)S(1)}, f32[24,12,16,128]{3,2,1,0:T(8,128)S(1)}) fusion(f32[24,128]{1,0:T(8,128)S(1)} %multiply_bitcast_fusion, f32[24,16,128]{2,1,0:T(8,128)S(1)} %convert_element_type.44, f32[12]{0:T(128)S(1)} %compare_convert_fusion, bf16[24,12,16,128]{3,2,1,0:T(8,128)(2,1)S(1)} %bitcast.29, ...), kind=kOutput, calls=%fused_computation.4 | convolution fusion | flops 153354240 | bytes 14364720 | tf_op jit(solution)/shard_map/tkrc,tkmc->tkmr/dot_general | solution.py:40
  51.8 2.0 %convolution_multiply_fusion = f32[24,12,16,16]{3,2,1,0:T(8,128)S(1)} fusion(bf16[24,12,16,128]{3,2,1,0:T(8,128)(2,1)S(1)} %get-tuple-element.4, f32[24,12,16,128]{3,2,1,0:T(8,128)S(1)} %get-tuple-element.5), kind=kOutput, calls=%fused_computation.5 | convolution fusion | flops 113319936 | bytes 3833856 | tf_op jit(solution)/shard_map/tkmr,tknr->tkmn/dot_general | solution.py:48
  53.8 1.7 %reshape.91 = f32[288,256]{1,0:T(8,128)} reshape(f32[24,12,16,16]{3,2,1,0:T(8,128)S(1)} %convolution_multiply_fusion) | data formatting | bytes 589824 | tf_op jit(solution)/shard_map/reshape | solution.py:53
  55.5 1.5 %fusion.2 = f32[222,256]{1,0:T(8,128)S(1)} fusion(f32[288,256]{1,0:T(8,128)} %reshape.91, s32[288]{0:T(512)S(1)} %eq.58), kind=kOutput, calls=%fused_computation.13 | convolution fusion | flops 196475328 | bytes 523392 | tf_op jit(solution)/shard_map/dot_general | solution.py:58
  57.1 0.3 convolution_convert_fusion
  57.4 0.7 copy.41
  58.0 3.6 %all-to-all-start.2 = ((bf16[8,18,256]{2,1,0:T(8,128)(2,1)}), bf16[8,18,256]{2,1,0:T(8,128)(2,1)S(1)}, u32[]{:S(2)}, u32[]{:S(2)}) async-start(bf16[8,18,256]{2,1,0:T(8,128)(2,1)} %copy.41), calls=%async_computation.2 | async-start | bytes 196608 | tf_op jit(solution)/shard_map/all_to_all | solution.py:68
  61.7 7.1 %all-to-all-done.2 = bf16[8,18,256]{2,1,0:T(8,128)(2,1)S(1)} async-done(((bf16[8,18,256]{2,1,0:T(8,128)(2,1)}), bf16[8,18,256]{2,1,0:T(8,128)(2,1)S(1)}, u32[]{:S(2)}, u32[]{:S(2)}) %all-to-all-start.2) | async-done | bytes 73760 | tf_op jit(solution)/shard_map/all_to_all | solution.py:68
  68.8 0.3 fusion.1
  69.1 10.5 %psum.7 = bf16[96,256]{1,0:T(8,128)(2,1)S(1)} all-reduce(bf16[96,256]{1,0:T(8,128)(2,1)S(1)} %fusion.1), channel_id=1, replica_groups=mesh['sub'=8,'blk'=4] {'blk'}, use_global_device_ids=true, to_apply=%region_1.2 | all-reduce | flops 24576 | bytes 98304 | tf_op jit(solution)/shard_map/psum | solution.py:77
  79.6 0.6 convert_element_type.51
  (34 shorter events, 1.1 us)
Async XLA Ops:
  0.6 24.7 %copy-start.1 = (bf16[24,16,128]{2,1,0:T(8,128)(2,1)S(1)}, bf16[24,16,128]{2,1,0:T(8,128)(2,1)}, u32[]{:S(2)}) copy-start(bf16[24,16,128]{2,1,0:T(8,128)(2,1)} %param.5) | copy-start | bytes 294916
  3.5 14.0 %all-to-all-start = ((s32[8,1,18]{2,1,0:T(1,128)}), s32[8,1,18]{2,1,0:T(1,128)S(1)}, u32[]{:S(2)}, u32[]{:S(2)}) async-start(s32[8,1,18]{2,1,0:T(1,128)} %bitcast.4), calls=%async_computation | async-start | bytes 8192 | tf_op jit(solution)/shard_map/all_to_all | solution.py:31
  18.3 7.1 %slice-start = ((bf16[24,12,128,128]{3,2,1,0:T(8,128)(2,1)}), bf16[24,1,128,128]{3,2,1,0:T(8,128)(2,1)S(1)}, s32[]{:S(2)}) async-start(bf16[24,12,128,128]{3,2,1,0:T(8,128)(2,1)} %param.4), calls=%async_computation.3 | async-start | bytes 1572864 | tf_op jit(solution)/shard_map/slice | solution.py:41
  19.4 22.4 %all-to-all-start.1 = ((bf16[8,18,16,128]{3,2,1,0:T(8,128)(2,1)}), bf16[8,18,16,128]{3,2,1,0:T(8,128)(2,1)S(1)}, u32[]{:S(2)}, u32[]{:S(2)}) async-start(bf16[8,18,16,128]{3,2,1,0:T(8,128)(2,1)} %broadcast_select_fusion), calls=%async_computation.1 | async-start | bytes 1179648 | tf_op jit(solution)/shard_map/all_to_all | solution.py:35
  25.4 5.3 %copy-start.2 = (s32[24,12]{0,1:T(8,128)S(1)}, s32[24,12]{0,1:T(8,128)}, u32[]{:S(2)}) copy-start(s32[24,12]{0,1:T(8,128)} %param.6) | copy-start | bytes 3460
  51.8 2.0 %copy-start = (bf16[24,12,16,128]{3,2,1,0:T(8,128)(2,1)}, bf16[24,12,16,128]{3,2,1,0:T(8,128)(2,1)S(1)}, u32[]{:S(2)}) copy-start(bf16[24,12,16,128]{3,2,1,0:T(8,128)(2,1)S(1)} %get-tuple-element.4) | copy-start | bytes 3538948
  58.0 10.8 %all-to-all-start.2 = ((bf16[8,18,256]{2,1,0:T(8,128)(2,1)}), bf16[8,18,256]{2,1,0:T(8,128)(2,1)S(1)}, u32[]{:S(2)}, u32[]{:S(2)}) async-start(bf16[8,18,256]{2,1,0:T(8,128)(2,1)} %copy.41), calls=%async_computation.2 | async-start | bytes 196608 | tf_op jit(solution)/shard_map/all_to_all | solution.py:68
where the time goes:
time: 80.7 us; the launch traced here: 80.3 us
  waiting for transfers between devices  17.8 us (22%)
  blocking collectives  17.2 us (21%)
  starting transfers between devices  16.9 us (21%)
  local copies, waits for them, and re-layouts  12 us (15%)
  matrix products  11.6 us (14%)
  other arithmetic  4.03 us (5%)
  between operations  0.83 us (1%)
    all_to_all x1, waiting for transfers between devices, shards(): lax.all_to_all(picked, 'sub', split_axis=0, concat_axis=0, tiled=True)  10.7 us
    psum x1, blocking collectives, shards(): lax.psum(local_sum.astype(jnp.bfloat16), 'blk').astype(jnp.float32)  10.5 us
    dot_general x1, matrix products, shards(): jnp.einsum('tkrc,tkmc->tkmr', a_tiles, gathered, preferred_element_type=j...  7.47 us
    all_to_all x1, starting transfers between devices, shards(): lax.all_to_all(requests, 'sub', split_axis=0, concat_axis=0, tiled=True)  7.28 us
    all_to_all x1, waiting for transfers between devices, shards(): lax.all_to_all(outgoing.astype(jnp.bfloat16), 'sub', split_axis=0, concat...  7.12 us
    all_gather x1, blocking collectives, shards(): group_modes = lax.all_gather(modes, 'blk', axis=0, tiled=True)  6.68 us
    all_to_all x1, starting transfers between devices, shards(): lax.all_to_all(picked, 'sub', split_axis=0, concat_axis=0, tiled=True)  5.99 us
    unnamed x9, local copies, waits for them, and re-layouts  3.84 us
  transfers between devices with their start and end apart: 3, of which 2 were waited for; matrix products, arithmetic and copies ran while one was open for 7% of the time, Pallas kernels for 0%

commit v1 on v0

v1 whole, which is shorter than its diff:
```python
import functools

import jax
import jax.numpy as jnp
from jax import lax
from jax.experimental import pallas as pl
from jax.experimental.pallas import tpu as pltpu
from jax.sharding import PartitionSpec as P

NEIGHBOURS = 26
LANES = 128
BATCH = 8

damping = 2.0 / 3.0

VMEM = pl.BlockSpec(memory_space=pltpu.VMEM)
SMEM = pl.BlockSpec(memory_space=pltpu.SMEM)
PARAMS = pltpu.CompilerParams(vmem_limit_bytes=8 << 20)
NT = (((1,), (1,)), ((), ()))


def xor_permute(x, axis, bit):
    count = lax.axis_size(axis)
    return lax.ppermute(x, axis, [(i, i ^ bit) for i in range(count)])


def flatten_rows(load, rows, modes):
    per_vector = LANES // modes
    lane_block = lax.broadcasted_iota(jnp.int32, (rows, LANES), 1) // modes
    halves = []
    for half in range(modes // per_vector):
        total = jnp.zeros((rows, LANES), jnp.float32)
        for place in range(per_vector):
            value = load(half * per_vector + place)
            if place:
                value = pltpu.roll(value, place * modes, 1)
            total = jnp.where(lane_block == place, value, total)
        halves.append(total)
    return halves


def one_hot_sum(one_hot, value):
    high = value.astype(jnp.bfloat16)
    low = (value - high.astype(jnp.float32)).astype(jnp.bfloat16)
    return jnp.dot(one_hot, high, preferred_element_type=jnp.float32) + jnp.dot(
        one_hot, low, preferred_element_type=jnp.float32
    )


def pick_kernel(count, place_ref, table_ref, far_ref, *out_refs):
    for peer, out_ref in enumerate(out_refs):

        @pl.loop(0, count, unroll=2)
        def _(i):
            out_ref[i] = table_ref[place_ref[peer, i]]
            out_ref[count + i] = far_ref[place_ref[peer, count + i]]


def own_kernel(
    slots, own_place, source, cols_ref, table_ref, a_hbm,
    prolong_ref, weight_ref, sums_ref, lists_ref, counts_ref, a_ref, blocks_ref, arrived,
):
    tile_dev = weight_ref.shape[0]
    mode_count, tile_rows = table_ref.shape[1:]
    pair = 2
    per_step = pair * slots
    diagonal = lax.broadcasted_iota(jnp.int32, (tile_rows, tile_rows), 0) == lax.broadcasted_iota(
        jnp.int32, (tile_rows, tile_rows), 1
    )

    def fetch(step):
        part = pl.ds(step * per_step, per_step)
        return pltpu.make_async_copy(a_hbm.at[part], a_ref.at[part], arrived.at[step])

    @pl.loop(0, tile_dev // pair)
    def _(step):
        fetch(step).start()

    @pl.loop(0, tile_dev // pair)
    def _(step):
        fetch(step).wait()
        stages = []
        for i in range(pair):
            tile = step * pair + i
            first = a_ref[tile * slots].astype(jnp.float32)
            entries = jnp.sum(jnp.where(diagonal, first, 0.0), axis=0, keepdims=True)
            weight = damping * (1.0 / entries)
            weight_ref[pl.ds(tile, 1), :] = weight
            for k in range(slots):
                slot = tile * slots + k
                place = own_place[slot]
                picked = table_ref[jnp.maximum(place, 0)]
                picked = jnp.where(place >= 0, picked, jnp.zeros_like(picked))
                product = lax.dot_general(picked, a_ref[slot], NT, preferred_element_type=jnp.float32)
                smooth = -(weight * product)
                if k == 0:
                    smooth = picked.astype(jnp.float32) + smooth
                smooth = smooth.astype(jnp.bfloat16)
                prolong_ref[slot] = smooth
                stages.append((smooth, product.astype(jnp.bfloat16)))
        for b in range(per_step // BATCH):
            part = stages[b * BATCH : (b + 1) * BATCH]
            block = lax.dot_general(
                jnp.concatenate([s for s, _ in part], axis=0),
                jnp.concatenate([q for _, q in part], axis=0),
                NT,
                preferred_element_type=jnp.float32,
            )
            row = (step * (per_step // BATCH) + b) * BATCH * mode_count
            row = pl.multiple_of(row, BATCH * mode_count)
            for j in range(BATCH):
                value = block[j * mode_count : (j + 1) * mode_count]
                if j:
                    value = pltpu.roll(value, LANES - j * mode_count, 1)
                blocks_ref[pl.ds(row + j * mode_count, mode_count), :] = value

    source_count = counts_ref.shape[0]
    for s in range(source_count):
        counts_ref[s] = 0

    @pl.loop(0, tile_dev * slots)
    def _(slot):
        s = source[slot]

        @pl.when(s >= 0)
        def _():
            at = counts_ref[s]
            lists_ref[s, at] = slot
            counts_ref[s] = at + 1

    total = tile_dev * slots
    halves = flatten_rows(
        lambda m: blocks_ref[pl.ds(m, total, stride=mode_count), :], total, mode_count
    )
    group_size = sums_ref.shape[0]
    one_hot = (
        lax.broadcasted_iota(jnp.int32, (group_size, total), 0) == cols_ref[...]
    ).astype(jnp.bfloat16)
    for half, value in enumerate(halves):
        result = one_hot_sum(one_hot, value) * (1.0 / tile_rows)
        sums_ref[:, half * LANES : (half + 1) * LANES] = result.astype(jnp.bfloat16)


def ghost_kernel(
    slots, pitch, entry, lists_ref, counts_ref, target_ref, index_ref, a_ref, weight_ref, old_ref,
    *refs,
):
    sources = refs[:-3]
    prolong_ref, out_ref, blocks_ref = refs[-3:]
    mode_count, tile_rows = sources[0].shape[1:]
    total = a_ref.shape[0]
    blocks_ref[...] = jnp.zeros_like(blocks_ref)

    for s, table_ref in enumerate(sources):
        count = counts_ref[s]

        @pl.loop(0, (count + BATCH - 1) // BATCH)
        def _(step):
            stages = []
            for i in range(BATCH):
                slot = lists_ref[s, jnp.minimum(step * BATCH + i, count - 1)]
                picked = table_ref[entry[slot]]
                product = lax.dot_general(picked, a_ref[slot], NT, preferred_element_type=jnp.float32)
                weight = weight_ref[pl.ds(slot // slots, 1), :]
                smooth = (-(weight * product)).astype(jnp.bfloat16)
                prolong_ref[slot] = smooth
                stages.append((slot, smooth, product.astype(jnp.bfloat16)))
            for slot, smooth, product in stages:
                block = lax.dot_general(smooth, product, NT, preferred_element_type=jnp.float32)
                row = pl.multiple_of(slot * mode_count, mode_count)
                blocks_ref[pl.ds(row, mode_count), 0:mode_count] = block

    halves = flatten_rows(
        lambda m: blocks_ref[pl.ds(m, total, stride=mode_count), :], total, mode_count
    )
    groups, _, rows, _ = out_ref.shape
    one_hot = (
        lax.broadcasted_iota(jnp.int32, (groups * rows, total), 0) == target_ref[...]
    ).astype(jnp.bfloat16)
    row_place = lax.broadcasted_iota(jnp.int32, (groups, rows, LANES), 1)
    for half, value in enumerate(halves):
        result = one_hot_sum(one_hot, value) * (1.0 / tile_rows)
        result = result.reshape(groups, rows, LANES)
        result = jnp.where(row_place == pitch, index_ref[:, :, half * LANES : (half + 1) * LANES], result)
        result = result.astype(jnp.bfloat16)
        for copy in range(out_ref.shape[1]):
            out_ref[:, copy, :, half * LANES : (half + 1) * LANES] = result


def target_kernel(pitch, incoming_ref, out_ref):
    senders, rows, width = incoming_ref.shape
    group_size = out_ref.shape[0]
    tile = lax.broadcasted_iota(jnp.int32, (group_size, rows), 0)
    total = jnp.zeros((group_size, width), jnp.float32)
    for sender in range(senders):
        value = incoming_ref[sender]
        wanted = value[pitch : pitch + 1, :rows].astype(jnp.float32).astype(jnp.int32)
        one_hot = (tile == wanted).astype(jnp.bfloat16)
        total = total + jnp.dot(one_hot, value, preferred_element_type=jnp.float32)
    out_ref[...] = total.astype(jnp.bfloat16)


def shards(a_tiles, modes, col_tiles, fetch_list):
    blk_count = lax.axis_size("blk")
    sub_count = lax.axis_size("sub")
    tile_dev, slot_count, tile_rows = a_tiles.shape[:3]
    mode_count = modes.shape[1]
    width = mode_count * mode_count
    group_size = tile_dev * blk_count
    ghost_count = fetch_list.shape[1]
    peer_count = min(NEIGHBOURS, sub_count - 1)
    per_peer = ghost_count // peer_count
    slot_total = tile_dev * slot_count
    half = sub_count // 2
    blk_half = blk_count // 2
    me = lax.axis_index("sub")
    lane = lax.axis_index("blk")

    far = xor_permute(modes, "sub", half)
    tables = []
    bits = []
    bit = blk_half
    own_part, far_part = modes[None], far[None]
    while bit:
        own_part = jnp.concatenate([own_part, xor_permute(own_part, "blk", bit)], axis=0)
        far_part = jnp.concatenate([far_part, xor_permute(far_part, "blk", bit)], axis=0)
        bits.append(bit)
        bit //= 2
    own_table = own_part.reshape(group_size, mode_count, tile_rows)
    far_table = far_part.reshape(group_size, mode_count, tile_rows)

    def place_of(within):
        relative = (within // tile_dev) ^ lane
        order = jnp.zeros_like(relative)
        for i, b in enumerate(bits):
            order = order + jnp.where((relative & b) != 0, 1 << i, 0)
        return order * tile_dev + within % tile_dev

    fetched = fetch_list[0]
    places = []
    for peer in range(1, half):
        theirs = xor_permute(fetch_list, "sub", peer)[0].reshape(peer_count, per_peer)
        owner = theirs[:, :1] // group_size
        wanted = theirs % group_size
        near = jnp.sum(jnp.where(owner == me, wanted, 0), axis=0)
        away = jnp.sum(jnp.where(owner == (me ^ half), wanted, 0), axis=0)
        places.append(place_of(jnp.concatenate([near, away])))
    places = jnp.stack(places)

    picks = pl.pallas_call(
        functools.partial(pick_kernel, per_peer),
        out_shape=[jax.ShapeDtypeStruct((2 * per_peer, mode_count, tile_rows), modes.dtype)] * (half - 1),
        in_specs=[SMEM, VMEM, VMEM],
        out_specs=[VMEM] * (half - 1),
        name="pick",
        compiler_params=PARAMS,
    )(places, own_table, far_table)
    received = [xor_permute(picks[peer - 1], "sub", peer) for peer in range(1, half)]

    cols = col_tiles.reshape(slot_total)
    ghost = cols - group_size
    ghost_iota = jnp.arange(ghost_count, dtype=jnp.int32)
    match = ghost[:, None] == ghost_iota[None, :]
    owner_of = fetched // group_size
    apart = owner_of ^ me
    low = apart & (half - 1)
    within = fetched % group_size
    member = ghost_iota % per_peer
    entry_of = jnp.where(low == 0, place_of(within), jnp.where(apart >= half, per_peer, 0) + member)
    rows = -(-(per_peer + 1) // 8) * 8
    row_of = owner_of * rows + member
    packed = (low * group_size * 2 + entry_of) * (sub_count * rows) + row_of
    packed = jnp.sum(jnp.where(match, packed[None, :], 0), axis=1)
    is_ghost = ghost >= 0
    target = jnp.where(is_ghost, packed % (sub_count * rows), -1)
    packed = packed // (sub_count * rows)
    source = jnp.where(is_ghost, packed // (2 * group_size), -1)
    entry = packed % (2 * group_size)
    own_place = jnp.where(is_ghost, -1, place_of(cols))
    index_rows = jnp.sum(
        jnp.where(
            owner_of.reshape(peer_count, per_peer)[:, :1] == jnp.arange(sub_count, dtype=jnp.int32)[None, :],
            1, 0,
        )[:, :, None]
        * (within.reshape(peer_count, per_peer) + 1)[:, None, :],
        axis=0,
    ) - 1
    index_rows = jnp.pad(index_rows, ((0, 0), (0, width - per_peer)), constant_values=-1)
    index_rows = index_rows.astype(jnp.float32).reshape(sub_count, 1, width)

    tiles = a_tiles.reshape(slot_total, tile_rows, tile_rows)
    tiles = pltpu.with_memory_space_constraint(tiles, pltpu.HBM)
    prolong, weight, own_sums, lists, counts, tiles = pl.pallas_call(
        functools.partial(own_kernel, slot_count),
        out_shape=[
            pltpu.VMEM((slot_total, mode_count, tile_rows), jnp.bfloat16),
            jax.ShapeDtypeStruct((tile_dev, tile_rows), jnp.float32),
            jax.ShapeDtypeStruct((group_size, width), jnp.bfloat16),
            jax.ShapeDtypeStruct((half, slot_total), jnp.int32),
            jax.ShapeDtypeStruct((half,), jnp.int32),
            pltpu.VMEM((slot_total, tile_rows, tile_rows), jnp.bfloat16),
        ],
        in_specs=[SMEM, SMEM, VMEM, VMEM, pl.BlockSpec(memory_space=pltpu.HBM)],
        out_specs=[VMEM, VMEM, VMEM, SMEM, SMEM, VMEM],
        scratch_shapes=[
            pltpu.VMEM((slot_total * mode_count, LANES), jnp.float32),
            pltpu.SemaphoreType.DMA((tile_dev // 2,)),
        ],
        name="own",
        compiler_params=PARAMS,
    )(own_place, source, cols[None, :], own_table, tiles)

    prolong = pltpu.with_memory_space_constraint(prolong, pltpu.VMEM)
    tiles = pltpu.with_memory_space_constraint(tiles, pltpu.VMEM)
    own_total = own_sums
    bit = blk_half
    while bit:
        other = xor_permute(own_total, "blk", bit)
        own_total = own_total.astype(jnp.float32) + other.astype(jnp.float32)
        bit //= 2
        if bit:
            own_total = own_total.astype(jnp.bfloat16)

    prolong, outgoing = pl.pallas_call(
        functools.partial(ghost_kernel, slot_count, per_peer),
        out_shape=[
            pltpu.VMEM((slot_total, mode_count, tile_rows), jnp.bfloat16),
            jax.ShapeDtypeStruct((sub_count, blk_half, rows, width), jnp.bfloat16),
        ],
        in_specs=[SMEM, SMEM, SMEM, VMEM, VMEM, VMEM, VMEM, VMEM] + [VMEM] * half,
        out_specs=[VMEM, VMEM],
        input_output_aliases={7: 0},
        scratch_shapes=[pltpu.VMEM((slot_total * mode_count, LANES), jnp.float32)],
        name="ghost",
        compiler_params=PARAMS,
    )(entry, lists, counts, target[None, :], index_rows, tiles, weight, prolong, far_table, *received)

    groups = [
        [s * blk_count + high * 2 + core for s in range(sub_count) for high in range(blk_half)]
        for core in range(2)
    ]
    incoming = lax.all_to_all(
        outgoing.reshape(sub_count * blk_half, rows, width),
        ("sub", "blk"), split_axis=0, concat_axis=0, axis_index_groups=groups, tiled=True,
    )
    arrived = pl.pallas_call(
        functools.partial(target_kernel, per_peer),
        out_shape=jax.ShapeDtypeStruct((group_size, width), jnp.bfloat16),
        in_specs=[VMEM],
        out_specs=VMEM,
        name="target",
        compiler_params=PARAMS,
    )(incoming)
    other = xor_permute(arrived, "blk", 1)
    coarse_diag = own_total + (arrived.astype(jnp.float32) + other.astype(jnp.float32))
    return prolong.reshape(tile_dev, slot_count, mode_count, tile_rows), coarse_diag


def solution(mesh):
    in_specs = (
        P(("sub", "blk"), None, None, None),
        P(("sub", "blk"), None, None),
        P(("sub", "blk"), None),
        P(("sub", "blk"), None),
    )
    out_specs = (P(("sub", "blk"), None, None, None), P("sub", None))
    return jax.shard_map(shards, mesh=mesh, in_specs=in_specs, out_specs=out_specs, check_vma=False)
```

time: 80.7 us -> 71.8 us (0.89)
  Pallas kernels: 0 us -> 27.4 us
  blocking collectives: 17.2 us -> 0 us
  matrix products: 11.6 us -> 0 us
  local copies, waits for them, and re-layouts: 12 us -> 3.75 us
  waiting for transfers between devices: 17.8 us -> 10.7 us
  other arithmetic: 4.03 us -> 9.18 us
  starting transfers between devices: 16.9 us -> 19.4 us
    pallas_call x0 -> x4, Pallas kernels: none -> 27.4 us  [the longest x1 16.9 us: shards(): pl.pallas_call(functools.partial(own_kernel, slot_count), out_shape=[pltp...]
    ppermute x0 -> x14, starting transfers between devices: none -> 15.5 us  [xor_permute(): return lax.ppermute(x, axis, [(i, i ^ bit) for i in range(count)])]
    all_to_all x3 -> x1, waiting for transfers between devices: 17.8 us -> 3.37 us  [shards(): lax.all_to_all(outgoing.reshape(sub_count * blk_half, rows, width), ('sub...]
    all_to_all x3 -> x1, starting transfers between devices: 16.9 us -> 3.88 us  [shards(): lax.all_to_all(outgoing.reshape(sub_count * blk_half, rows, width), ('sub...]
    dot_general x5 -> x0, matrix products: 11.6 us -> none  [the longest x1 7.47 us: shards(): jnp.einsum('tkrc,tkmc->tkmr', a_tiles, gathered, preferred_element_type=j...]
    psum x1 -> x0, blocking collectives: 10.5 us -> none  [shards(): lax.psum(local_sum.astype(jnp.bfloat16), 'blk').astype(jnp.float32)]
    ppermute x0 -> x14, waiting for transfers between devices: none -> 7.35 us  [xor_permute(): return lax.ppermute(x, axis, [(i, i ^ bit) for i in range(count)])]
    all_gather x1 -> x0, blocking collectives: 6.68 us -> none  [shards(): group_modes = lax.all_gather(modes, 'blk', axis=0, tiled=True)]
  transfers between devices with their start and end apart: 3 -> 15, of which waited for: 2 -> 5; matrix products, arithmetic and copies ran while one was open for 7% -> 17% of each run, Pallas kernels for 0% -> 24%
where the time goes in v1:
time: 71.8 us; the launch traced here: 71.3 us
  Pallas kernels  27.4 us (38%)
  starting transfers between devices  19.4 us (27%)
  waiting for transfers between devices  10.7 us (15%)
  other arithmetic  9.18 us (13%)
  local copies, waits for them, and re-layouts  3.75 us (5%)
  between operations  0.87 us (1%)
    pallas_call x1, Pallas kernels, shards(): pl.pallas_call(functools.partial(own_kernel, slot_count), out_shape=[pltp...  16.9 us
    ppermute x14, starting transfers between devices, xor_permute(): return lax.ppermute(x, axis, [(i, i ^ bit) for i in range(count)])  15.5 us
    pallas_call x1, Pallas kernels, shards(): pl.pallas_call(functools.partial(ghost_kernel, slot_count, per_peer), out...  9.34 us
    ppermute x14, waiting for transfers between devices, xor_permute(): return lax.ppermute(x, axis, [(i, i ^ bit) for i in range(count)])  7.35 us
    all_to_all x1, starting transfers between devices, shards(): lax.all_to_all(outgoing.reshape(sub_count * blk_half, rows, width), ('sub...  3.88 us
    all_to_all x1, waiting for transfers between devices, shards(): lax.all_to_all(outgoing.reshape(sub_count * blk_half, rows, width), ('sub...  3.37 us
    ppermute x3, other arithmetic, xor_permute(): return lax.ppermute(x, axis, [(i, i ^ bit) for i in range(count)])  2 us
    unnamed x4, local copies, waits for them, and re-layouts  1.8 us
  transfers between devices with their start and end apart: 15, of which 5 were waited for; matrix products, arithmetic and copies ran while one was open for 17% of the time, Pallas kernels for 24%

profile of v1, /device:TPU:0, one launch (start us, length us, event | category | flops | bytes accessed | tf_op | source)
XLA Modules:
  0.0 71.3 jit_solution(16136797076170749228)
XLA Ops:
  0.6 3.0 %collective-permute-start.5 = (s32[1,126]{1,0:T(1,128)}, s32[1,126]{1,0:T(1,128)S(1)}, u32[]{:S(2)}, u32[]{:S(2)}) collective-permute-start(s32[1,126]{1,0:T(1,128)} %param.7), channel_id=1, source_target_pairs={{0,4},{4,0},{8,12},{12,8},{16,20},{20,16},{24,28},{28,24},{1,5},{5... | collective-permute-start | bytes 1520 | tf_op jit(solution)/shard_map/ppermute | solution.py:24
  3.7 1.5 %collective-permute-start.7 = (s32[1,126]{1,0:T(1,128)}, s32[1,126]{1,0:T(1,128)S(1)}, u32[]{:S(2)}, u32[]{:S(2)}) collective-permute-start(s32[1,126]{1,0:T(1,128)} %param.7), channel_id=1, source_target_pairs={{0,12},{4,8},{8,4},{12,0},{16,28},{20,24},{24,20},{28,16},{1,13},{... | collective-permute-start | bytes 1520 | tf_op jit(solution)/shard_map/ppermute | solution.py:24
  5.3 3.0 %collective-permute-start.2 = (bf16[24,16,128]{2,1,0:T(8,128)(2,1)}, bf16[24,16,128]{2,1,0:T(8,128)(2,1)S(1)}, u32[]{:S(2)}, u32[]{:S(2)}) collective-permute-start(bf16[24,16,128]{2,1,0:T(8,128)(2,1)} %param.5), channel_id=1, source_target_pairs={{0,16},{4,20},{8,24},{12,28},{16,0},{20,4},{24,8},{28,12},{1,17},{... | collective-permute-start | bytes 294920 | tf_op jit(solution)/shard_map/ppermute | solution.py:24
  8.3 1.5 %collective-permute-start = (bf16[1,24,16,128]{3,2,1,0:T(8,128)(2,1)}, bf16[1,24,16,128]{3,2,1,0:T(8,128)(2,1)S(1)}, u32[]{:S(2)}, u32[]{:S(2)}) collective-permute-start(bf16[1,24,16,128]{3,2,1,0:T(8,128)(2,1)} %bitcast.21), channel_id=1, source_target_pairs={{0,2},{1,3},{2,0},{3,1},{4,6},{5,7},{6,4},{7,5},{8,10},{9,11},{10,... | collective-permute-start | bytes 294920 | tf_op jit(solution)/shard_map/ppermute | solution.py:24
  9.8 0.7 compare_reduce_fusion.6
  10.5 0.7 sign_compare_fusion
  11.2 0.7 broadcast_divide_fusion
  12.5 1.3 %fusion.20 = (s32[126]{0:T(128)S(1)}, s32[1,126]{1,0:T(1,128)S(1)}, s32[126]{0:T(128)S(1)}) fusion(s32[]{:T(128)} %broadcast.851, s32[1,126]{1,0:T(1,128)} %param.7), kind=kLoop, calls=%fused_computation.107 | loop fusion | flops 252 | bytes 2020 | tf_op jit(solution)/shard_map/jit(floor_divide)/div | solution.py:264
  15.0 0.7 add_bitcast_fusion
  16.0 0.8 %copy.17 = s32[24,12]{1,0:T(8,128)S(1)} copy(s32[24,12]{0,1:T(8,128)} %param.6) | data formatting | bytes 2304 | tf_op args[2]
  17.6 0.7 reduce.35
  20.7 0.9 %pad_maximum_fusion.2 = bf16[2,24,16,128]{3,2,1,0:T(8,128)(2,1)S(1)} fusion(bf16[1,24,16,128]{3,2,1,0:T(8,128)(2,1)S(1)} %collective-permute-done, bf16[1,24,16,128]{3,2,1,0:T(8,128)(2,1)} %bitcast.22), kind=kLoop, calls=%fused_computation.2 | loop fusion | flops 98304 | bytes 393216 | tf_op jit(solution)/shard_map/concatenate | solution.py:225
  21.7 3.1 %collective-permute-done.3 = bf16[1,24,16,128]{3,2,1,0:T(8,128)(2,1)S(1)} collective-permute-done((bf16[1,24,16,128]{3,2,1,0:T(8,128)(2,1)S(1)}, bf16[1,24,16,128]{3,2,1,0:T(8,128)(2,1)S(1)}, u32[]{:S(2)}, u32[]{:S(2)}) %collective-permute-start.3) | collective-permute-done | bytes 98336 | tf_op jit(solution)/shard_map/ppermute | solution.py:24
  25.0 1.3 %collective-permute-done.4 = bf16[2,24,16,128]{3,2,1,0:T(8,128)(2,1)S(1)} collective-permute-done((bf16[2,24,16,128]{3,2,1,0:T(8,128)(2,1)S(1)}, bf16[2,24,16,128]{3,2,1,0:T(8,128)(2,1)S(1)}, u32[]{:S(2)}, u32[]{:S(2)}) %collective-permute-start.4) | collective-permute-done | bytes 196640 | tf_op jit(solution)/shard_map/ppermute | solution.py:24
  26.3 0.9 %pick.1 = (bf16[36,16,128]{2,1,0:T(8,128)(2,1)S(1)}, bf16[36,16,128]{2,1,0:T(8,128)(2,1)S(1)}, bf16[36,16,128]{2,1,0:T(8,128)(2,1)S(1)}) custom-call(s32[3,36]{1,0:T(4,128)S(1)} %pad_add_fusion.place_ref, bf16[96,16,128]{2,1,0:T(8,128)(2,1)S(1)} %bitcast.18, bf16[96,16,128]{2,1,0:T(8,128)(2,1)S(1)} %bitcast.16), custom_call_target="tpu_custom_call" | custom-call | tf_op jit(solution)/shard_map/pick/pallas_call | solution.py:250
  27.2 1.6 %collective-permute-start.8 = (bf16[36,16,128]{2,1,0:T(8,128)(2,1)S(1)}, bf16[36,16,128]{2,1,0:T(8,128)(2,1)S(1)}, u32[]{:S(2)}, u32[]{:S(2)}) collective-permute-start(bf16[36,16,128]{2,1,0:T(8,128)(2,1)S(1)} %get-tuple-element.18), channel_id=1, source_target_pairs={{0,4},{4,0},{8,12},{12,8},{16,20},{20,16},{24,28},{28,24},{1,5},{5... | collective-permute-start | bytes 442376 | tf_op jit(solution)/shard_map/ppermute | solution.py:24
  28.8 1.6 %collective-permute-start.9 = (bf16[36,16,128]{2,1,0:T(8,128)(2,1)S(1)}, bf16[36,16,128]{2,1,0:T(8,128)(2,1)S(1)}, u32[]{:S(2)}, u32[]{:S(2)}) collective-permute-start(bf16[36,16,128]{2,1,0:T(8,128)(2,1)S(1)} %get-tuple-element.19), channel_id=1, source_target_pairs={{0,8},{4,12},{8,0},{12,4},{16,24},{20,28},{24,16},{28,20},{1,9},{5... | collective-permute-start | bytes 442376 | tf_op jit(solution)/shard_map/ppermute | solution.py:24
  30.8 16.9 %own.1 = (bf16[288,16,128]{2,1,0:T(8,128)(2,1)S(1)}, f32[24,128]{1,0:T(8,128)S(1)}, bf16[96,256]{1,0:T(8,128)(2,1)S(1)}, s32[4,288]{1,0:T(4,128)S(1)}, s32[4]{0:T(128)S(1)}, /*index=5*/bf16[288,128,128]{2,1,0:T(8,128)(2,1)S(1)}) custom-call(s32[288]{0:T(512)S(1)} %fusion.7.own_place, s32[288]{0:T(512)S(1)} %get-tuple-element.38.source, ...), custom_call_target="tpu_custom_call" | custom-call | tf_op jit(solution)/shard_map/own/pallas_call | solution.py:293
  47.7 9.3 %ghost.1 = (bf16[288,16,128]{2,1,0:T(8,128)(2,1)S(1)}, bf16[8,2,24,256]{3,2,1,0:T(8,128)(2,1)}) custom-call(s32[288]{0:T(512)S(1)} %get-tuple-element.46.entry, s32[4,288]{1,0:T(4,128)S(1)} %get-tuple-element.13.lists_ref, s32[4]{0:T(128)S(1)} %get-tuple-element.14.counts_ref, ...), custom_call_target="tpu_custom_call", output_to_operand_aliasing={{0}: (7, {})} | custom-call | tf_op jit(solution)/shard_map/ghost/pallas_call | solution.py:324
  57.1 3.9 %all-to-all-start = ((bf16[16,24,256]{2,1,0:T(8,128)(2,1)}), bf16[16,24,256]{2,1,0:T(8,128)(2,1)S(1)}, u32[]{:S(2)}, u32[]{:S(2)}) async-start(bf16[16,24,256]{2,1,0:T(8,128)(2,1)} %bitcast.13), calls=%async_computation | async-start | bytes 393216 | tf_op jit(solution)/shard_map/all_to_all | solution.py:342
  60.9 1.9 %collective-permute-start.11 = (bf16[96,256]{1,0:T(8,128)(2,1)S(1)}, bf16[96,256]{1,0:T(8,128)(2,1)S(1)}, u32[]{:S(2)}, u32[]{:S(2)}) collective-permute-start(bf16[96,256]{1,0:T(8,128)(2,1)S(1)} %get-tuple-element.22), channel_id=1, source_target_pairs={{0,2},{1,3},{2,0},{3,1},{4,6},{5,7},{6,4},{7,5},{8,10},{9,11},{10,... | collective-permute-start | bytes 147464 | tf_op jit(solution)/shard_map/ppermute | solution.py:24
  62.9 2.7 %collective-permute-done.11 = bf16[96,256]{1,0:T(8,128)(2,1)S(1)} collective-permute-done((bf16[96,256]{1,0:T(8,128)(2,1)S(1)}, bf16[96,256]{1,0:T(8,128)(2,1)S(1)}, u32[]{:S(2)}, u32[]{:S(2)}) %collective-permute-start.11) | collective-permute-done | bytes 49184 | tf_op jit(solution)/shard_map/ppermute | solution.py:24
  65.6 3.4 %all-to-all-done.incoming_ref = bf16[16,24,256]{2,1,0:T(8,128)(2,1)S(1)} async-done(((bf16[16,24,256]{2,1,0:T(8,128)(2,1)}), bf16[16,24,256]{2,1,0:T(8,128)(2,1)S(1)}, u32[]{:S(2)}, u32[]{:S(2)}) %all-to-all-start) | async-done | bytes 196640 | tf_op jit(solution)/shard_map/all_to_all | solution.py:342
  69.4 1.0 %copy.19 = bf16[24,12,16,128]{3,2,1,0:T(8,128)(2,1)} copy(bf16[24,12,16,128]{3,2,1,0:T(8,128)(2,1)S(1)} %bitcast.15) | data formatting | bytes 2359296
  (64 shorter events, 7.3 us)
Async XLA Ops:
  0.6 24.3 %copy-start = (bf16[24,16,128]{2,1,0:T(8,128)(2,1)S(1)}, bf16[24,16,128]{2,1,0:T(8,128)(2,1)}, u32[]{:S(2)}) copy-start(bf16[24,16,128]{2,1,0:T(8,128)(2,1)} %param.5) | copy-start | bytes 294916
  0.6 16.2 %collective-permute-start.5 = (s32[1,126]{1,0:T(1,128)}, s32[1,126]{1,0:T(1,128)S(1)}, u32[]{:S(2)}, u32[]{:S(2)}) collective-permute-start(s32[1,126]{1,0:T(1,128)} %param.7), channel_id=1, source_target_pairs={{0,4},{4,0},{8,12},{12,8},{16,20},{20,16},{24,28},{28,24},{1,5},{5... | collective-permute-start | bytes 1520 | tf_op jit(solution)/shard_map/ppermute | solution.py:24
  3.7 13.9 %collective-permute-start.7 = (s32[1,126]{1,0:T(1,128)}, s32[1,126]{1,0:T(1,128)S(1)}, u32[]{:S(2)}, u32[]{:S(2)}) collective-permute-start(s32[1,126]{1,0:T(1,128)} %param.7), channel_id=1, source_target_pairs={{0,12},{4,8},{8,4},{12,0},{16,28},{20,24},{24,20},{28,16},{1,13},{... | collective-permute-start | bytes 1520 | tf_op jit(solution)/shard_map/ppermute | solution.py:24
  5.2 13.5 %collective-permute-start.6 = (s32[1,126]{1,0:T(1,128)}, s32[1,126]{1,0:T(1,128)S(1)}, u32[]{:S(2)}, u32[]{:S(2)}) collective-permute-start(s32[1,126]{1,0:T(1,128)} %param.7), channel_id=1, source_target_pairs={{0,8},{4,12},{8,0},{12,4},{16,24},{20,28},{24,16},{28,20},{1,9},{5... | collective-permute-start | bytes 1520 | tf_op jit(solution)/shard_map/ppermute | solution.py:24
  5.3 14.8 %collective-permute-start.2 = (bf16[24,16,128]{2,1,0:T(8,128)(2,1)}, bf16[24,16,128]{2,1,0:T(8,128)(2,1)S(1)}, u32[]{:S(2)}, u32[]{:S(2)}) collective-permute-start(bf16[24,16,128]{2,1,0:T(8,128)(2,1)} %param.5), channel_id=1, source_target_pairs={{0,16},{4,20},{8,24},{12,28},{16,0},{20,4},{24,8},{28,12},{1,17},{... | collective-permute-start | bytes 294920 | tf_op jit(solution)/shard_map/ppermute | solution.py:24
  8.3 12.4 %collective-permute-start = (bf16[1,24,16,128]{3,2,1,0:T(8,128)(2,1)}, bf16[1,24,16,128]{3,2,1,0:T(8,128)(2,1)S(1)}, u32[]{:S(2)}, u32[]{:S(2)}) collective-permute-start(bf16[1,24,16,128]{3,2,1,0:T(8,128)(2,1)} %bitcast.21), channel_id=1, source_target_pairs={{0,2},{1,3},{2,0},{3,1},{4,6},{5,7},{6,4},{7,5},{8,10},{9,11},{10,... | collective-permute-start | bytes 294920 | tf_op jit(solution)/shard_map/ppermute | solution.py:24
  20.1 4.7 %collective-permute-start.3 = (bf16[1,24,16,128]{3,2,1,0:T(8,128)(2,1)S(1)}, bf16[1,24,16,128]{3,2,1,0:T(8,128)(2,1)S(1)}, u32[]{:S(2)}, u32[]{:S(2)}) collective-permute-start(bf16[1,24,16,128]{3,2,1,0:T(8,128)(2,1)S(1)} %bitcast.24), channel_id=1, source_target_pairs={{0,2},{1,3},{2,0},{3,1},{4,6},{5,7},{6,4},{7,5},{8,10},{9,11},{10,... | collective-permute-start | bytes 294920 | tf_op jit(solution)/shard_map/ppermute | solution.py:24
  21.6 3.3 %collective-permute-start.1 = (bf16[2,24,16,128]{3,2,1,0:T(8,128)(2,1)S(1)}, bf16[2,24,16,128]{3,2,1,0:T(8,128)(2,1)S(1)}, u32[]{:S(2)}, u32[]{:S(2)}) collective-permute-start(bf16[2,24,16,128]{3,2,1,0:T(8,128)(2,1)S(1)} %pad_maximum_fusion.2), channel_id=1, source_target_pairs={{0,1},{1,0},{2,3},{3,2},{4,5},{5,4},{6,7},{7,6},{8,9},{9,8},{10,11... | collective-permute-start | bytes 589832 | tf_op jit(solution)/shard_map/ppermute | solution.py:24
  24.8 1.5 %collective-permute-start.4 = (bf16[2,24,16,128]{3,2,1,0:T(8,128)(2,1)S(1)}, bf16[2,24,16,128]{3,2,1,0:T(8,128)(2,1)S(1)}, u32[]{:S(2)}, u32[]{:S(2)}) collective-permute-start(bf16[2,24,16,128]{3,2,1,0:T(8,128)(2,1)S(1)} %pad_maximum_fusion.3), channel_id=1, source_target_pairs={{0,1},{1,0},{2,3},{3,2},{4,5},{5,4},{6,7},{7,6},{8,9},{9,8},{10,11... | collective-permute-start | bytes 589832 | tf_op jit(solution)/shard_map/ppermute | solution.py:24
  27.2 20.4 %collective-permute-start.8 = (bf16[36,16,128]{2,1,0:T(8,128)(2,1)S(1)}, bf16[36,16,128]{2,1,0:T(8,128)(2,1)S(1)}, u32[]{:S(2)}, u32[]{:S(2)}) collective-permute-start(bf16[36,16,128]{2,1,0:T(8,128)(2,1)S(1)} %get-tuple-element.18), channel_id=1, source_target_pairs={{0,4},{4,0},{8,12},{12,8},{16,20},{20,16},{24,28},{28,24},{1,5},{5... | collective-permute-start | bytes 442376 | tf_op jit(solution)/shard_map/ppermute | solution.py:24
  28.8 18.9 %collective-permute-start.9 = (bf16[36,16,128]{2,1,0:T(8,128)(2,1)S(1)}, bf16[36,16,128]{2,1,0:T(8,128)(2,1)S(1)}, u32[]{:S(2)}, u32[]{:S(2)}) collective-permute-start(bf16[36,16,128]{2,1,0:T(8,128)(2,1)S(1)} %get-tuple-element.19), channel_id=1, source_target_pairs={{0,8},{4,12},{8,0},{12,4},{16,24},{20,28},{24,16},{28,20},{1,9},{5... | collective-permute-start | bytes 442376 | tf_op jit(solution)/shard_map/ppermute | solution.py:24
  30.4 17.3 %collective-permute-start.10 = (bf16[36,16,128]{2,1,0:T(8,128)(2,1)S(1)}, bf16[36,16,128]{2,1,0:T(8,128)(2,1)S(1)}, u32[]{:S(2)}, u32[]{:S(2)}) collective-permute-start(bf16[36,16,128]{2,1,0:T(8,128)(2,1)S(1)} %get-tuple-element.20), channel_id=1, source_target_pairs={{0,12},{4,8},{8,4},{12,0},{16,28},{20,24},{24,20},{28,16},{1,13},{... | collective-permute-start | bytes 442376 | tf_op jit(solution)/shard_map/ppermute | solution.py:24
  57.1 12.0 %all-to-all-start = ((bf16[16,24,256]{2,1,0:T(8,128)(2,1)}), bf16[16,24,256]{2,1,0:T(8,128)(2,1)S(1)}, u32[]{:S(2)}, u32[]{:S(2)}) async-start(bf16[16,24,256]{2,1,0:T(8,128)(2,1)} %bitcast.13), calls=%async_computation | async-start | bytes 393216 | tf_op jit(solution)/shard_map/all_to_all | solution.py:342
  60.9 4.6 %collective-permute-start.11 = (bf16[96,256]{1,0:T(8,128)(2,1)S(1)}, bf16[96,256]{1,0:T(8,128)(2,1)S(1)}, u32[]{:S(2)}, u32[]{:S(2)}) collective-permute-start(bf16[96,256]{1,0:T(8,128)(2,1)S(1)} %get-tuple-element.22), channel_id=1, source_target_pairs={{0,2},{1,3},{2,0},{3,1},{4,6},{5,7},{6,4},{7,5},{8,10},{9,11},{10,... | collective-permute-start | bytes 147464 | tf_op jit(solution)/shard_map/ppermute | solution.py:24
  65.6 4.9 %collective-permute-start.12 = (bf16[96,256]{1,0:T(8,128)(2,1)S(1)}, bf16[96,256]{1,0:T(8,128)(2,1)S(1)}, u32[]{:S(2)}, u32[]{:S(2)}) collective-permute-start(bf16[96,256]{1,0:T(8,128)(2,1)S(1)} %add_convert_fusion), channel_id=1, source_target_pairs={{0,1},{1,0},{2,3},{3,2},{4,5},{5,4},{6,7},{7,6},{8,9},{9,8},{10,11... | collective-permute-start | bytes 147464 | tf_op jit(solution)/shard_map/ppermute | solution.py:24
  69.4 1.3 %collective-permute-start.13 = (bf16[96,256]{1,0:T(8,128)(2,1)S(1)}, bf16[96,256]{1,0:T(8,128)(2,1)S(1)}, u32[]{:S(2)}, u32[]{:S(2)}) collective-permute-start(bf16[96,256]{1,0:T(8,128)(2,1)S(1)} %target.1), channel_id=1, source_target_pairs={{0,1},{1,0},{2,3},{3,2},{4,5},{5,4},{6,7},{7,6},{8,9},{9,8},{10,11... | collective-permute-start | bytes 147464 | tf_op jit(solution)/shard_map/ppermute | solution.py:24

commit v2 on v0

v2 whole, which is shorter than its diff:
```python
import functools

import jax
import jax.numpy as jnp
from jax import lax
from jax.experimental import pallas as pl
from jax.experimental.pallas import tpu as pltpu
from jax.sharding import PartitionSpec as P

NEIGHBOURS = 26
LANES = 128
BATCH = 8

damping = 2.0 / 3.0

VMEM = pl.BlockSpec(memory_space=pltpu.VMEM)
SMEM = pl.BlockSpec(memory_space=pltpu.SMEM)
PARAMS = pltpu.CompilerParams(vmem_limit_bytes=8 << 20)
NT = (((1,), (1,)), ((), ()))


def xor_permute(x, axis, bit):
    count = lax.axis_size(axis)
    return lax.ppermute(x, axis, [(i, i ^ bit) for i in range(count)])


def divided(value, by):
    return jnp.floor((value.astype(jnp.float32) + 0.5) * (1.0 / by)).astype(jnp.int32)


def table_place(within, lane, tile_dev, bits):
    relative = divided(within, tile_dev)
    rest = within - relative * tile_dev
    relative = relative ^ lane
    order = jnp.zeros_like(relative)
    for i, bit in enumerate(bits):
        order = order + jnp.where((relative & bit) != 0, 1 << i, 0)
    return order * tile_dev + rest


def pick_kernel(count, half, here, owner_ref, place_ref, table_ref, *out_refs):
    for peer, out_ref in enumerate(out_refs):
        near = away = 0
        for p in range(owner_ref.shape[1]):
            owner = owner_ref[peer, p]
            near = jnp.where(owner == here[0], p * count, near)
            away = jnp.where(owner == here[0] ^ half, p * count, away)

        @pl.loop(0, count, unroll=2)
        def _(i):
            out_ref[i] = table_ref[place_ref[peer, near + i]]
            out_ref[count + i] = table_ref[place_ref[peer, away + i]]


def prep_kernel(
    slots, tile_dev, per_peer, rows, half, bits, here,
    cols_ref, fetch_ref, place_ref, row_ref, lists_ref, counts_ref, target_ref, index_ref,
):
    me, lane = here[0], here[1]
    total, ghosts = cols_ref.shape[1], fetch_ref.shape[1]
    group_size = tile_dev * (2 ** len(bits))
    fetched = fetch_ref[...]
    owner = divided(fetched, group_size)
    within = fetched - owner * group_size
    apart = owner ^ me
    low = apart & (half - 1)
    ghost_lane = lax.broadcasted_iota(jnp.int32, (1, ghosts), 1)
    member = ghost_lane - divided(ghost_lane, per_peer) * per_peer
    entry = jnp.where(
        low == 0,
        table_place(within, lane, tile_dev, bits),
        jnp.where(apart >= half, per_peer, 0) + member,
    )
    known = jnp.concatenate([low, entry, owner, member], axis=0).astype(jnp.float32)
    known = known.astype(jnp.bfloat16)
    cols = cols_ref[...]
    match = lax.broadcasted_iota(jnp.int32, (ghosts, total), 0) == cols - group_size
    match = jnp.where(match, 1.0, 0.0).astype(jnp.bfloat16)
    found = jnp.dot(known, match, preferred_element_type=jnp.float32)
    low, entry, owner, member = (found[i : i + 1] for i in range(4))
    is_ghost = cols >= group_size
    source = jnp.where(is_ghost, low.astype(jnp.int32), -1)
    entry_int = entry.astype(jnp.int32)
    place_ref[...] = jnp.where(
        source < 0,
        table_place(cols, lane, tile_dev, bits),
        jnp.where(source == 0, group_size + entry_int, 2 * group_size),
    )
    row_ref[...] = jnp.where(
        source < 0, cols, jnp.where(source == 0, group_size + member.astype(jnp.int32), -1)
    )

    height = -(-half // 8) * 8
    by_source = lax.broadcasted_iota(jnp.int32, (height, total), 0) == source
    by_source = jnp.where(by_source, 1.0, 0.0)
    before = lax.broadcasted_iota(jnp.int32, (total, total), 0) < lax.broadcasted_iota(
        jnp.int32, (total, total), 1
    )
    before = jnp.where(before, 1.0, 0.0).astype(jnp.bfloat16)
    rank = jnp.dot(by_source.astype(jnp.bfloat16), before, preferred_element_type=jnp.float32)
    rank = jnp.where(by_source > 0.5, rank, -1.0).astype(jnp.int32)
    counts = jnp.sum(by_source, axis=1, keepdims=True).astype(jnp.int32)
    counts_ref[...] = jnp.broadcast_to(counts, counts_ref.shape)

    slot = lax.broadcasted_iota(jnp.int32, (1, total), 1)
    tile = divided(slot, slots)
    carried = jnp.concatenate(
        [
            tile.astype(jnp.float32), (slot - tile * slots).astype(jnp.float32), entry, owner,
            member, jnp.ones((1, total), jnp.float32),
        ],
        axis=0,
    ).astype(jnp.bfloat16)
    at = lax.broadcasted_iota(jnp.int32, (total, total), 0)
    for s in range(1, half):
        chosen = jnp.where(at == rank[s : s + 1], 1.0, 0.0).astype(jnp.bfloat16)
        listed = lax.dot_general(carried, chosen, NT, preferred_element_type=jnp.float32)
        listed = listed.astype(jnp.int32)
        lists_ref[3 * s - 3 : 3 * s - 2, :] = listed[0:1] * slots + listed[1:2]
        lists_ref[3 * s - 2 : 3 * s - 1, :] = listed[2:3]
        lists_ref[3 * s - 1 : 3 * s, :] = listed[0:1]
        target_ref[s - 1 : s, :] = jnp.where(listed[5:6] > 0, listed[3:4] * rows + listed[4:5], -1)

    index_ref[...] = jnp.full(index_ref.shape, -1.0, jnp.float32)
    groups = fetch_ref.shape[1] // per_peer
    for p in range(groups):
        part = within[:, p * per_peer : (p + 1) * per_peer].astype(jnp.float32)
        group = jnp.max(
            jnp.where(ghost_lane == p * per_peer, divided(fetched, group_size), 0)
        )
        index_ref[group, :, 0:per_peer] = part


def terms_of(parts, spread, lane_block):
    mode_count = parts[0][0].shape[0]
    halves = [[] for _ in range(mode_count // BATCH)]
    for b in range(len(parts) // BATCH):
        part = parts[b * BATCH : (b + 1) * BATCH]
        block = lax.dot_general(
            jnp.concatenate([s for s, _ in part], axis=0),
            jnp.concatenate([q for _, q in part[::-1]], axis=0),
            NT,
            preferred_element_type=jnp.float32,
        )
        for j in range(BATCH):
            for half in range(mode_count // BATCH):
                row = j * mode_count + half * BATCH
                value = pltpu.roll(block[row : row + BATCH], 0, 1, stride=mode_count, stride_axis=0)
                value = jnp.where(lane_block == BATCH - 1 - j, value, 0.0)
                halves[half].append(value)
    halves = [jnp.concatenate(h, axis=0).astype(jnp.bfloat16) for h in halves]
    flat = jnp.dot(spread, jnp.concatenate(halves, axis=1), preferred_element_type=jnp.float32)
    rows = []
    for b in range(len(parts) // BATCH):
        row = flat[b * BATCH : (b + 1) * BATCH]
        rows.append(
            jnp.concatenate(
                [
                    pltpu.roll(row[:, h * LANES : (h + 1) * LANES], mode_count, 1, stride=mode_count, stride_axis=0)
                    for h in range(len(halves))
                ],
                axis=1,
            )
        )
    return jnp.concatenate(rows, axis=0)


def term_constants(count, mode_count):
    spread = lax.broadcasted_iota(jnp.int32, (count, count * BATCH), 1) // BATCH
    spread = spread == lax.broadcasted_iota(jnp.int32, (count, count * BATCH), 0)
    lane_block = (
        lax.broadcasted_iota(jnp.int32, (BATCH, LANES), 1) // mode_count
        - lax.broadcasted_iota(jnp.int32, (BATCH, LANES), 0)
    ) & (BATCH - 1)
    return jnp.where(spread, 1.0, 0.0).astype(jnp.bfloat16), lane_block


def product_pair(picked, tiles):
    zero = jnp.zeros_like(picked[0])
    left = jnp.concatenate(
        [
            jnp.concatenate([picked[0], zero], axis=1),
            jnp.concatenate([zero, picked[1]], axis=1),
        ],
        axis=0,
    )
    right = jnp.concatenate(tiles, axis=1)
    both = lax.dot_general(left, right, NT, preferred_element_type=jnp.float32)
    rows = picked[0].shape[0]
    return both[:rows], both[rows:]


def own_kernel(
    slots, group_size, place, row_ref, table_ref, a_hbm,
    prolong_ref, weight_ref, sums_ref, far_ref, a_ref, product_ref, terms_ref, arrived,
):
    tile_dev = weight_ref.shape[0]
    mode_count, tile_rows = table_ref.shape[1:]
    pair = 2
    per_step = pair * slots
    steps = tile_dev // pair
    diagonal = lax.broadcasted_iota(jnp.int32, (tile_rows, tile_rows), 0) == lax.broadcasted_iota(
        jnp.int32, (tile_rows, tile_rows), 1
    )
    spread, lane_block = term_constants(per_step, mode_count)

    def fetch(step):
        part = pl.ds(step * per_step, per_step)
        return pltpu.make_async_copy(a_hbm.at[part], a_ref.at[part], arrived.at[step])

    @pl.loop(0, steps)
    def _(step):
        fetch(step).start()

    def finish(step):
        first = step * per_step
        parts = [(prolong_ref[first + k], product_ref[first + k]) for k in range(per_step)]
        terms_ref[pl.ds(pl.multiple_of(first, 8), per_step), :] = terms_of(parts, spread, lane_block)

    def begin(step):
        for i in range(pair):
            tile = step * pair + i
            lead = a_ref[tile * slots].astype(jnp.float32)
            entries = jnp.sum(jnp.where(diagonal, lead, 0.0), axis=0, keepdims=True)
            weight = damping * (1.0 / entries)
            weight_ref[pl.ds(tile, 1), :] = weight
            for k in range(0, slots, 2):
                slot = tile * slots + k
                picked = [table_ref[place[slot]], table_ref[place[slot + 1]]]
                products = product_pair(picked, [a_ref[slot], a_ref[slot + 1]])
                for d, product in enumerate(products):
                    smooth = -(weight * product)
                    if k + d == 0:
                        smooth = picked[0].astype(jnp.float32) + smooth
                    prolong_ref[slot + d] = smooth.astype(jnp.bfloat16)
                    product_ref[slot + d] = product.astype(jnp.bfloat16)

    fetch(0).wait()
    begin(0)

    @pl.loop(1, steps)
    def _(step):
        fetch(step).wait()
        finish(step - 1)
        begin(step)

    finish(steps - 1)

    total = tile_dev * slots
    height = group_size + far_ref.shape[0]
    one_hot = lax.broadcasted_iota(jnp.int32, (height, total), 0) == row_ref[...]
    one_hot = jnp.where(one_hot, 1.0, 0.0).astype(jnp.bfloat16)
    sums = jnp.dot(one_hot, terms_ref[...].astype(jnp.bfloat16), preferred_element_type=jnp.float32)
    sums = sums * (1.0 / tile_rows)
    sums_ref[...] = sums[:group_size].astype(jnp.bfloat16)
    far_ref[...] = sums[group_size:]


def ghost_kernel(
    pitch, half, here, lists_ref, counts_ref, target_ref, index_ref, far_ref, a_ref, weight_ref, old_ref,
    *refs,
):
    sources = refs[:-5]
    prolong_ref, out_ref, smooth_ref, product_ref, terms_ref = refs[-5:]
    mode_count, tile_rows = sources[0].shape[1:]
    groups, copies, rows, width = out_ref.shape
    total = a_ref.shape[0]
    batch = 2 * BATCH
    spread, lane_block = term_constants(batch, mode_count)
    terms_ref[...] = jnp.zeros_like(terms_ref)
    result = jnp.zeros((groups * rows, width), jnp.float32)

    for s, table_ref in enumerate(sources):
        count = counts_ref[s + 1, 0]
        steps = (count + batch - 1) // batch

        def begin(step):
            for i in range(0, batch, 2):
                at = [jnp.minimum(step * batch + i + d, count - 1) for d in range(2)]
                slot = [lists_ref[3 * s, a] for a in at]
                picked = [table_ref[lists_ref[3 * s + 1, a]] for a in at]
                products = product_pair(picked, [a_ref[f] for f in slot])
                for d, product in enumerate(products):
                    weight = weight_ref[pl.ds(lists_ref[3 * s + 2, at[d]], 1), :]
                    smooth = (-(weight * product)).astype(jnp.bfloat16)
                    prolong_ref[slot[d]] = smooth
                    smooth_ref[i + d] = smooth
                    product_ref[i + d] = product.astype(jnp.bfloat16)

        def finish(step):
            parts = [(smooth_ref[i], product_ref[i]) for i in range(batch)]
            row = pl.multiple_of(step * batch, batch)
            terms_ref[pl.ds(row, batch), :] = terms_of(parts, spread, lane_block)

        @pl.when(count > 0)
        def _():
            begin(0)

            @pl.loop(1, steps)
            def _(step):
                finish(step - 1)
                begin(step)

            finish(steps - 1)

        one_hot = (
            lax.broadcasted_iota(jnp.int32, (groups * rows, total), 0) == target_ref[s : s + 1, :]
        )
        one_hot = jnp.where(one_hot, 1.0, 0.0).astype(jnp.bfloat16)
        result = result + jnp.dot(
            one_hot, terms_ref[0:total, :].astype(jnp.bfloat16), preferred_element_type=jnp.float32
        )

    result = (result * (1.0 / tile_rows)).reshape(groups, rows, width)
    row_place = lax.broadcasted_iota(jnp.int32, (groups, rows, width), 1)
    group_place = lax.broadcasted_iota(jnp.int32, (groups, rows, width), 0)
    result = jnp.where(group_place == (here[0] ^ half), far_ref[...][None], result)
    result = jnp.where(row_place == pitch, index_ref[...], result).astype(jnp.bfloat16)
    for copy in range(copies):
        out_ref[:, copy] = result


def target_kernel(pitch, incoming_ref, out_ref):
    senders, rows, width = incoming_ref.shape
    group_size = out_ref.shape[0]
    tile = lax.broadcasted_iota(jnp.int32, (group_size, rows), 0)
    total = jnp.zeros((group_size, width), jnp.float32)
    for sender in range(senders):
        value = incoming_ref[sender]
        wanted = value[pitch : pitch + 1, :rows].astype(jnp.float32).astype(jnp.int32)
        one_hot = (tile == wanted).astype(jnp.bfloat16)
        total = total + jnp.dot(one_hot, value, preferred_element_type=jnp.float32)
    out_ref[...] = total.astype(jnp.bfloat16)


def shards(a_tiles, modes, col_tiles, fetch_list):
    blk_count = lax.axis_size("blk")
    sub_count = lax.axis_size("sub")
    tile_dev, slot_count, tile_rows = a_tiles.shape[:3]
    mode_count = modes.shape[1]
    width = mode_count * mode_count
    group_size = tile_dev * blk_count
    ghost_count = fetch_list.shape[1]
    peer_count = min(NEIGHBOURS, sub_count - 1)
    per_peer = ghost_count // peer_count
    slot_total = tile_dev * slot_count
    half = sub_count // 2
    blk_half = blk_count // 2
    me = lax.axis_index("sub")
    lane = lax.axis_index("blk")

    far = xor_permute(modes, "sub", half)
    bits = []
    bit = blk_half
    own_part, far_part = modes[None], far[None]
    while bit:
        own_part = jnp.concatenate([own_part, xor_permute(own_part, "blk", bit)], axis=0)
        far_part = jnp.concatenate([far_part, xor_permute(far_part, "blk", bit)], axis=0)
        bits.append(bit)
        bit //= 2
    blank = jnp.zeros((1, mode_count, tile_rows), modes.dtype)
    table = jnp.concatenate(
        [
            own_part.reshape(group_size, mode_count, tile_rows),
            far_part.reshape(group_size, mode_count, tile_rows),
            blank,
        ],
        axis=0,
    )

    theirs = jnp.concatenate([xor_permute(fetch_list, "sub", peer) for peer in range(1, half)], axis=0)
    owners = theirs // group_size
    places = table_place(theirs % group_size, lane, tile_dev, bits)
    places = places + jnp.where(owners == (me ^ half), group_size, 0)
    here = jnp.stack([me, lane]).astype(jnp.int32)
    picks = pl.pallas_call(
        functools.partial(pick_kernel, per_peer, half),
        out_shape=[jax.ShapeDtypeStruct((2 * per_peer, mode_count, tile_rows), modes.dtype)] * (half - 1),
        in_specs=[SMEM, SMEM, SMEM, VMEM],
        out_specs=[VMEM] * (half - 1),
        name="pick",
        compiler_params=PARAMS,
    )(here, owners[:, ::per_peer], places, table)
    received = [xor_permute(picks[peer - 1], "sub", peer) for peer in range(1, half)]

    rows = -(-(per_peer + 1) // 8) * 8
    place, own_row, lists, counts, target, index_rows = pl.pallas_call(
        functools.partial(prep_kernel, slot_count, tile_dev, per_peer, rows, half, tuple(bits)),
        out_shape=[
            jax.ShapeDtypeStruct((1, slot_total), jnp.int32),
            jax.ShapeDtypeStruct((1, slot_total), jnp.int32),
            jax.ShapeDtypeStruct((3 * (half - 1), slot_total), jnp.int32),
            jax.ShapeDtypeStruct((-(-half // 8) * 8, LANES), jnp.int32),
            jax.ShapeDtypeStruct((half - 1, slot_total), jnp.int32),
            jax.ShapeDtypeStruct((sub_count, 1, width), jnp.float32),
        ],
        in_specs=[SMEM, VMEM, VMEM],
        out_specs=[VMEM] * 6,
        name="prep",
        compiler_params=PARAMS,
    )(here, col_tiles.reshape(1, slot_total), fetch_list)

    tiles = a_tiles.reshape(slot_total, tile_rows, tile_rows)
    tiles = pltpu.with_memory_space_constraint(tiles, pltpu.HBM)
    prolong, weight, own_sums, far_sums, tiles = pl.pallas_call(
        functools.partial(own_kernel, slot_count, group_size),
        out_shape=[
            pltpu.VMEM((slot_total, mode_count, tile_rows), jnp.bfloat16),
            jax.ShapeDtypeStruct((tile_dev, tile_rows), jnp.float32),
            jax.ShapeDtypeStruct((group_size, width), jnp.bfloat16),
            jax.ShapeDtypeStruct((rows, width), jnp.float32),
            pltpu.VMEM((slot_total, tile_rows, tile_rows), jnp.bfloat16),
        ],
        in_specs=[SMEM, VMEM, VMEM, pl.BlockSpec(memory_space=pltpu.HBM)],
        out_specs=[VMEM] * 5,
        scratch_shapes=[
            pltpu.VMEM((slot_total, mode_count, tile_rows), jnp.bfloat16),
            pltpu.VMEM((slot_total, width), jnp.float32),
            pltpu.SemaphoreType.DMA((tile_dev // 2,)),
        ],
        name="own",
        compiler_params=PARAMS,
    )(place.reshape(slot_total), own_row, table, tiles)

    prolong = pltpu.with_memory_space_constraint(prolong, pltpu.VMEM)
    tiles = pltpu.with_memory_space_constraint(tiles, pltpu.VMEM)
    own_total = own_sums
    bit = blk_half
    while bit:
        other = xor_permute(own_total, "blk", bit)
        own_total = own_total.astype(jnp.float32) + other.astype(jnp.float32)
        bit //= 2
        if bit:
            own_total = own_total.astype(jnp.bfloat16)

    prolong, outgoing = pl.pallas_call(
        functools.partial(ghost_kernel, per_peer, half),
        out_shape=[
            pltpu.VMEM((slot_total, mode_count, tile_rows), jnp.bfloat16),
            jax.ShapeDtypeStruct((sub_count, blk_half, rows, width), jnp.bfloat16),
        ],
        in_specs=[SMEM] * 3 + [VMEM] * (6 + half - 1),
        out_specs=[VMEM, VMEM],
        input_output_aliases={8: 0},
        scratch_shapes=[
            pltpu.VMEM((2 * BATCH, mode_count, tile_rows), jnp.bfloat16),
            pltpu.VMEM((2 * BATCH, mode_count, tile_rows), jnp.bfloat16),
            pltpu.VMEM((slot_total + 2 * BATCH, width), jnp.float32),
        ],
        name="ghost",
        compiler_params=PARAMS,
    )(here, lists, counts, target, index_rows, far_sums, tiles, weight, prolong, *received)

    groups = [
        [s * blk_count + high * 2 + core for s in range(sub_count) for high in range(blk_half)]
        for core in range(2)
    ]
    incoming = lax.all_to_all(
        outgoing.reshape(sub_count * blk_half, rows, width),
        ("sub", "blk"), split_axis=0, concat_axis=0, axis_index_groups=groups, tiled=True,
    )
    arrived = pl.pallas_call(
        functools.partial(target_kernel, per_peer),
        out_shape=jax.ShapeDtypeStruct((group_size, width), jnp.bfloat16),
        in_specs=[VMEM],
        out_specs=VMEM,
        name="target",
        compiler_params=PARAMS,
    )(incoming)
    other = xor_permute(arrived, "blk", 1)
    coarse_diag = own_total + (arrived.astype(jnp.float32) + other.astype(jnp.float32))
    return prolong.reshape(tile_dev, slot_count, mode_count, tile_rows), coarse_diag


def solution(mesh):
    in_specs = (
        P(("sub", "blk"), None, None, None),
        P(("sub", "blk"), None, None),
        P(("sub", "blk"), None),
        P(("sub", "blk"), None),
    )
    out_specs = (P(("sub", "blk"), None, None, None), P("sub", None))
    return jax.shard_map(shards, mesh=mesh, in_specs=in_specs, out_specs=out_specs, check_vma=False)
```

time: 80.7 us -> 59.5 us (0.74)
  Pallas kernels: 0 us -> 19.6 us
  blocking collectives: 17.2 us -> 0 us
  matrix products: 11.6 us -> 0 us
  local copies, waits for them, and re-layouts: 12 us -> 1.38 us
  waiting for transfers between devices: 17.8 us -> 11.2 us
  starting transfers between devices: 16.9 us -> 23.3 us
  other arithmetic: 4.03 us -> 2.99 us
    pallas_call x0 -> x5, Pallas kernels: none -> 19.6 us  [the longest x1 9.59 us: shards(): pl.pallas_call(functools.partial(own_kernel, slot_count, group_size), out...]
    ppermute x0 -> x14, starting transfers between devices: none -> 16.5 us  [xor_permute(): return lax.ppermute(x, axis, [(i, i ^ bit) for i in range(count)])]
    all_to_all x3 -> x1, waiting for transfers between devices: 17.8 us -> 3.37 us  [shards(): lax.all_to_all(outgoing.reshape(sub_count * blk_half, rows, width), ('sub...]
    dot_general x5 -> x0, matrix products: 11.6 us -> none  [the longest x1 7.47 us: shards(): jnp.einsum('tkrc,tkmc->tkmr', a_tiles, gathered, preferred_element_type=j...]
    psum x1 -> x0, blocking collectives: 10.5 us -> none  [shards(): lax.psum(local_sum.astype(jnp.bfloat16), 'blk').astype(jnp.float32)]
    all_to_all x3 -> x1, starting transfers between devices: 16.9 us -> 6.79 us  [shards(): lax.all_to_all(outgoing.reshape(sub_count * blk_half, rows, width), ('sub...]
    ppermute x0 -> x14, waiting for transfers between devices: none -> 7.88 us  [xor_permute(): return lax.ppermute(x, axis, [(i, i ^ bit) for i in range(count)])]
    all_gather x1 -> x0, blocking collectives: 6.68 us -> none  [shards(): group_modes = lax.all_gather(modes, 'blk', axis=0, tiled=True)]
  transfers between devices with their start and end apart: 3 -> 15, of which waited for: 2 -> 6; matrix products, arithmetic and copies ran while one was open for 7% -> 6% of each run, Pallas kernels for 0% -> 19%
where the time goes in v2:
time: 59.5 us; the launch traced here: 59.3 us
  starting transfers between devices  23.3 us (39%)
  Pallas kernels  19.6 us (33%)
  waiting for transfers between devices  11.2 us (19%)
  other arithmetic  2.99 us (5%)
  local copies, waits for them, and re-layouts  1.38 us (2%)
  between operations  0.81 us (1%)
    ppermute x14, starting transfers between devices, xor_permute(): return lax.ppermute(x, axis, [(i, i ^ bit) for i in range(count)])  16.5 us
    pallas_call x1, Pallas kernels, shards(): pl.pallas_call(functools.partial(own_kernel, slot_count, group_size), out...  9.59 us
    ppermute x14, waiting for transfers between devices, xor_permute(): return lax.ppermute(x, axis, [(i, i ^ bit) for i in range(count)])  7.88 us
    pallas_call x1, Pallas kernels, shards(): pl.pallas_call(functools.partial(ghost_kernel, per_peer, half), out_shape...  7.55 us
    all_to_all x1, starting transfers between devices, shards(): lax.all_to_all(outgoing.reshape(sub_count * blk_half, rows, width), ('sub...  6.79 us
    all_to_all x1, waiting for transfers between devices, shards(): lax.all_to_all(outgoing.reshape(sub_count * blk_half, rows, width), ('sub...  3.37 us
    concatenate x2, other arithmetic, shards(): jnp.concatenate([own_part, xor_permute(own_part, 'blk', bit)], axis=0)  1.85 us
  transfers between devices with their start and end apart: 15, of which 6 were waited for; matrix products, arithmetic and copies ran while one was open for 6% of the time, Pallas kernels for 19%

profile of v2, /device:TPU:0, one launch (start us, length us, event | category | flops | bytes accessed | tf_op | source)
XLA Modules:
  0.0 59.3 jit_solution(8162671149348029667)
XLA Ops:
  0.6 3.0 %collective-permute-start.5 = (s32[1,126]{1,0:T(1,128)}, s32[1,126]{1,0:T(1,128)S(1)}, u32[]{:S(2)}, u32[]{:S(2)}) collective-permute-start(s32[1,126]{1,0:T(1,128)} %fetch_ref.1), channel_id=1, source_target_pairs={{0,4},{4,0},{8,12},{12,8},{16,20},{20,16},{24,28},{28,24},{1,5},{5... | collective-permute-start | bytes 1520 | tf_op jit(solution)/shard_map/ppermute | solution.py:24
  3.7 1.5 %collective-permute-start.7 = (s32[1,126]{1,0:T(1,128)}, s32[1,126]{1,0:T(1,128)S(1)}, u32[]{:S(2)}, u32[]{:S(2)}) collective-permute-start(s32[1,126]{1,0:T(1,128)} %fetch_ref.1), channel_id=1, source_target_pairs={{0,12},{4,8},{8,4},{12,0},{16,28},{20,24},{24,20},{28,16},{1,13},{... | collective-permute-start | bytes 1520 | tf_op jit(solution)/shard_map/ppermute | solution.py:24
  5.2 3.0 %collective-permute-start.2 = (bf16[24,16,128]{2,1,0:T(8,128)(2,1)}, bf16[24,16,128]{2,1,0:T(8,128)(2,1)S(1)}, u32[]{:S(2)}, u32[]{:S(2)}) collective-permute-start(bf16[24,16,128]{2,1,0:T(8,128)(2,1)} %param.5), channel_id=1, source_target_pairs={{0,16},{4,20},{8,24},{12,28},{16,0},{20,4},{24,8},{28,12},{1,17},{... | collective-permute-start | bytes 294920 | tf_op jit(solution)/shard_map/ppermute | solution.py:24
  8.2 1.5 %collective-permute-start = (bf16[1,24,16,128]{3,2,1,0:T(8,128)(2,1)}, bf16[1,24,16,128]{3,2,1,0:T(8,128)(2,1)S(1)}, u32[]{:S(2)}, u32[]{:S(2)}) collective-permute-start(bf16[1,24,16,128]{3,2,1,0:T(8,128)(2,1)} %bitcast.14), channel_id=1, source_target_pairs={{0,2},{1,3},{2,0},{3,1},{4,6},{5,7},{6,4},{7,5},{8,10},{9,11},{10,... | collective-permute-start | bytes 294920 | tf_op jit(solution)/shard_map/ppermute | solution.py:24
  9.9 2.6 %collective-permute-done.2 = bf16[24,16,128]{2,1,0:T(8,128)(2,1)S(1)} collective-permute-done((bf16[24,16,128]{2,1,0:T(8,128)(2,1)}, bf16[24,16,128]{2,1,0:T(8,128)(2,1)S(1)}, u32[]{:S(2)}, u32[]{:S(2)}) %collective-permute-start.2) | collective-permute-done | bytes 98336 | tf_op jit(solution)/shard_map/ppermute | solution.py:24
  12.5 1.6 %collective-permute-start.3 = (bf16[1,24,16,128]{3,2,1,0:T(8,128)(2,1)S(1)}, bf16[1,24,16,128]{3,2,1,0:T(8,128)(2,1)S(1)}, u32[]{:S(2)}, u32[]{:S(2)}) collective-permute-start(bf16[1,24,16,128]{3,2,1,0:T(8,128)(2,1)S(1)} %bitcast.17), channel_id=1, source_target_pairs={{0,2},{1,3},{2,0},{3,1},{4,6},{5,7},{6,4},{7,5},{8,10},{9,11},{10,... | collective-permute-start | bytes 294920 | tf_op jit(solution)/shard_map/ppermute | solution.py:24
  14.1 0.9 %pad_maximum_fusion.2 = bf16[2,24,16,128]{3,2,1,0:T(8,128)(2,1)S(1)} fusion(bf16[1,24,16,128]{3,2,1,0:T(8,128)(2,1)S(1)} %collective-permute-done, bf16[1,24,16,128]{3,2,1,0:T(8,128)(2,1)} %bitcast.15), kind=kLoop, calls=%fused_computation.3 | loop fusion | flops 98304 | bytes 393216 | tf_op jit(solution)/shard_map/concatenate | solution.py:357
  15.1 2.1 %collective-permute-done.3 = bf16[1,24,16,128]{3,2,1,0:T(8,128)(2,1)S(1)} collective-permute-done((bf16[1,24,16,128]{3,2,1,0:T(8,128)(2,1)S(1)}, bf16[1,24,16,128]{3,2,1,0:T(8,128)(2,1)S(1)}, u32[]{:S(2)}, u32[]{:S(2)}) %collective-permute-start.3) | collective-permute-done | bytes 98336 | tf_op jit(solution)/shard_map/ppermute | solution.py:24
  17.4 0.9 %pad_maximum_fusion = bf16[4,24,16,128]{3,2,1,0:T(8,128)(2,1)S(1)} fusion(bf16[2,24,16,128]{3,2,1,0:T(8,128)(2,1)S(1)} %collective-permute-done.1, bf16[1,24,16,128]{3,2,1,0:T(8,128)(2,1)S(1)} %collective-permute-done, bf16[1,24,16,128]{3,2,1,0:T(8,128)(2,1)} %bitcast.16), kind=kLoop, calls=%fused_computation.1 | loop fusion | flops 393216 | bytes 786432 | tf_op jit(solution)/shard_map/concatenate | solution.py:357
  18.4 0.3 collective-permute-done.4
  19.0 1.0 %pick.1 = (bf16[36,16,128]{2,1,0:T(8,128)(2,1)S(1)}, bf16[36,16,128]{2,1,0:T(8,128)(2,1)S(1)}, bf16[36,16,128]{2,1,0:T(8,128)(2,1)S(1)}) custom-call(s32[2]{0:T(128)S(1)} %pad_add_fusion.1.here, s32[3,7]{1,0:T(4,128)S(1)} %slice.3.owner_ref, s32[3,126]{1,0:T(4,128)S(1)} %get-tuple-element.34.place_ref, bf16[193,16,128]{2,1,0:T(8,128)(2,1)S(1)} %maximum_maximum_fusion.table_ref), custom_call_target="tpu_custom_call" | custom-call | tf_op jit(solution)/shard_map/pick/pallas_call | solution.py:376
  20.0 1.6 %collective-permute-start.8 = (bf16[36,16,128]{2,1,0:T(8,128)(2,1)S(1)}, bf16[36,16,128]{2,1,0:T(8,128)(2,1)S(1)}, u32[]{:S(2)}, u32[]{:S(2)}) collective-permute-start(bf16[36,16,128]{2,1,0:T(8,128)(2,1)S(1)} %get-tuple-element.28), channel_id=1, source_target_pairs={{0,4},{4,0},{8,12},{12,8},{16,20},{20,16},{24,28},{28,24},{1,5},{5... | collective-permute-start | bytes 442376 | tf_op jit(solution)/shard_map/ppermute | solution.py:24
  21.6 0.8 %collective-permute-start.9 = (bf16[36,16,128]{2,1,0:T(8,128)(2,1)S(1)}, bf16[36,16,128]{2,1,0:T(8,128)(2,1)S(1)}, u32[]{:S(2)}, u32[]{:S(2)}) collective-permute-start(bf16[36,16,128]{2,1,0:T(8,128)(2,1)S(1)} %get-tuple-element.29), channel_id=1, source_target_pairs={{0,8},{4,12},{8,0},{12,4},{16,24},{20,28},{24,16},{28,20},{1,9},{5... | collective-permute-start | bytes 442376 | tf_op jit(solution)/shard_map/ppermute | solution.py:24
  22.4 1.2 %collective-permute-start.10 = (bf16[36,16,128]{2,1,0:T(8,128)(2,1)S(1)}, bf16[36,16,128]{2,1,0:T(8,128)(2,1)S(1)}, u32[]{:S(2)}, u32[]{:S(2)}) collective-permute-start(bf16[36,16,128]{2,1,0:T(8,128)(2,1)S(1)} %get-tuple-element.30), channel_id=1, source_target_pairs={{0,12},{4,8},{8,4},{12,0},{16,28},{20,24},{24,20},{28,16},{1,13},{... | collective-permute-start | bytes 442376 | tf_op jit(solution)/shard_map/ppermute | solution.py:24
  23.8 1.1 %prep.1 = (s32[1,288]{1,0:T(1,128)S(1)}, s32[1,288]{1,0:T(1,128)S(1)}, s32[9,288]{1,0:T(8,128)S(1)}, s32[8,128]{1,0:T(8,128)S(1)}, s32[3,288]{1,0:T(4,128)S(1)}, /*index=5*/f32[8,1,256]{2,1,0:T(1,128)S(1)}) custom-call(s32[2]{0:T(128)S(1)} %pad_add_fusion.1.here, s32[1,288]{1,0:T(1,128)S(1)} %reshape.25.cols_ref, s32[1,126]{1,0:T(1,128)S(1)} %copy-done), custom_call_target="tpu_custom_call" | custom-call | tf_op jit(solution)/shard_map/prep/pallas_call | solution.py:387
  24.9 9.6 %own.1 = (bf16[288,16,128]{2,1,0:T(8,128)(2,1)S(1)}, f32[24,128]{1,0:T(8,128)S(1)}, bf16[96,256]{1,0:T(8,128)(2,1)S(1)}, f32[24,256]{1,0:T(8,128)S(1)}, bf16[288,128,128]{2,1,0:T(8,128)(2,1)S(1)}) custom-call(s32[288]{0:T(512)S(1)} %reduce.place, s32[1,288]{1,0:T(1,128)S(1)} %get-tuple-element.23.row_ref, ...), custom_call_target="tpu_custom_call" | custom-call | tf_op jit(solution)/shard_map/own/pallas_call | solution.py:405
  34.6 7.5 %ghost.1 = (bf16[288,16,128]{2,1,0:T(8,128)(2,1)S(1)}, bf16[8,2,24,256]{3,2,1,0:T(8,128)(2,1)}) custom-call(s32[2]{0:T(128)S(1)} %pad_add_fusion.1.here, s32[9,288]{1,0:T(8,128)S(1)} %get-tuple-element.18.lists_ref, s32[8,128]{1,0:T(8,128)S(1)} %get-tuple-element.19.counts_ref, ...), custom_call_target="tpu_custom_call", output_to_operand_aliasing={{0}: (8, {})} | custom-call | tf_op jit(solution)/shard_map/ghost/pallas_call | solution.py:436
  42.1 6.8 %all-to-all-start = ((bf16[16,24,256]{2,1,0:T(8,128)(2,1)}), bf16[16,24,256]{2,1,0:T(8,128)(2,1)S(1)}, u32[]{:S(2)}, u32[]{:S(2)}) async-start(bf16[16,24,256]{2,1,0:T(8,128)(2,1)} %bitcast.8), calls=%async_computation | async-start | bytes 393216 | tf_op jit(solution)/shard_map/all_to_all | solution.py:458
  48.9 1.9 %collective-permute-start.11 = (bf16[96,256]{1,0:T(8,128)(2,1)S(1)}, bf16[96,256]{1,0:T(8,128)(2,1)S(1)}, u32[]{:S(2)}, u32[]{:S(2)}) collective-permute-start(bf16[96,256]{1,0:T(8,128)(2,1)S(1)} %get-tuple-element.32), channel_id=1, source_target_pairs={{0,2},{1,3},{2,0},{3,1},{4,6},{5,7},{6,4},{7,5},{8,10},{9,11},{10,... | collective-permute-start | bytes 147464 | tf_op jit(solution)/shard_map/ppermute | solution.py:24
  50.8 2.7 %collective-permute-done.11 = bf16[96,256]{1,0:T(8,128)(2,1)S(1)} collective-permute-done((bf16[96,256]{1,0:T(8,128)(2,1)S(1)}, bf16[96,256]{1,0:T(8,128)(2,1)S(1)}, u32[]{:S(2)}, u32[]{:S(2)}) %collective-permute-start.11) | collective-permute-done | bytes 49184 | tf_op jit(solution)/shard_map/ppermute | solution.py:24
  53.6 3.4 %all-to-all-done.incoming_ref = bf16[16,24,256]{2,1,0:T(8,128)(2,1)S(1)} async-done(((bf16[16,24,256]{2,1,0:T(8,128)(2,1)}), bf16[16,24,256]{2,1,0:T(8,128)(2,1)S(1)}, u32[]{:S(2)}, u32[]{:S(2)}) %all-to-all-start) | async-done | bytes 196640 | tf_op jit(solution)/shard_map/all_to_all | solution.py:458
  57.0 0.3 target.1
  57.4 1.0 %copy.10 = bf16[24,12,16,128]{3,2,1,0:T(8,128)(2,1)} copy(bf16[24,12,16,128]{3,2,1,0:T(8,128)(2,1)S(1)} %bitcast.10) | data formatting | bytes 2359296
  58.6 0.7 %add_add_fusion = f32[96,256]{1,0:T(8,128)} fusion(bf16[96,256]{1,0:T(8,128)(2,1)S(1)} %collective-permute-done.13, bf16[96,256]{1,0:T(8,128)(2,1)S(1)} %target.1, bf16[96,256]{1,0:T(8,128)(2,1)S(1)} %collective-permute-done.12, bf16[96,256]{1,0:T(8,128)(2,1)S(1)} %add_convert_fusion), kind=kLoop, calls=%fused_computation.5 | loop fusion | flops 172032 | bytes 294912 | tf_op jit(solution)/shard_map/add | solution.py:471
  (30 shorter events, 1.4 us)
Async XLA Ops:
  0.6 16.6 %collective-permute-start.5 = (s32[1,126]{1,0:T(1,128)}, s32[1,126]{1,0:T(1,128)S(1)}, u32[]{:S(2)}, u32[]{:S(2)}) collective-permute-start(s32[1,126]{1,0:T(1,128)} %fetch_ref.1), channel_id=1, source_target_pairs={{0,4},{4,0},{8,12},{12,8},{16,20},{20,16},{24,28},{28,24},{1,5},{5... | collective-permute-start | bytes 1520 | tf_op jit(solution)/shard_map/ppermute | solution.py:24
  3.7 13.6 %collective-permute-start.7 = (s32[1,126]{1,0:T(1,128)}, s32[1,126]{1,0:T(1,128)S(1)}, u32[]{:S(2)}, u32[]{:S(2)}) collective-permute-start(s32[1,126]{1,0:T(1,128)} %fetch_ref.1), channel_id=1, source_target_pairs={{0,12},{4,8},{8,4},{12,0},{16,28},{20,24},{24,20},{28,16},{1,13},{... | collective-permute-start | bytes 1520 | tf_op jit(solution)/shard_map/ppermute | solution.py:24
  5.2 12.1 %collective-permute-start.6 = (s32[1,126]{1,0:T(1,128)}, s32[1,126]{1,0:T(1,128)S(1)}, u32[]{:S(2)}, u32[]{:S(2)}) collective-permute-start(s32[1,126]{1,0:T(1,128)} %fetch_ref.1), channel_id=1, source_target_pairs={{0,8},{4,12},{8,0},{12,4},{16,24},{20,28},{24,16},{28,20},{1,9},{5... | collective-permute-start | bytes 1520 | tf_op jit(solution)/shard_map/ppermute | solution.py:24
  5.2 7.3 %collective-permute-start.2 = (bf16[24,16,128]{2,1,0:T(8,128)(2,1)}, bf16[24,16,128]{2,1,0:T(8,128)(2,1)S(1)}, u32[]{:S(2)}, u32[]{:S(2)}) collective-permute-start(bf16[24,16,128]{2,1,0:T(8,128)(2,1)} %param.5), channel_id=1, source_target_pairs={{0,16},{4,20},{8,24},{12,28},{16,0},{20,4},{24,8},{28,12},{1,17},{... | collective-permute-start | bytes 294920 | tf_op jit(solution)/shard_map/ppermute | solution.py:24
  8.2 5.8 %collective-permute-start = (bf16[1,24,16,128]{3,2,1,0:T(8,128)(2,1)}, bf16[1,24,16,128]{3,2,1,0:T(8,128)(2,1)S(1)}, u32[]{:S(2)}, u32[]{:S(2)}) collective-permute-start(bf16[1,24,16,128]{3,2,1,0:T(8,128)(2,1)} %bitcast.14), channel_id=1, source_target_pairs={{0,2},{1,3},{2,0},{3,1},{4,6},{5,7},{6,4},{7,5},{8,10},{9,11},{10,... | collective-permute-start | bytes 294920 | tf_op jit(solution)/shard_map/ppermute | solution.py:24
  12.5 4.6 %collective-permute-start.3 = (bf16[1,24,16,128]{3,2,1,0:T(8,128)(2,1)S(1)}, bf16[1,24,16,128]{3,2,1,0:T(8,128)(2,1)S(1)}, u32[]{:S(2)}, u32[]{:S(2)}) collective-permute-start(bf16[1,24,16,128]{3,2,1,0:T(8,128)(2,1)S(1)} %bitcast.17), channel_id=1, source_target_pairs={{0,2},{1,3},{2,0},{3,1},{4,6},{5,7},{6,4},{7,5},{8,10},{9,11},{10,... | collective-permute-start | bytes 294920 | tf_op jit(solution)/shard_map/ppermute | solution.py:24
  15.0 2.4 %collective-permute-start.1 = (bf16[2,24,16,128]{3,2,1,0:T(8,128)(2,1)S(1)}, bf16[2,24,16,128]{3,2,1,0:T(8,128)(2,1)S(1)}, u32[]{:S(2)}, u32[]{:S(2)}) collective-permute-start(bf16[2,24,16,128]{3,2,1,0:T(8,128)(2,1)S(1)} %pad_maximum_fusion.2), channel_id=1, source_target_pairs={{0,1},{1,0},{2,3},{3,2},{4,5},{5,4},{6,7},{7,6},{8,9},{9,8},{10,11... | collective-permute-start | bytes 589832 | tf_op jit(solution)/shard_map/ppermute | solution.py:24
  17.2 1.5 %collective-permute-start.4 = (bf16[2,24,16,128]{3,2,1,0:T(8,128)(2,1)S(1)}, bf16[2,24,16,128]{3,2,1,0:T(8,128)(2,1)S(1)}, u32[]{:S(2)}, u32[]{:S(2)}) collective-permute-start(bf16[2,24,16,128]{3,2,1,0:T(8,128)(2,1)S(1)} %pad_maximum_fusion.3), channel_id=1, source_target_pairs={{0,1},{1,0},{2,3},{3,2},{4,5},{5,4},{6,7},{7,6},{8,9},{9,8},{10,11... | collective-permute-start | bytes 589832 | tf_op jit(solution)/shard_map/ppermute | solution.py:24
  18.7 4.8 %copy-start.1 = (s32[24,12]{0,1:T(8,128)S(1)}, s32[24,12]{0,1:T(8,128)}, u32[]{:S(2)}) copy-start(s32[24,12]{0,1:T(8,128)} %param.6) | copy-start | bytes 3460
  18.7 5.0 %copy-start = (s32[1,126]{1,0:T(1,128)S(1)}, s32[1,126]{1,0:T(1,128)}, u32[]{:S(2)}) copy-start(s32[1,126]{1,0:T(1,128)} %fetch_ref.1) | copy-start | bytes 1516
  20.0 14.5 %collective-permute-start.8 = (bf16[36,16,128]{2,1,0:T(8,128)(2,1)S(1)}, bf16[36,16,128]{2,1,0:T(8,128)(2,1)S(1)}, u32[]{:S(2)}, u32[]{:S(2)}) collective-permute-start(bf16[36,16,128]{2,1,0:T(8,128)(2,1)S(1)} %get-tuple-element.28), channel_id=1, source_target_pairs={{0,4},{4,0},{8,12},{12,8},{16,20},{20,16},{24,28},{28,24},{1,5},{5... | collective-permute-start | bytes 442376 | tf_op jit(solution)/shard_map/ppermute | solution.py:24
  21.6 12.9 %collective-permute-start.9 = (bf16[36,16,128]{2,1,0:T(8,128)(2,1)S(1)}, bf16[36,16,128]{2,1,0:T(8,128)(2,1)S(1)}, u32[]{:S(2)}, u32[]{:S(2)}) collective-permute-start(bf16[36,16,128]{2,1,0:T(8,128)(2,1)S(1)} %get-tuple-element.29), channel_id=1, source_target_pairs={{0,8},{4,12},{8,0},{12,4},{16,24},{20,28},{24,16},{28,20},{1,9},{5... | collective-permute-start | bytes 442376 | tf_op jit(solution)/shard_map/ppermute | solution.py:24
  22.4 12.2 %collective-permute-start.10 = (bf16[36,16,128]{2,1,0:T(8,128)(2,1)S(1)}, bf16[36,16,128]{2,1,0:T(8,128)(2,1)S(1)}, u32[]{:S(2)}, u32[]{:S(2)}) collective-permute-start(bf16[36,16,128]{2,1,0:T(8,128)(2,1)S(1)} %get-tuple-element.30), channel_id=1, source_target_pairs={{0,12},{4,8},{8,4},{12,0},{16,28},{20,24},{24,20},{28,16},{1,13},{... | collective-permute-start | bytes 442376 | tf_op jit(solution)/shard_map/ppermute | solution.py:24
  42.1 14.9 %all-to-all-start = ((bf16[16,24,256]{2,1,0:T(8,128)(2,1)}), bf16[16,24,256]{2,1,0:T(8,128)(2,1)S(1)}, u32[]{:S(2)}, u32[]{:S(2)}) async-start(bf16[16,24,256]{2,1,0:T(8,128)(2,1)} %bitcast.8), calls=%async_computation | async-start | bytes 393216 | tf_op jit(solution)/shard_map/all_to_all | solution.py:458
  48.9 4.6 %collective-permute-start.11 = (bf16[96,256]{1,0:T(8,128)(2,1)S(1)}, bf16[96,256]{1,0:T(8,128)(2,1)S(1)}, u32[]{:S(2)}, u32[]{:S(2)}) collective-permute-start(bf16[96,256]{1,0:T(8,128)(2,1)S(1)} %get-tuple-element.32), channel_id=1, source_target_pairs={{0,2},{1,3},{2,0},{3,1},{4,6},{5,7},{6,4},{7,5},{8,10},{9,11},{10,... | collective-permute-start | bytes 147464 | tf_op jit(solution)/shard_map/ppermute | solution.py:24
  53.5 4.9 %collective-permute-start.12 = (bf16[96,256]{1,0:T(8,128)(2,1)S(1)}, bf16[96,256]{1,0:T(8,128)(2,1)S(1)}, u32[]{:S(2)}, u32[]{:S(2)}) collective-permute-start(bf16[96,256]{1,0:T(8,128)(2,1)S(1)} %add_convert_fusion), channel_id=1, source_target_pairs={{0,1},{1,0},{2,3},{3,2},{4,5},{5,4},{6,7},{7,6},{8,9},{9,8},{10,11... | collective-permute-start | bytes 147464 | tf_op jit(solution)/shard_map/ppermute | solution.py:24
  57.3 1.3 %collective-permute-start.13 = (bf16[96,256]{1,0:T(8,128)(2,1)S(1)}, bf16[96,256]{1,0:T(8,128)(2,1)S(1)}, u32[]{:S(2)}, u32[]{:S(2)}) collective-permute-start(bf16[96,256]{1,0:T(8,128)(2,1)S(1)} %target.1), channel_id=1, source_target_pairs={{0,1},{1,0},{2,3},{3,2},{4,5},{5,4},{6,7},{7,6},{8,9},{9,8},{10,11... | collective-permute-start | bytes 147464 | tf_op jit(solution)/shard_map/ppermute | solution.py:24

commit v3 on v2

--- a/solution.py
+++ b/solution.py
@@ -6,6 +6,7 @@
 from jax.experimental import pallas as pl
 from jax.experimental.pallas import tpu as pltpu
 from jax.sharding import PartitionSpec as P
+
 
 NEIGHBOURS = 26
 LANES = 128
@@ -86,20 +87,18 @@
         table_place(cols, lane, tile_dev, bits),
         jnp.where(source == 0, group_size + entry_int, 2 * group_size),
     )
-    row_ref[...] = jnp.where(
-        source < 0, cols, jnp.where(source == 0, group_size + member.astype(jnp.int32), -1)
-    )
-
-    height = -(-half // 8) * 8
-    by_source = lax.broadcasted_iota(jnp.int32, (height, total), 0) == source
-    by_source = jnp.where(by_source, 1.0, 0.0)
+    row_ref[...] = jnp.where(source < 0, cols, -1)
+
+    kind = lax.broadcasted_iota(jnp.int32, (8, total), 0)
+    chosen = jnp.where(source > 0, 1, source)
+    by_kind = jnp.where(kind == chosen, 1.0, 0.0)
     before = lax.broadcasted_iota(jnp.int32, (total, total), 0) < lax.broadcasted_iota(
         jnp.int32, (total, total), 1
     )
     before = jnp.where(before, 1.0, 0.0).astype(jnp.bfloat16)
-    rank = jnp.dot(by_source.astype(jnp.bfloat16), before, preferred_element_type=jnp.float32)
-    rank = jnp.where(by_source > 0.5, rank, -1.0).astype(jnp.int32)
-    counts = jnp.sum(by_source, axis=1, keepdims=True).astype(jnp.int32)
+    rank = jnp.dot(by_kind.astype(jnp.bfloat16), before, preferred_element_type=jnp.float32)
+    rank = jnp.where(by_kind > 0.5, rank, -1.0).astype(jnp.int32)
+    counts = jnp.sum(by_kind, axis=1, keepdims=True).astype(jnp.int32)
     counts_ref[...] = jnp.broadcast_to(counts, counts_ref.shape)
 
     slot = lax.broadcasted_iota(jnp.int32, (1, total), 1)
@@ -107,19 +106,23 @@
     carried = jnp.concatenate(
         [
             tile.astype(jnp.float32), (slot - tile * slots).astype(jnp.float32), entry, owner,
-            member, jnp.ones((1, total), jnp.float32),
+            member, low,
         ],
         axis=0,
     ).astype(jnp.bfloat16)
     at = lax.broadcasted_iota(jnp.int32, (total, total), 0)
-    for s in range(1, half):
-        chosen = jnp.where(at == rank[s : s + 1], 1.0, 0.0).astype(jnp.bfloat16)
+    for which in range(2):
+        count = counts[which : which + 1]
+        wanted = jnp.where(at < count, at, 0)
+        chosen = jnp.where(wanted == rank[which : which + 1], 1.0, 0.0).astype(jnp.bfloat16)
         listed = lax.dot_general(carried, chosen, NT, preferred_element_type=jnp.float32)
         listed = listed.astype(jnp.int32)
-        lists_ref[3 * s - 3 : 3 * s - 2, :] = listed[0:1] * slots + listed[1:2]
-        lists_ref[3 * s - 2 : 3 * s - 1, :] = listed[2:3]
-        lists_ref[3 * s - 1 : 3 * s, :] = listed[0:1]
-        target_ref[s - 1 : s, :] = jnp.where(listed[5:6] > 0, listed[3:4] * rows + listed[4:5], -1)
+        base = 3 * which
+        lists_ref[base : base + 1, :] = listed[0:1] * slots + listed[1:2]
+        lists_ref[base + 1 : base + 2, :] = listed[2:3] + (listed[5:6] - 1) * (2 * per_peer)
+        lists_ref[base + 2 : base + 3, :] = listed[0:1]
+        row = listed[4:5] if which == 0 else listed[3:4] * rows + listed[4:5]
+        target_ref[which : which + 1, :] = jnp.where(slot < count, row, -1)
 
     index_ref[...] = jnp.full(index_ref.shape, -1.0, jnp.float32)
     groups = fetch_ref.shape[1] // per_peer
@@ -190,19 +193,26 @@
     return both[:rows], both[rows:]
 
 
+def summed(one_hot_rows, place, terms, tile_rows):
+    one_hot = lax.broadcasted_iota(jnp.int32, (one_hot_rows, place.shape[1]), 0) == place
+    one_hot = jnp.where(one_hot, 1.0, 0.0).astype(jnp.bfloat16)
+    sums = jnp.dot(one_hot, terms.astype(jnp.bfloat16), preferred_element_type=jnp.float32)
+    return sums * (1.0 / tile_rows)
+
+
 def own_kernel(
-    slots, group_size, place, row_ref, table_ref, a_hbm,
-    prolong_ref, weight_ref, sums_ref, far_ref, a_ref, product_ref, terms_ref, arrived,
+    slots, place, lists_ref, counts_ref, target_ref, table_ref, a_hbm,
+    prolong_ref, weight_ref, product_ref, far_ref, a_ref, terms_ref, arrived,
 ):
     tile_dev = weight_ref.shape[0]
     mode_count, tile_rows = table_ref.shape[1:]
     pair = 2
     per_step = pair * slots
     steps = tile_dev // pair
+    batch = 2 * BATCH
     diagonal = lax.broadcasted_iota(jnp.int32, (tile_rows, tile_rows), 0) == lax.broadcasted_iota(
         jnp.int32, (tile_rows, tile_rows), 1
     )
-    spread, lane_block = term_constants(per_step, mode_count)
 
     def fetch(step):
         part = pl.ds(step * per_step, per_step)
@@ -212,12 +222,9 @@
     def _(step):
         fetch(step).start()
 
-    def finish(step):
-        first = step * per_step
-        parts = [(prolong_ref[first + k], product_ref[first + k]) for k in range(per_step)]
-        terms_ref[pl.ds(pl.multiple_of(first, 8), per_step), :] = terms_of(parts, spread, lane_block)
-
-    def begin(step):
+    @pl.loop(0, steps)
+    def _(step):
+        fetch(step).wait()
         for i in range(pair):
             tile = step * pair + i
             lead = a_ref[tile * slots].astype(jnp.float32)
@@ -235,83 +242,84 @@
                     prolong_ref[slot + d] = smooth.astype(jnp.bfloat16)
                     product_ref[slot + d] = product.astype(jnp.bfloat16)
 
-    fetch(0).wait()
-    begin(0)
-
-    @pl.loop(1, steps)
+    spread, lane_block = term_constants(batch, mode_count)
+    terms_ref[...] = jnp.zeros_like(terms_ref)
+
+    @pl.loop(0, (counts_ref[0, 0] + batch - 1) // batch)
     def _(step):
-        fetch(step).wait()
-        finish(step - 1)
-        begin(step)
-
-    finish(steps - 1)
+        slot = [lists_ref[0, step * batch + i] for i in range(batch)]
+        parts = [(prolong_ref[f], product_ref[f]) for f in slot]
+        row = pl.multiple_of(step * batch, batch)
+        terms_ref[pl.ds(row, batch), :] = terms_of(parts, spread, lane_block)
 
     total = tile_dev * slots
-    height = group_size + far_ref.shape[0]
-    one_hot = lax.broadcasted_iota(jnp.int32, (height, total), 0) == row_ref[...]
-    one_hot = jnp.where(one_hot, 1.0, 0.0).astype(jnp.bfloat16)
-    sums = jnp.dot(one_hot, terms_ref[...].astype(jnp.bfloat16), preferred_element_type=jnp.float32)
-    sums = sums * (1.0 / tile_rows)
-    sums_ref[...] = sums[:group_size].astype(jnp.bfloat16)
-    far_ref[...] = sums[group_size:]
+    far_ref[...] = summed(far_ref.shape[0], target_ref[0:1, :], terms_ref[0:total, :], tile_rows)
+
+
+def terms_kernel(row_ref, prolong_ref, product_ref, sums_ref, terms_ref):
+    total, mode_count, tile_rows = prolong_ref.shape
+    per_step = 6 * BATCH
+    spread, lane_block = term_constants(per_step, mode_count)
+
+    @pl.loop(0, total // per_step)
+    def _(step):
+        first = step * per_step
+        parts = [(prolong_ref[first + k], product_ref[first + k]) for k in range(per_step)]
+        terms_ref[pl.ds(pl.multiple_of(first, BATCH), per_step), :] = terms_of(parts, spread, lane_block)
+
+    sums = summed(sums_ref.shape[0], row_ref[...], terms_ref[...], tile_rows)
+    sums_ref[...] = sums.astype(jnp.bfloat16)
 
 
 def ghost_kernel(
-    pitch, half, here, lists_ref, counts_ref, target_ref, index_ref, far_ref, a_ref, weight_ref, old_ref,
-    *refs,
+    pitch, half, here, lists_ref, counts_ref, target_ref, index_ref, far_ref, a_ref, weight_ref,
+    old_ref, *refs,
 ):
-    sources = refs[:-5]
-    prolong_ref, out_ref, smooth_ref, product_ref, terms_ref = refs[-5:]
-    mode_count, tile_rows = sources[0].shape[1:]
+    received = refs[: half - 1]
+    prolong_ref, out_ref, table_ref, smooth_ref, product_ref, terms_ref = refs[half - 1 :]
+    mode_count, tile_rows = table_ref.shape[1:]
+    for s, part_ref in enumerate(received):
+        count = part_ref.shape[0]
+        table_ref[s * count : (s + 1) * count] = part_ref[...]
     groups, copies, rows, width = out_ref.shape
     total = a_ref.shape[0]
     batch = 2 * BATCH
     spread, lane_block = term_constants(batch, mode_count)
     terms_ref[...] = jnp.zeros_like(terms_ref)
-    result = jnp.zeros((groups * rows, width), jnp.float32)
-
-    for s, table_ref in enumerate(sources):
-        count = counts_ref[s + 1, 0]
-        steps = (count + batch - 1) // batch
-
-        def begin(step):
-            for i in range(0, batch, 2):
-                at = [jnp.minimum(step * batch + i + d, count - 1) for d in range(2)]
-                slot = [lists_ref[3 * s, a] for a in at]
-                picked = [table_ref[lists_ref[3 * s + 1, a]] for a in at]
-                products = product_pair(picked, [a_ref[f] for f in slot])
-                for d, product in enumerate(products):
-                    weight = weight_ref[pl.ds(lists_ref[3 * s + 2, at[d]], 1), :]
-                    smooth = (-(weight * product)).astype(jnp.bfloat16)
-                    prolong_ref[slot[d]] = smooth
-                    smooth_ref[i + d] = smooth
-                    product_ref[i + d] = product.astype(jnp.bfloat16)
-
-        def finish(step):
-            parts = [(smooth_ref[i], product_ref[i]) for i in range(batch)]
-            row = pl.multiple_of(step * batch, batch)
-            terms_ref[pl.ds(row, batch), :] = terms_of(parts, spread, lane_block)
-
-        @pl.when(count > 0)
-        def _():
-            begin(0)
-
-            @pl.loop(1, steps)
-            def _(step):
-                finish(step - 1)
-                begin(step)
-
-            finish(steps - 1)
-
-        one_hot = (
-            lax.broadcasted_iota(jnp.int32, (groups * rows, total), 0) == target_ref[s : s + 1, :]
-        )
-        one_hot = jnp.where(one_hot, 1.0, 0.0).astype(jnp.bfloat16)
-        result = result + jnp.dot(
-            one_hot, terms_ref[0:total, :].astype(jnp.bfloat16), preferred_element_type=jnp.float32
-        )
-
-    result = (result * (1.0 / tile_rows)).reshape(groups, rows, width)
+    count = counts_ref[1, 0]
+    steps = (count + batch - 1) // batch
+
+    def begin(step):
+        first = step * batch
+        for i in range(0, batch, 2):
+            slot = [lists_ref[3, first + i + d] for d in range(2)]
+            picked = [table_ref[lists_ref[4, first + i + d]] for d in range(2)]
+            products = product_pair(picked, [a_ref[f] for f in slot])
+            for d, product in enumerate(products):
+                weight = weight_ref[pl.ds(lists_ref[5, first + i + d], 1), :]
+                smooth = (-(weight * product)).astype(jnp.bfloat16)
+                prolong_ref[slot[d]] = smooth
+                smooth_ref[i + d] = smooth
+                product_ref[i + d] = product.astype(jnp.bfloat16)
+
+    def finish(step):
+        parts = [(smooth_ref[i], product_ref[i]) for i in range(batch)]
+        row = pl.multiple_of(step * batch, batch)
+        terms_ref[pl.ds(row, batch), :] = terms_of(parts, spread, lane_block)
+
+    @pl.when(count > 0)
+    def _():
+        begin(0)
+
+        @pl.loop(1, steps)
+        def _(step):
+            finish(step - 1)
+            begin(step)
+
+        finish(steps - 1)
+
+    result = summed(groups * rows, target_ref[1:2, :], terms_ref[0:total, :], tile_rows)
+    result = result.reshape(groups, rows, width)
     row_place = lax.broadcasted_iota(jnp.int32, (groups, rows, width), 1)
     group_place = lax.broadcasted_iota(jnp.int32, (groups, rows, width), 0)
     result = jnp.where(group_place == (here[0] ^ half), far_ref[...][None], result)
@@ -352,23 +360,19 @@
     far = xor_permute(modes, "sub", half)
     bits = []
     bit = blk_half
-    own_part, far_part = modes[None], far[None]
+    own_part, far_part = [modes], [far]
     while bit:
-        own_part = jnp.concatenate([own_part, xor_permute(own_part, "blk", bit)], axis=0)
-        far_part = jnp.concatenate([far_part, xor_permute(far_part, "blk", bit)], axis=0)
+        own_part = own_part + [xor_permute(part, "blk", bit) for part in own_part]
+        far_part = far_part + [xor_permute(part, "blk", bit) for part in far_part]
         bits.append(bit)
         bit //= 2
     blank = jnp.zeros((1, mode_count, tile_rows), modes.dtype)
-    table = jnp.concatenate(
-        [
-            own_part.reshape(group_size, mode_count, tile_rows),
-            far_part.reshape(group_size, mode_count, tile_rows),
-            blank,
-        ],
-        axis=0,
-    )
-
-    theirs = jnp.concatenate([xor_permute(fetch_list, "sub", peer) for peer in range(1, half)], axis=0)
+    table = jnp.concatenate(own_part + far_part + [blank], axis=0)
+
+    theirs = []
+    for peer in range(1, half):
+        theirs.append(xor_permute(fetch_list, "sub", peer))
+    theirs = jnp.concatenate(theirs, axis=0)
     owners = theirs // group_size
     places = table_place(theirs % group_size, lane, tile_dev, bits)
     places = places + jnp.where(owners == (me ^ half), group_size, 0)
@@ -381,7 +385,9 @@
         name="pick",
         compiler_params=PARAMS,
     )(here, owners[:, ::per_peer], places, table)
-    received = [xor_permute(picks[peer - 1], "sub", peer) for peer in range(1, half)]
+    received = []
+    for peer in range(1, half):
+        received.append(xor_permute(picks[peer - 1], "sub", peer))
 
     rows = -(-(per_peer + 1) // 8) * 8
     place, own_row, lists, counts, target, index_rows = pl.pallas_call(
@@ -389,9 +395,9 @@
         out_shape=[
             jax.ShapeDtypeStruct((1, slot_total), jnp.int32),
             jax.ShapeDtypeStruct((1, slot_total), jnp.int32),
-            jax.ShapeDtypeStruct((3 * (half - 1), slot_total), jnp.int32),
-            jax.ShapeDtypeStruct((-(-half // 8) * 8, LANES), jnp.int32),
-            jax.ShapeDtypeStruct((half - 1, slot_total), jnp.int32),
+            jax.ShapeDtypeStruct((6, slot_total), jnp.int32),
+            jax.ShapeDtypeStruct((8, LANES), jnp.int32),
+            jax.ShapeDtypeStruct((2, slot_total), jnp.int32),
             jax.ShapeDtypeStruct((sub_count, 1, width), jnp.float32),
         ],
         in_specs=[SMEM, VMEM, VMEM],
@@ -402,29 +408,65 @@
 
     tiles = a_tiles.reshape(slot_total, tile_rows, tile_rows)
     tiles = pltpu.with_memory_space_constraint(tiles, pltpu.HBM)
-    prolong, weight, own_sums, far_sums, tiles = pl.pallas_call(
-        functools.partial(own_kernel, slot_count, group_size),
+    terms_scratch = pltpu.VMEM((slot_total + 2 * BATCH, width), jnp.float32)
+    vectors = (slot_total, mode_count, tile_rows)
+    prolong, weight, product, far_sums, tiles = pl.pallas_call(
+        functools.partial(own_kernel, slot_count),
         out_shape=[
-            pltpu.VMEM((slot_total, mode_count, tile_rows), jnp.bfloat16),
+            pltpu.VMEM(vectors, jnp.bfloat16),
             jax.ShapeDtypeStruct((tile_dev, tile_rows), jnp.float32),
-            jax.ShapeDtypeStruct((group_size, width), jnp.bfloat16),
+            pltpu.VMEM(vectors, jnp.bfloat16),
             jax.ShapeDtypeStruct((rows, width), jnp.float32),
             pltpu.VMEM((slot_total, tile_rows, tile_rows), jnp.bfloat16),
         ],
-        in_specs=[SMEM, VMEM, VMEM, pl.BlockSpec(memory_space=pltpu.HBM)],
+        in_specs=[SMEM, SMEM, SMEM, VMEM, VMEM, pl.BlockSpec(memory_space=pltpu.HBM)],
         out_specs=[VMEM] * 5,
+        scratch_shapes=[terms_scratch, pltpu.SemaphoreType.DMA((tile_dev // 2,))],
+        name="own",
+        compiler_params=PARAMS,
+    )(place.reshape(slot_total), lists, counts, target, table, tiles)
+
+    prolong = pltpu.with_memory_space_constraint(prolong, pltpu.VMEM)
+    product = pltpu.with_memory_space_constraint(product, pltpu.VMEM)
+    tiles = pltpu.with_memory_space_constraint(tiles, pltpu.VMEM)
+    prolong, outgoing = pl.pallas_call(
+        functools.partial(ghost_kernel, per_peer, half),
+        out_shape=[
+            pltpu.VMEM(vectors, jnp.bfloat16),
+            jax.ShapeDtypeStruct((sub_count, blk_half, rows, width), jnp.bfloat16),
+        ],
+        in_specs=[SMEM] * 3 + [VMEM] * (6 + half - 1),
+        out_specs=[VMEM, VMEM],
+        input_output_aliases={8: 0},
         scratch_shapes=[
-            pltpu.VMEM((slot_total, mode_count, tile_rows), jnp.bfloat16),
-            pltpu.VMEM((slot_total, width), jnp.float32),
-            pltpu.SemaphoreType.DMA((tile_dev // 2,)),
-        ],
-        name="own",
-        compiler_params=PARAMS,
-    )(place.reshape(slot_total), own_row, table, tiles)
-
-    prolong = pltpu.with_memory_space_constraint(prolong, pltpu.VMEM)
-    tiles = pltpu.with_memory_space_constraint(tiles, pltpu.VMEM)
-    own_total = own_sums
+            pltpu.VMEM((2 * per_peer * (half - 1), mode_count, tile_rows), jnp.bfloat16),
+            pltpu.VMEM((2 * BATCH, mode_count, tile_rows), jnp.bfloat16),
+            pltpu.VMEM((2 * BATCH, mode_count, tile_rows), jnp.bfloat16),
+            terms_scratch,
+        ],
+        name="ghost",
+        compiler_params=PARAMS,
+    )(here, lists, counts, target, index_rows, far_sums, tiles, weight, prolong, *received)
+    finished = pltpu.with_memory_space_constraint(prolong, pltpu.VMEM)
+
+    groups = [
+        [s * blk_count + high * 2 + core for s in range(sub_count) for high in range(blk_half)]
+        for core in range(2)
+    ]
+    incoming = lax.all_to_all(
+        outgoing.reshape(sub_count * blk_half, rows, width),
+        ("sub", "blk"), split_axis=0, concat_axis=0, axis_index_groups=groups, tiled=True,
+    )
+
+    own_total = pl.pallas_call(
+        terms_kernel,
+        out_shape=jax.ShapeDtypeStruct((group_size, width), jnp.bfloat16),
+        in_specs=[VMEM] * 3,
+        out_specs=VMEM,
+        scratch_shapes=[pltpu.VMEM((slot_total, width), jnp.float32)],
+        name="terms",
+        compiler_params=PARAMS,
+    )(own_row, finished, product)
     bit = blk_half
     while bit:
         other = xor_permute(own_total, "blk", bit)
@@ -432,33 +474,6 @@
         bit //= 2
         if bit:
             own_total = own_total.astype(jnp.bfloat16)
-
-    prolong, outgoing = pl.pallas_call(
-        functools.partial(ghost_kernel, per_peer, half),
-        out_shape=[
-            pltpu.VMEM((slot_total, mode_count, tile_rows), jnp.bfloat16),
-            jax.ShapeDtypeStruct((sub_count, blk_half, rows, width), jnp.bfloat16),
-        ],
-        in_specs=[SMEM] * 3 + [VMEM] * (6 + half - 1),
-        out_specs=[VMEM, VMEM],
-        input_output_aliases={8: 0},
-        scratch_shapes=[
-            pltpu.VMEM((2 * BATCH, mode_count, tile_rows), jnp.bfloat16),
-            pltpu.VMEM((2 * BATCH, mode_count, tile_rows), jnp.bfloat16),
-            pltpu.VMEM((slot_total + 2 * BATCH, width), jnp.float32),
-        ],
-        name="ghost",
-        compiler_params=PARAMS,
-    )(here, lists, counts, target, index_rows, far_sums, tiles, weight, prolong, *received)
-
-    groups = [
-        [s * blk_count + high * 2 + core for s in range(sub_count) for high in range(blk_half)]
-        for core in range(2)
-    ]
-    incoming = lax.all_to_all(
-        outgoing.reshape(sub_count * blk_half, rows, width),
-        ("sub", "blk"), split_axis=0, concat_axis=0, axis_index_groups=groups, tiled=True,
-    )
     arrived = pl.pallas_call(
         functools.partial(target_kernel, per_peer),
         out_shape=jax.ShapeDtypeStruct((group_size, width), jnp.bfloat16),
@@ -480,4 +495,5 @@
         P(("sub", "blk"), None),
     )
     out_specs = (P(("sub", "blk"), None, None, None), P("sub", None))
+
     return jax.shard_map(shards, mesh=mesh, in_specs=in_specs, out_specs=out_specs, check_vma=False)

time: 59.5 us -> 59.5 us (level)
  waiting for transfers between devices: 11.2 us -> 13.7 us
  other arithmetic: 2.99 us -> 0.81 us
  starting transfers between devices: 23.3 us -> 21.7 us
  local copies, waits for them, and re-layouts: 1.38 us -> 2.33 us
    ppermute x14 -> x16, waiting for transfers between devices: 7.88 us -> 13.6 us  [xor_permute(): return lax.ppermute(x, axis, [(i, i ^ bit) for i in range(count)])]
    all_to_all x1, waiting for transfers between devices: 3.37 us -> 0.1 us  [shards(): lax.all_to_all(outgoing.reshape(sub_count * blk_half, rows, width), ('sub...]
    concatenate x5 -> x0, other arithmetic: 2.18 us -> none  [the longest x2 1.85 us: shards(): jnp.concatenate([own_part, xor_permute(own_part, 'blk', bit)], axis=0)]
    pallas_call x1, Pallas kernels: 7.55 us -> 5.69 us  [shards(): pl.pallas_call(functools.partial(ghost_kernel, per_peer, half), out_shape...]
    pallas_call x1 -> x2, Pallas kernels: 9.59 us -> 11.1 us  [the longest x1 7.67 us: shards(): pl.pallas_call(functools.partial(own_kernel, slot_count), out_shape=[pltp...]
    unnamed x6 -> x14, local copies, waits for them, and re-layouts: 1.11 us -> 2.13 us
    all_to_all x1, starting transfers between devices: 6.79 us -> 5.8 us  [shards(): lax.all_to_all(outgoing.reshape(sub_count * blk_half, rows, width), ('sub...]
    pallas_call x1, Pallas kernels: 0.98 us -> 1.74 us  [shards(): pl.pallas_call(functools.partial(pick_kernel, per_peer, half), out_shape=...]
  transfers between devices with their start and end apart: 15 -> 17, of which waited for: 6 -> 5; matrix products, arithmetic and copies ran while one was open for 6% -> 4% of each run, Pallas kernels for 19% -> 21%
where the time goes in v3:
time: 59.5 us; the launch traced here: 59.2 us
  starting transfers between devices  21.7 us (36%)
  Pallas kernels  20 us (34%)
  waiting for transfers between devices  13.7 us (23%)
  local copies, waits for them, and re-layouts  2.33 us (4%)
  other arithmetic  0.81 us (1%)
  between operations  0.8 us (1%)
    ppermute x16, starting transfers between devices, xor_permute(): return lax.ppermute(x, axis, [(i, i ^ bit) for i in range(count)])  15.8 us
    ppermute x16, waiting for transfers between devices, xor_permute(): return lax.ppermute(x, axis, [(i, i ^ bit) for i in range(count)])  13.6 us
    pallas_call x1, Pallas kernels, shards(): pl.pallas_call(functools.partial(own_kernel, slot_count), out_shape=[pltp...  7.67 us
    all_to_all x1, starting transfers between devices, shards(): lax.all_to_all(outgoing.reshape(sub_count * blk_half, rows, width), ('sub...  5.8 us
    pallas_call x1, Pallas kernels, shards(): pl.pallas_call(functools.partial(ghost_kernel, per_peer, half), out_shape...  5.69 us
    pallas_call x1, Pallas kernels, shards(): pl.pallas_call(terms_kernel, out_shape=jax.ShapeDtypeStruct((group_size,...  3.44 us
    unnamed x14, local copies, waits for them, and re-layouts  2.13 us
    pallas_call x1, Pallas kernels, shards(): pl.pallas_call(functools.partial(pick_kernel, per_peer, half), out_shape=...  1.74 us
  transfers between devices with their start and end apart: 17, of which 5 were waited for; matrix products, arithmetic and copies ran while one was open for 4% of the time, Pallas kernels for 21%

profile of v3, /device:TPU:0, one launch (start us, length us, event | category | flops | bytes accessed | tf_op | source)
XLA Modules:
  0.0 59.2 jit_solution(10810312873217887397)
XLA Ops:
  0.6 3.0 %collective-permute-start.7 = (s32[1,126]{1,0:T(1,128)}, s32[1,126]{1,0:T(1,128)S(1)}, u32[]{:S(2)}, u32[]{:S(2)}) collective-permute-start(s32[1,126]{1,0:T(1,128)} %fetch_ref.1), channel_id=1, source_target_pairs={{0,4},{4,0},{8,12},{12,8},{16,20},{20,16},{24,28},{28,24},{1,5},{5... | collective-permute-start | bytes 1520 | tf_op jit(solution)/shard_map/ppermute | solution.py:25
  3.7 1.5 %collective-permute-start.9 = (s32[1,126]{1,0:T(1,128)}, s32[1,126]{1,0:T(1,128)S(1)}, u32[]{:S(2)}, u32[]{:S(2)}) collective-permute-start(s32[1,126]{1,0:T(1,128)} %fetch_ref.1), channel_id=1, source_target_pairs={{0,12},{4,8},{8,4},{12,0},{16,28},{20,24},{24,20},{28,16},{1,13},{... | collective-permute-start | bytes 1520 | tf_op jit(solution)/shard_map/ppermute | solution.py:25
  5.2 1.9 %collective-permute-start = (bf16[24,16,128]{2,1,0:T(8,128)(2,1)}, bf16[24,16,128]{2,1,0:T(8,128)(2,1)S(1)}, u32[]{:S(2)}, u32[]{:S(2)}) collective-permute-start(bf16[24,16,128]{2,1,0:T(8,128)(2,1)} %param.5), channel_id=1, source_target_pairs={{0,2},{1,3},{2,0},{3,1},{4,6},{5,7},{6,4},{7,5},{8,10},{9,11},{10,... | collective-permute-start | bytes 294920 | tf_op jit(solution)/shard_map/ppermute | solution.py:25
  7.2 0.9 %constant_dynamic-update-slice_fusion.8 = bf16[193,16,128]{2,1,0:T(8,128)(2,1)S(1)} fusion(bf16[24,16,128]{2,1,0:T(8,128)(2,1)} %param.5), kind=kLoop, calls=%fused_computation.10 | loop fusion | bytes 196608
  8.2 2.6 %collective-permute-start.3 = (bf16[24,16,128]{2,1,0:T(8,128)(2,1)}, bf16[24,16,128]{2,1,0:T(8,128)(2,1)S(1)}, u32[]{:S(2)}, u32[]{:S(2)}) collective-permute-start(bf16[24,16,128]{2,1,0:T(8,128)(2,1)} %param.5), channel_id=1, source_target_pairs={{0,16},{4,20},{8,24},{12,28},{16,0},{20,4},{24,8},{28,12},{1,17},{... | collective-permute-start | bytes 294920 | tf_op jit(solution)/shard_map/ppermute | solution.py:25
  10.9 5.4 %collective-permute-done.3 = bf16[24,16,128]{2,1,0:T(8,128)(2,1)S(1)} collective-permute-done((bf16[24,16,128]{2,1,0:T(8,128)(2,1)}, bf16[24,16,128]{2,1,0:T(8,128)(2,1)S(1)}, u32[]{:S(2)}, u32[]{:S(2)}) %collective-permute-start.3) | collective-permute-done | bytes 98336 | tf_op jit(solution)/shard_map/ppermute | solution.py:25
  16.4 0.5 collective-permute-start.4
  17.1 4.5 %collective-permute-done.4 = bf16[24,16,128]{2,1,0:T(8,128)(2,1)S(1)} collective-permute-done((bf16[24,16,128]{2,1,0:T(8,128)(2,1)S(1)}, bf16[24,16,128]{2,1,0:T(8,128)(2,1)S(1)}, u32[]{:S(2)}, u32[]{:S(2)}) %collective-permute-start.4) | collective-permute-done | bytes 98336 | tf_op jit(solution)/shard_map/ppermute | solution.py:25
  21.7 1.2 %collective-permute-done.6 = bf16[24,16,128]{2,1,0:T(8,128)(2,1)S(1)} collective-permute-done((bf16[24,16,128]{2,1,0:T(8,128)(2,1)S(1)}, bf16[24,16,128]{2,1,0:T(8,128)(2,1)S(1)}, u32[]{:S(2)}, u32[]{:S(2)}) %collective-permute-start.6) | collective-permute-done | bytes 98336 | tf_op jit(solution)/shard_map/ppermute | solution.py:25
  22.9 1.7 %pick.1 = (bf16[36,16,128]{2,1,0:T(8,128)(2,1)}, bf16[36,16,128]{2,1,0:T(8,128)(2,1)}, bf16[36,16,128]{2,1,0:T(8,128)(2,1)}) custom-call(s32[2]{0:T(128)S(1)} %pad_add_fusion.1.here, s32[3,7]{1,0:T(4,128)S(1)} %slice.3.owner_ref, s32[3,126]{1,0:T(4,128)S(1)} %get-tuple-element.34.place_ref, bf16[193,16,128]{2,1,0:T(8,128)(2,1)S(1)} %constant_dynamic-update-slice_fusion.table_ref), custom_call_target="tpu_custom_call" | custom-call | tf_op jit(solution)/shard_map/pick/pallas_call | solution.py:380
  24.6 1.5 %collective-permute-start.10 = (bf16[36,16,128]{2,1,0:T(8,128)(2,1)}, bf16[36,16,128]{2,1,0:T(8,128)(2,1)S(1)}, u32[]{:S(2)}, u32[]{:S(2)}) collective-permute-start(bf16[36,16,128]{2,1,0:T(8,128)(2,1)} %get-tuple-element.27), channel_id=1, source_target_pairs={{0,4},{4,0},{8,12},{12,8},{16,20},{20,16},{24,28},{28,24},{1,5},{5... | collective-permute-start | bytes 442376 | tf_op jit(solution)/shard_map/ppermute | solution.py:25
  26.1 0.8 %collective-permute-start.11 = (bf16[36,16,128]{2,1,0:T(8,128)(2,1)}, bf16[36,16,128]{2,1,0:T(8,128)(2,1)S(1)}, u32[]{:S(2)}, u32[]{:S(2)}) collective-permute-start(bf16[36,16,128]{2,1,0:T(8,128)(2,1)} %get-tuple-element.28), channel_id=1, source_target_pairs={{0,8},{4,12},{8,0},{12,4},{16,24},{20,28},{24,16},{28,20},{1,9},{5... | collective-permute-start | bytes 442376 | tf_op jit(solution)/shard_map/ppermute | solution.py:25
  26.9 1.2 %collective-permute-start.12 = (bf16[36,16,128]{2,1,0:T(8,128)(2,1)}, bf16[36,16,128]{2,1,0:T(8,128)(2,1)}, u32[]{:S(2)}, u32[]{:S(2)}) collective-permute-start(bf16[36,16,128]{2,1,0:T(8,128)(2,1)} %get-tuple-element.29), channel_id=1, source_target_pairs={{0,12},{4,8},{8,4},{12,0},{16,28},{20,24},{24,20},{28,16},{1,13},{... | collective-permute-start | bytes 442376 | tf_op jit(solution)/shard_map/ppermute | solution.py:25
  28.3 1.1 %prep.1 = (s32[1,288]{1,0:T(1,128)S(1)}, s32[1,288]{1,0:T(1,128)S(1)}, s32[6,288]{1,0:T(8,128)S(1)}, s32[8,128]{1,0:T(8,128)S(1)}, s32[2,288]{1,0:T(2,128)S(1)}, /*index=5*/f32[8,1,256]{2,1,0:T(1,128)S(1)}) custom-call(s32[2]{0:T(128)S(1)} %pad_add_fusion.1.here, s32[1,288]{1,0:T(1,128)S(1)} %reshape.19.cols_ref, s32[1,126]{1,0:T(1,128)S(1)} %copy-done), custom_call_target="tpu_custom_call" | custom-call | tf_op jit(solution)/shard_map/prep/pallas_call | solution.py:393
  29.4 7.7 %own.1 = (bf16[288,16,128]{2,1,0:T(8,128)(2,1)S(1)}, f32[24,128]{1,0:T(8,128)S(1)}, bf16[288,16,128]{2,1,0:T(8,128)(2,1)S(1)}, f32[24,256]{1,0:T(8,128)S(1)}, bf16[288,128,128]{2,1,0:T(8,128)(2,1)S(1)}) custom-call(s32[288]{0:T(512)S(1)} %reduce.place, s32[6,288]{1,0:T(8,128)S(1)} %get-tuple-element.18.lists_ref, s32[8,128]{1,0:T(8,128)S(1)} %get-tuple-element.19.counts_ref, ...), custom_call_target="tpu_custom_call" | custom-call | tf_op jit(solution)/shard_map/own/pallas_call | solution.py:413
  37.2 5.7 %ghost.1 = (bf16[288,16,128]{2,1,0:T(8,128)(2,1)S(1)}, bf16[8,2,24,256]{3,2,1,0:T(8,128)(2,1)}) custom-call(s32[2]{0:T(128)S(1)} %pad_add_fusion.1.here, s32[6,288]{1,0:T(8,128)S(1)} %get-tuple-element.18.lists_ref, s32[8,128]{1,0:T(8,128)S(1)} %get-tuple-element.19.counts_ref, ...), custom_call_target="tpu_custom_call", output_to_operand_aliasing={{0}: (8, {})} | custom-call | tf_op jit(solution)/shard_map/ghost/pallas_call | solution.py:432
  42.9 5.8 %all-to-all-start = ((bf16[16,24,256]{2,1,0:T(8,128)(2,1)}), bf16[16,24,256]{2,1,0:T(8,128)(2,1)S(1)}, u32[]{:S(2)}, u32[]{:S(2)}) async-start(bf16[16,24,256]{2,1,0:T(8,128)(2,1)} %bitcast.4), calls=%async_computation | async-start | bytes 393216 | tf_op jit(solution)/shard_map/all_to_all | solution.py:456
  48.7 3.4 %terms.1 = bf16[96,256]{1,0:T(8,128)(2,1)S(1)} custom-call(s32[1,288]{1,0:T(1,128)S(1)} %get-tuple-element.31.row_ref, bf16[288,16,128]{2,1,0:T(8,128)(2,1)S(1)} %get-tuple-element.30.prolong_ref, bf16[288,16,128]{2,1,0:T(8,128)(2,1)S(1)} %get-tuple-element.32.product_ref), custom_call_target="tpu_custom_call" | custom-call | tf_op jit(solution)/shard_map/terms/pallas_call | solution.py:461
  52.1 2.0 %collective-permute-start.13 = (bf16[96,256]{1,0:T(8,128)(2,1)S(1)}, bf16[96,256]{1,0:T(8,128)(2,1)S(1)}, u32[]{:S(2)}, u32[]{:S(2)}) collective-permute-start(bf16[96,256]{1,0:T(8,128)(2,1)S(1)} %terms.1), channel_id=1, source_target_pairs={{0,2},{1,3},{2,0},{3,1},{4,6},{5,7},{6,4},{7,5},{8,10},{9,11},{10,... | collective-permute-start | bytes 147464 | tf_op jit(solution)/shard_map/ppermute | solution.py:25
  54.1 2.4 %collective-permute-done.13 = bf16[96,256]{1,0:T(8,128)(2,1)S(1)} collective-permute-done((bf16[96,256]{1,0:T(8,128)(2,1)S(1)}, bf16[96,256]{1,0:T(8,128)(2,1)S(1)}, u32[]{:S(2)}, u32[]{:S(2)}) %collective-permute-start.13) | collective-permute-done | bytes 49184 | tf_op jit(solution)/shard_map/ppermute | solution.py:25
  56.7 0.3 target.1
  57.1 0.5 collective-permute-start.15
  57.5 1.0 %copy.18 = bf16[24,12,16,128]{3,2,1,0:T(8,128)(2,1)} copy(bf16[24,12,16,128]{3,2,1,0:T(8,128)(2,1)S(1)} %bitcast.5) | data formatting | bytes 2359296
  58.6 0.7 %add_add_fusion = f32[96,256]{1,0:T(8,128)} fusion(bf16[96,256]{1,0:T(8,128)(2,1)S(1)} %collective-permute-done.15, bf16[96,256]{1,0:T(8,128)(2,1)S(1)} %target.1, bf16[96,256]{1,0:T(8,128)(2,1)S(1)} %collective-permute-done.14, bf16[96,256]{1,0:T(8,128)(2,1)S(1)} %add_convert_fusion), kind=kLoop, calls=%fused_computation | loop fusion | flops 172032 | bytes 294912 | tf_op jit(solution)/shard_map/add | solution.py:486
  (38 shorter events, 1.0 us)
Async XLA Ops:
  0.6 7.6 %collective-permute-start.7 = (s32[1,126]{1,0:T(1,128)}, s32[1,126]{1,0:T(1,128)S(1)}, u32[]{:S(2)}, u32[]{:S(2)}) collective-permute-start(s32[1,126]{1,0:T(1,128)} %fetch_ref.1), channel_id=1, source_target_pairs={{0,4},{4,0},{8,12},{12,8},{16,20},{20,16},{24,28},{28,24},{1,5},{5... | collective-permute-start | bytes 1520 | tf_op jit(solution)/shard_map/ppermute | solution.py:25
  3.7 7.1 %collective-permute-start.9 = (s32[1,126]{1,0:T(1,128)}, s32[1,126]{1,0:T(1,128)S(1)}, u32[]{:S(2)}, u32[]{:S(2)}) collective-permute-start(s32[1,126]{1,0:T(1,128)} %fetch_ref.1), channel_id=1, source_target_pairs={{0,12},{4,8},{8,4},{12,0},{16,28},{20,24},{24,20},{28,16},{1,13},{... | collective-permute-start | bytes 1520 | tf_op jit(solution)/shard_map/ppermute | solution.py:25
  5.2 5.6 %collective-permute-start.8 = (s32[1,126]{1,0:T(1,128)}, s32[1,126]{1,0:T(1,128)S(1)}, u32[]{:S(2)}, u32[]{:S(2)}) collective-permute-start(s32[1,126]{1,0:T(1,128)} %fetch_ref.1), channel_id=1, source_target_pairs={{0,8},{4,12},{8,0},{12,4},{16,24},{20,28},{24,16},{28,20},{1,9},{5... | collective-permute-start | bytes 1520 | tf_op jit(solution)/shard_map/ppermute | solution.py:25
  5.2 11.8 %collective-permute-start.1 = (bf16[24,16,128]{2,1,0:T(8,128)(2,1)}, bf16[24,16,128]{2,1,0:T(8,128)(2,1)S(1)}, u32[]{:S(2)}, u32[]{:S(2)}) collective-permute-start(bf16[24,16,128]{2,1,0:T(8,128)(2,1)} %param.5), channel_id=1, source_target_pairs={{0,1},{1,0},{2,3},{3,2},{4,5},{5,4},{6,7},{7,6},{8,9},{9,8},{10,11... | collective-permute-start | bytes 294920 | tf_op jit(solution)/shard_map/ppermute | solution.py:25
  5.2 11.6 %collective-permute-start = (bf16[24,16,128]{2,1,0:T(8,128)(2,1)}, bf16[24,16,128]{2,1,0:T(8,128)(2,1)S(1)}, u32[]{:S(2)}, u32[]{:S(2)}) collective-permute-start(bf16[24,16,128]{2,1,0:T(8,128)(2,1)} %param.5), channel_id=1, source_target_pairs={{0,2},{1,3},{2,0},{3,1},{4,6},{5,7},{6,4},{7,5},{8,10},{9,11},{10,... | collective-permute-start | bytes 294920 | tf_op jit(solution)/shard_map/ppermute | solution.py:25
  7.2 20.9 %copy-start.1 = (s32[24,12]{0,1:T(8,128)S(1)}, s32[24,12]{0,1:T(8,128)}, u32[]{:S(2)}) copy-start(s32[24,12]{0,1:T(8,128)} %param.6) | copy-start | bytes 3460
  7.2 21.1 %copy-start = (s32[1,126]{1,0:T(1,128)S(1)}, s32[1,126]{1,0:T(1,128)}, u32[]{:S(2)}) copy-start(s32[1,126]{1,0:T(1,128)} %fetch_ref.1) | copy-start | bytes 1516
  8.2 8.2 %collective-permute-start.3 = (bf16[24,16,128]{2,1,0:T(8,128)(2,1)}, bf16[24,16,128]{2,1,0:T(8,128)(2,1)S(1)}, u32[]{:S(2)}, u32[]{:S(2)}) collective-permute-start(bf16[24,16,128]{2,1,0:T(8,128)(2,1)} %param.5), channel_id=1, source_target_pairs={{0,16},{4,20},{8,24},{12,28},{16,0},{20,4},{24,8},{28,12},{1,17},{... | collective-permute-start | bytes 294920 | tf_op jit(solution)/shard_map/ppermute | solution.py:25
  16.4 5.3 %collective-permute-start.5 = (bf16[24,16,128]{2,1,0:T(8,128)(2,1)S(1)}, bf16[24,16,128]{2,1,0:T(8,128)(2,1)S(1)}, u32[]{:S(2)}, u32[]{:S(2)}) collective-permute-start(bf16[24,16,128]{2,1,0:T(8,128)(2,1)S(1)} %collective-permute-done.3), channel_id=1, source_target_pairs={{0,1},{1,0},{2,3},{3,2},{4,5},{5,4},{6,7},{7,6},{8,9},{9,8},{10,11... | collective-permute-start | bytes 294920 | tf_op jit(solution)/shard_map/ppermute | solution.py:25
  16.4 5.2 %collective-permute-start.4 = (bf16[24,16,128]{2,1,0:T(8,128)(2,1)S(1)}, bf16[24,16,128]{2,1,0:T(8,128)(2,1)S(1)}, u32[]{:S(2)}, u32[]{:S(2)}) collective-permute-start(bf16[24,16,128]{2,1,0:T(8,128)(2,1)S(1)} %collective-permute-done.3), channel_id=1, source_target_pairs={{0,2},{1,3},{2,0},{3,1},{4,6},{5,7},{6,4},{7,5},{8,10},{9,11},{10,... | collective-permute-start | bytes 294920 | tf_op jit(solution)/shard_map/ppermute | solution.py:25
  16.8 4.8 %collective-permute-start.2 = (bf16[24,16,128]{2,1,0:T(8,128)(2,1)S(1)}, bf16[24,16,128]{2,1,0:T(8,128)(2,1)S(1)}, u32[]{:S(2)}, u32[]{:S(2)}) collective-permute-start(bf16[24,16,128]{2,1,0:T(8,128)(2,1)S(1)} %collective-permute-done), channel_id=1, source_target_pairs={{0,1},{1,0},{2,3},{3,2},{4,5},{5,4},{6,7},{7,6},{8,9},{9,8},{10,11... | collective-permute-start | bytes 294920 | tf_op jit(solution)/shard_map/ppermute | solution.py:25
  21.6 1.3 %collective-permute-start.6 = (bf16[24,16,128]{2,1,0:T(8,128)(2,1)S(1)}, bf16[24,16,128]{2,1,0:T(8,128)(2,1)S(1)}, u32[]{:S(2)}, u32[]{:S(2)}) collective-permute-start(bf16[24,16,128]{2,1,0:T(8,128)(2,1)S(1)} %collective-permute-done.4), channel_id=1, source_target_pairs={{0,1},{1,0},{2,3},{3,2},{4,5},{5,4},{6,7},{7,6},{8,9},{9,8},{10,11... | collective-permute-start | bytes 294920 | tf_op jit(solution)/shard_map/ppermute | solution.py:25
  24.6 12.5 %collective-permute-start.10 = (bf16[36,16,128]{2,1,0:T(8,128)(2,1)}, bf16[36,16,128]{2,1,0:T(8,128)(2,1)S(1)}, u32[]{:S(2)}, u32[]{:S(2)}) collective-permute-start(bf16[36,16,128]{2,1,0:T(8,128)(2,1)} %get-tuple-element.27), channel_id=1, source_target_pairs={{0,4},{4,0},{8,12},{12,8},{16,20},{20,16},{24,28},{28,24},{1,5},{5... | collective-permute-start | bytes 442376 | tf_op jit(solution)/shard_map/ppermute | solution.py:25
  26.1 11.0 %collective-permute-start.11 = (bf16[36,16,128]{2,1,0:T(8,128)(2,1)}, bf16[36,16,128]{2,1,0:T(8,128)(2,1)S(1)}, u32[]{:S(2)}, u32[]{:S(2)}) collective-permute-start(bf16[36,16,128]{2,1,0:T(8,128)(2,1)} %get-tuple-element.28), channel_id=1, source_target_pairs={{0,8},{4,12},{8,0},{12,4},{16,24},{20,28},{24,16},{28,20},{1,9},{5... | collective-permute-start | bytes 442376 | tf_op jit(solution)/shard_map/ppermute | solution.py:25
  26.9 10.2 %collective-permute-start.12 = (bf16[36,16,128]{2,1,0:T(8,128)(2,1)}, bf16[36,16,128]{2,1,0:T(8,128)(2,1)}, u32[]{:S(2)}, u32[]{:S(2)}) collective-permute-start(bf16[36,16,128]{2,1,0:T(8,128)(2,1)} %get-tuple-element.29), channel_id=1, source_target_pairs={{0,12},{4,8},{8,4},{12,0},{16,28},{20,24},{24,20},{28,16},{1,13},{... | collective-permute-start | bytes 442376 | tf_op jit(solution)/shard_map/ppermute | solution.py:25
  42.9 13.9 %all-to-all-start = ((bf16[16,24,256]{2,1,0:T(8,128)(2,1)}), bf16[16,24,256]{2,1,0:T(8,128)(2,1)S(1)}, u32[]{:S(2)}, u32[]{:S(2)}) async-start(bf16[16,24,256]{2,1,0:T(8,128)(2,1)} %bitcast.4), calls=%async_computation | async-start | bytes 393216 | tf_op jit(solution)/shard_map/all_to_all | solution.py:456
  52.1 4.4 %collective-permute-start.13 = (bf16[96,256]{1,0:T(8,128)(2,1)S(1)}, bf16[96,256]{1,0:T(8,128)(2,1)S(1)}, u32[]{:S(2)}, u32[]{:S(2)}) collective-permute-start(bf16[96,256]{1,0:T(8,128)(2,1)S(1)} %terms.1), channel_id=1, source_target_pairs={{0,2},{1,3},{2,0},{3,1},{4,6},{5,7},{6,4},{7,5},{8,10},{9,11},{10,... | collective-permute-start | bytes 147464 | tf_op jit(solution)/shard_map/ppermute | solution.py:25
  56.5 2.0 %collective-permute-start.14 = (bf16[96,256]{1,0:T(8,128)(2,1)S(1)}, bf16[96,256]{1,0:T(8,128)(2,1)S(1)}, u32[]{:S(2)}, u32[]{:S(2)}) collective-permute-start(bf16[96,256]{1,0:T(8,128)(2,1)S(1)} %add_convert_fusion), channel_id=1, source_target_pairs={{0,1},{1,0},{2,3},{3,2},{4,5},{5,4},{6,7},{7,6},{8,9},{9,8},{10,11... | collective-permute-start | bytes 147464 | tf_op jit(solution)/shard_map/ppermute | solution.py:25
  57.1 1.5 %collective-permute-start.15 = (bf16[96,256]{1,0:T(8,128)(2,1)S(1)}, bf16[96,256]{1,0:T(8,128)(2,1)S(1)}, u32[]{:S(2)}, u32[]{:S(2)}) collective-permute-start(bf16[96,256]{1,0:T(8,128)(2,1)S(1)} %target.1), channel_id=1, source_target_pairs={{0,1},{1,0},{2,3},{3,2},{4,5},{5,4},{6,7},{7,6},{8,9},{9,8},{10,11... | collective-permute-start | bytes 147464 | tf_op jit(solution)/shard_map/ppermute | solution.py:25

commit v4 on v3

--- a/solution.py
+++ b/solution.py
@@ -13,6 +13,7 @@
 BATCH = 8
 
 damping = 2.0 / 3.0
+
 
 VMEM = pl.BlockSpec(memory_space=pltpu.VMEM)
 SMEM = pl.BlockSpec(memory_space=pltpu.SMEM)
@@ -55,7 +56,8 @@
 
 def prep_kernel(
     slots, tile_dev, per_peer, rows, half, bits, here,
-    cols_ref, fetch_ref, place_ref, row_ref, lists_ref, counts_ref, target_ref, index_ref,
+    cols_ref, fetch_ref, place_ref, row_ref, far_slot_ref, slot_ref, entry_ref, tile_ref, counts_ref,
+    target_ref, index_ref,
 ):
     me, lane = here[0], here[1]
     total, ghosts = cols_ref.shape[1], fetch_ref.shape[1]
@@ -117,10 +119,10 @@
         chosen = jnp.where(wanted == rank[which : which + 1], 1.0, 0.0).astype(jnp.bfloat16)
         listed = lax.dot_general(carried, chosen, NT, preferred_element_type=jnp.float32)
         listed = listed.astype(jnp.int32)
-        base = 3 * which
-        lists_ref[base : base + 1, :] = listed[0:1] * slots + listed[1:2]
-        lists_ref[base + 1 : base + 2, :] = listed[2:3] + (listed[5:6] - 1) * (2 * per_peer)
-        lists_ref[base + 2 : base + 3, :] = listed[0:1]
+        (far_slot_ref, slot_ref)[which][...] = listed[0:1] * slots + listed[1:2]
+        if which:
+            entry_ref[...] = listed[2:3] + (listed[5:6] - 1) * (2 * per_peer)
+            tile_ref[...] = listed[0:1]
         row = listed[4:5] if which == 0 else listed[3:4] * rows + listed[4:5]
         target_ref[which : which + 1, :] = jnp.where(slot < count, row, -1)
 
@@ -201,12 +203,12 @@
 
 
 def own_kernel(
-    slots, place, lists_ref, counts_ref, target_ref, table_ref, a_hbm,
+    slots, place, far_slot, counts_ref, target_ref, table_ref, a_hbm,
     prolong_ref, weight_ref, product_ref, far_ref, a_ref, terms_ref, arrived,
 ):
     tile_dev = weight_ref.shape[0]
     mode_count, tile_rows = table_ref.shape[1:]
-    pair = 2
+    pair = 4
     per_step = pair * slots
     steps = tile_dev // pair
     batch = 2 * BATCH
@@ -230,7 +232,7 @@
             lead = a_ref[tile * slots].astype(jnp.float32)
             entries = jnp.sum(jnp.where(diagonal, lead, 0.0), axis=0, keepdims=True)
             weight = damping * (1.0 / entries)
-            weight_ref[pl.ds(tile, 1), :] = weight
+            weight_ref[tile] = weight
             for k in range(0, slots, 2):
                 slot = tile * slots + k
                 picked = [table_ref[place[slot]], table_ref[place[slot + 1]]]
@@ -247,7 +249,7 @@
 
     @pl.loop(0, (counts_ref[0, 0] + batch - 1) // batch)
     def _(step):
-        slot = [lists_ref[0, step * batch + i] for i in range(batch)]
+        slot = [far_slot[step * batch + i] for i in range(batch)]
         parts = [(prolong_ref[f], product_ref[f]) for f in slot]
         row = pl.multiple_of(step * batch, batch)
         terms_ref[pl.ds(row, batch), :] = terms_of(parts, spread, lane_block)
@@ -272,7 +274,7 @@
 
 
 def ghost_kernel(
-    pitch, half, here, lists_ref, counts_ref, target_ref, index_ref, far_ref, a_ref, weight_ref,
+    pitch, half, here, slots, entries, tiles, counts_ref, target_ref, index_ref, far_ref, a_ref, weight_ref,
     old_ref, *refs,
 ):
     received = refs[: half - 1]
@@ -292,11 +294,11 @@
     def begin(step):
         first = step * batch
         for i in range(0, batch, 2):
-            slot = [lists_ref[3, first + i + d] for d in range(2)]
-            picked = [table_ref[lists_ref[4, first + i + d]] for d in range(2)]
+            slot = [slots[first + i + d] for d in range(2)]
+            picked = [table_ref[entries[first + i + d]] for d in range(2)]
             products = product_pair(picked, [a_ref[f] for f in slot])
             for d, product in enumerate(products):
-                weight = weight_ref[pl.ds(lists_ref[5, first + i + d], 1), :]
+                weight = weight_ref[tiles[first + i + d]]
                 smooth = (-(weight * product)).astype(jnp.bfloat16)
                 prolong_ref[slot[d]] = smooth
                 smooth_ref[i + d] = smooth
@@ -379,7 +381,7 @@
     here = jnp.stack([me, lane]).astype(jnp.int32)
     picks = pl.pallas_call(
         functools.partial(pick_kernel, per_peer, half),
-        out_shape=[jax.ShapeDtypeStruct((2 * per_peer, mode_count, tile_rows), modes.dtype)] * (half - 1),
+        out_shape=[pltpu.VMEM((2 * per_peer, mode_count, tile_rows), modes.dtype)] * (half - 1),
         in_specs=[SMEM, SMEM, SMEM, VMEM],
         out_specs=[VMEM] * (half - 1),
         name="pick",
@@ -390,21 +392,20 @@
         received.append(xor_permute(picks[peer - 1], "sub", peer))
 
     rows = -(-(per_peer + 1) // 8) * 8
-    place, own_row, lists, counts, target, index_rows = pl.pallas_call(
+    columns = col_tiles.reshape(1, slot_total)
+    place, own_row, far_slot, slot, entry, tile, counts, target, index_rows = pl.pallas_call(
         functools.partial(prep_kernel, slot_count, tile_dev, per_peer, rows, half, tuple(bits)),
         out_shape=[
-            jax.ShapeDtypeStruct((1, slot_total), jnp.int32),
-            jax.ShapeDtypeStruct((1, slot_total), jnp.int32),
-            jax.ShapeDtypeStruct((6, slot_total), jnp.int32),
+            *[jax.ShapeDtypeStruct((1, slot_total), jnp.int32)] * 6,
             jax.ShapeDtypeStruct((8, LANES), jnp.int32),
             jax.ShapeDtypeStruct((2, slot_total), jnp.int32),
             jax.ShapeDtypeStruct((sub_count, 1, width), jnp.float32),
         ],
         in_specs=[SMEM, VMEM, VMEM],
-        out_specs=[VMEM] * 6,
+        out_specs=[VMEM] * 9,
         name="prep",
         compiler_params=PARAMS,
-    )(here, col_tiles.reshape(1, slot_total), fetch_list)
+    )(here, columns, fetch_list)
 
     tiles = a_tiles.reshape(slot_total, tile_rows, tile_rows)
     tiles = pltpu.with_memory_space_constraint(tiles, pltpu.HBM)
@@ -414,17 +415,17 @@
         functools.partial(own_kernel, slot_count),
         out_shape=[
             pltpu.VMEM(vectors, jnp.bfloat16),
-            jax.ShapeDtypeStruct((tile_dev, tile_rows), jnp.float32),
+            jax.ShapeDtypeStruct((tile_dev, 1, tile_rows), jnp.float32),
             pltpu.VMEM(vectors, jnp.bfloat16),
             jax.ShapeDtypeStruct((rows, width), jnp.float32),
             pltpu.VMEM((slot_total, tile_rows, tile_rows), jnp.bfloat16),
         ],
         in_specs=[SMEM, SMEM, SMEM, VMEM, VMEM, pl.BlockSpec(memory_space=pltpu.HBM)],
         out_specs=[VMEM] * 5,
-        scratch_shapes=[terms_scratch, pltpu.SemaphoreType.DMA((tile_dev // 2,))],
+        scratch_shapes=[terms_scratch, pltpu.SemaphoreType.DMA((tile_dev // 4,))],
         name="own",
         compiler_params=PARAMS,
-    )(place.reshape(slot_total), lists, counts, target, table, tiles)
+    )(place.reshape(slot_total), far_slot.reshape(slot_total), counts, target, table, tiles)
 
     prolong = pltpu.with_memory_space_constraint(prolong, pltpu.VMEM)
     product = pltpu.with_memory_space_constraint(product, pltpu.VMEM)
@@ -435,9 +436,9 @@
             pltpu.VMEM(vectors, jnp.bfloat16),
             jax.ShapeDtypeStruct((sub_count, blk_half, rows, width), jnp.bfloat16),
         ],
-        in_specs=[SMEM] * 3 + [VMEM] * (6 + half - 1),
+        in_specs=[SMEM] * 5 + [VMEM] * (6 + half - 1),
         out_specs=[VMEM, VMEM],
-        input_output_aliases={8: 0},
+        input_output_aliases={10: 0},
         scratch_shapes=[
             pltpu.VMEM((2 * per_peer * (half - 1), mode_count, tile_rows), jnp.bfloat16),
             pltpu.VMEM((2 * BATCH, mode_count, tile_rows), jnp.bfloat16),
@@ -446,7 +447,10 @@
         ],
         name="ghost",
         compiler_params=PARAMS,
-    )(here, lists, counts, target, index_rows, far_sums, tiles, weight, prolong, *received)
+    )(
+        here, slot.reshape(slot_total), entry.reshape(slot_total), tile.reshape(slot_total), counts,
+        target, index_rows, far_sums, tiles, weight, prolong, *received,
+    )
     finished = pltpu.with_memory_space_constraint(prolong, pltpu.VMEM)
 
     groups = [

time: 59.5 us -> 59 us (level)
  Pallas kernels: 20 us -> 19.4 us
  transfers between devices with their start and end apart: 17 -> 17, of which waited for: 5 -> 5; matrix products, arithmetic and copies ran while one was open for 4% -> 4% of each run, Pallas kernels for 21% -> 20%
where the time goes in v4:
time: 59 us; the launch traced here: 58.7 us
  starting transfers between devices  21.7 us (37%)
  Pallas kernels  19.4 us (33%)
  waiting for transfers between devices  13.6 us (23%)
  local copies, waits for them, and re-layouts  2.33 us (4%)
  other arithmetic  0.89 us (2%)
  between operations  0.8 us (1%)
    ppermute x16, starting transfers between devices, xor_permute(): return lax.ppermute(x, axis, [(i, i ^ bit) for i in range(count)])  15.9 us
    ppermute x16, waiting for transfers between devices, xor_permute(): return lax.ppermute(x, axis, [(i, i ^ bit) for i in range(count)])  13.5 us
    pallas_call x1, Pallas kernels, shards(): pl.pallas_call(functools.partial(own_kernel, slot_count), out_shape=[pltp...  7.09 us
    all_to_all x1, starting transfers between devices, shards(): lax.all_to_all(outgoing.reshape(sub_count * blk_half, rows, width), ('sub...  5.8 us
    pallas_call x1, Pallas kernels, shards(): pl.pallas_call(functools.partial(ghost_kernel, per_peer, half), out_shape...  5.7 us
    pallas_call x1, Pallas kernels, shards(): pl.pallas_call(terms_kernel, out_shape=jax.ShapeDtypeStruct((group_size,...  3.44 us
    unnamed x14, local copies, waits for them, and re-layouts  2.13 us
    pallas_call x1, Pallas kernels, shards(): pl.pallas_call(functools.partial(pick_kernel, per_peer, half), out_shape=...  1.72 us
  transfers between devices with their start and end apart: 17, of which 5 were waited for; matrix products, arithmetic and copies ran while one was open for 4% of the time, Pallas kernels for 20%

profile of v4, /device:TPU:0, one launch (start us, length us, event | category | flops | bytes accessed | tf_op | source)
XLA Modules:
  0.0 58.7 jit_solution(5817766210395117791)
XLA Ops:
  0.6 3.0 %collective-permute-start.7 = (s32[1,126]{1,0:T(1,128)}, s32[1,126]{1,0:T(1,128)S(1)}, u32[]{:S(2)}, u32[]{:S(2)}) collective-permute-start(s32[1,126]{1,0:T(1,128)} %fetch_ref.1), channel_id=1, source_target_pairs={{0,4},{4,0},{8,12},{12,8},{16,20},{20,16},{24,28},{28,24},{1,5},{5... | collective-permute-start | bytes 1520 | tf_op jit(solution)/shard_map/ppermute | solution.py:26
  3.7 1.5 %collective-permute-start.9 = (s32[1,126]{1,0:T(1,128)}, s32[1,126]{1,0:T(1,128)S(1)}, u32[]{:S(2)}, u32[]{:S(2)}) collective-permute-start(s32[1,126]{1,0:T(1,128)} %fetch_ref.1), channel_id=1, source_target_pairs={{0,12},{4,8},{8,4},{12,0},{16,28},{20,24},{24,20},{28,16},{1,13},{... | collective-permute-start | bytes 1520 | tf_op jit(solution)/shard_map/ppermute | solution.py:26
  5.2 1.9 %collective-permute-start = (bf16[24,16,128]{2,1,0:T(8,128)(2,1)}, bf16[24,16,128]{2,1,0:T(8,128)(2,1)S(1)}, u32[]{:S(2)}, u32[]{:S(2)}) collective-permute-start(bf16[24,16,128]{2,1,0:T(8,128)(2,1)} %param.5), channel_id=1, source_target_pairs={{0,2},{1,3},{2,0},{3,1},{4,6},{5,7},{6,4},{7,5},{8,10},{9,11},{10,... | collective-permute-start | bytes 294920 | tf_op jit(solution)/shard_map/ppermute | solution.py:26
  7.2 0.9 %constant_dynamic-update-slice_fusion.8 = bf16[193,16,128]{2,1,0:T(8,128)(2,1)S(1)} fusion(bf16[24,16,128]{2,1,0:T(8,128)(2,1)} %param.5), kind=kLoop, calls=%fused_computation.10 | loop fusion | bytes 196608
  8.2 2.6 %collective-permute-start.3 = (bf16[24,16,128]{2,1,0:T(8,128)(2,1)}, bf16[24,16,128]{2,1,0:T(8,128)(2,1)S(1)}, u32[]{:S(2)}, u32[]{:S(2)}) collective-permute-start(bf16[24,16,128]{2,1,0:T(8,128)(2,1)} %param.5), channel_id=1, source_target_pairs={{0,16},{4,20},{8,24},{12,28},{16,0},{20,4},{24,8},{28,12},{1,17},{... | collective-permute-start | bytes 294920 | tf_op jit(solution)/shard_map/ppermute | solution.py:26
  10.9 5.4 %collective-permute-done.3 = bf16[24,16,128]{2,1,0:T(8,128)(2,1)S(1)} collective-permute-done((bf16[24,16,128]{2,1,0:T(8,128)(2,1)}, bf16[24,16,128]{2,1,0:T(8,128)(2,1)S(1)}, u32[]{:S(2)}, u32[]{:S(2)}) %collective-permute-start.3) | collective-permute-done | bytes 98336 | tf_op jit(solution)/shard_map/ppermute | solution.py:26
  16.4 0.5 collective-permute-start.4
  17.1 4.5 %collective-permute-done.4 = bf16[24,16,128]{2,1,0:T(8,128)(2,1)S(1)} collective-permute-done((bf16[24,16,128]{2,1,0:T(8,128)(2,1)S(1)}, bf16[24,16,128]{2,1,0:T(8,128)(2,1)S(1)}, u32[]{:S(2)}, u32[]{:S(2)}) %collective-permute-start.4) | collective-permute-done | bytes 98336 | tf_op jit(solution)/shard_map/ppermute | solution.py:26
  21.7 1.2 %collective-permute-done.6 = bf16[24,16,128]{2,1,0:T(8,128)(2,1)S(1)} collective-permute-done((bf16[24,16,128]{2,1,0:T(8,128)(2,1)S(1)}, bf16[24,16,128]{2,1,0:T(8,128)(2,1)S(1)}, u32[]{:S(2)}, u32[]{:S(2)}) %collective-permute-start.6) | collective-permute-done | bytes 98336 | tf_op jit(solution)/shard_map/ppermute | solution.py:26
  22.9 1.7 %pick.1 = (bf16[36,16,128]{2,1,0:T(8,128)(2,1)}, bf16[36,16,128]{2,1,0:T(8,128)(2,1)}, bf16[36,16,128]{2,1,0:T(8,128)(2,1)}) custom-call(s32[2]{0:T(128)S(1)} %pad_add_fusion.1.here, s32[3,7]{1,0:T(4,128)S(1)} %slice.3.owner_ref, s32[3,126]{1,0:T(4,128)S(1)} %get-tuple-element.40.place_ref, bf16[193,16,128]{2,1,0:T(8,128)(2,1)S(1)} %constant_dynamic-update-slice_fusion.table_ref), custom_call_target="tpu_custom_call" | custom-call | tf_op jit(solution)/shard_map/pick/pallas_call | solution.py:382
  24.6 1.5 %collective-permute-start.10 = (bf16[36,16,128]{2,1,0:T(8,128)(2,1)}, bf16[36,16,128]{2,1,0:T(8,128)(2,1)S(1)}, u32[]{:S(2)}, u32[]{:S(2)}) collective-permute-start(bf16[36,16,128]{2,1,0:T(8,128)(2,1)} %get-tuple-element.33), channel_id=1, source_target_pairs={{0,4},{4,0},{8,12},{12,8},{16,20},{20,16},{24,28},{28,24},{1,5},{5... | collective-permute-start | bytes 442376 | tf_op jit(solution)/shard_map/ppermute | solution.py:26
  26.1 0.8 %collective-permute-start.11 = (bf16[36,16,128]{2,1,0:T(8,128)(2,1)}, bf16[36,16,128]{2,1,0:T(8,128)(2,1)S(1)}, u32[]{:S(2)}, u32[]{:S(2)}) collective-permute-start(bf16[36,16,128]{2,1,0:T(8,128)(2,1)} %get-tuple-element.34), channel_id=1, source_target_pairs={{0,8},{4,12},{8,0},{12,4},{16,24},{20,28},{24,16},{28,20},{1,9},{5... | collective-permute-start | bytes 442376 | tf_op jit(solution)/shard_map/ppermute | solution.py:26
  26.9 1.2 %collective-permute-start.12 = (bf16[36,16,128]{2,1,0:T(8,128)(2,1)}, bf16[36,16,128]{2,1,0:T(8,128)(2,1)}, u32[]{:S(2)}, u32[]{:S(2)}) collective-permute-start(bf16[36,16,128]{2,1,0:T(8,128)(2,1)} %get-tuple-element.35), channel_id=1, source_target_pairs={{0,12},{4,8},{8,4},{12,0},{16,28},{20,24},{24,20},{28,16},{1,13},{... | collective-permute-start | bytes 442376 | tf_op jit(solution)/shard_map/ppermute | solution.py:26
  28.3 1.1 %prep.1 = (s32[1,288]{1,0:T(1,128)S(1)}, s32[1,288]{1,0:T(1,128)S(1)}, s32[1,288]{1,0:T(1,128)S(1)}, s32[1,288]{1,0:T(1,128)S(1)}, s32[1,288]{1,0:T(1,128)S(1)},...) custom-call(s32[2]{0:T(128)S(1)} %pad_add_fusion.1.here, ...), custom_call_target="tpu_custom_call" | custom-call | tf_op jit(solution)/shard_map/prep/pallas_call | solution.py:396
  29.5 7.1 %own.1 = (bf16[288,16,128]{2,1,0:T(8,128)(2,1)S(1)}, f32[24,1,128]{2,1,0:T(1,128)S(1)}, bf16[288,16,128]{2,1,0:T(8,128)(2,1)S(1)}, f32[24,256]{1,0:T(8,128)S(1)}, bf16[288,128,128]{2,1,0:T(8,128)(2,1)S(1)}) custom-call(s32[288]{0:T(512)S(1)} %reduce.3.place, s32[288]{0:T(512)S(1)} %reduce.4.far_slot, s32[8,128]{1,0:T(8,128)S(1)} %get-tuple-element.24.counts_ref, ...), custom_call_target="tpu_custom_call" | custom-call | tf_op jit(solution)/shard_map/own/pallas_call | solution.py:414
  36.6 5.7 %ghost.1 = (bf16[288,16,128]{2,1,0:T(8,128)(2,1)S(1)}, bf16[8,2,24,256]{3,2,1,0:T(8,128)(2,1)}) custom-call(s32[2]{0:T(128)S(1)} %pad_add_fusion.1.here, s32[288]{0:T(512)S(1)} %reduce.slots, s32[288]{0:T(512)S(1)} %reduce.1.entries, s32[288]{0:T(512)S(1)} %reduce.2.tiles, ...), custom_call_target="tpu_custom_call", output_to_operand_aliasing={{0}: (10, {})} | custom-call | tf_op jit(solution)/shard_map/ghost/pallas_call | solution.py:433
  42.3 5.8 %all-to-all-start = ((bf16[16,24,256]{2,1,0:T(8,128)(2,1)}), bf16[16,24,256]{2,1,0:T(8,128)(2,1)S(1)}, u32[]{:S(2)}, u32[]{:S(2)}) async-start(bf16[16,24,256]{2,1,0:T(8,128)(2,1)} %bitcast.4), calls=%async_computation | async-start | bytes 393216 | tf_op jit(solution)/shard_map/all_to_all | solution.py:460
  48.2 3.4 %terms.1 = bf16[96,256]{1,0:T(8,128)(2,1)S(1)} custom-call(s32[1,288]{1,0:T(1,128)S(1)} %get-tuple-element.37.row_ref, bf16[288,16,128]{2,1,0:T(8,128)(2,1)S(1)} %get-tuple-element.36.prolong_ref, bf16[288,16,128]{2,1,0:T(8,128)(2,1)S(1)} %get-tuple-element.38.product_ref), custom_call_target="tpu_custom_call" | custom-call | tf_op jit(solution)/shard_map/terms/pallas_call | solution.py:465
  51.6 2.0 %collective-permute-start.13 = (bf16[96,256]{1,0:T(8,128)(2,1)S(1)}, bf16[96,256]{1,0:T(8,128)(2,1)S(1)}, u32[]{:S(2)}, u32[]{:S(2)}) collective-permute-start(bf16[96,256]{1,0:T(8,128)(2,1)S(1)} %terms.1), channel_id=1, source_target_pairs={{0,2},{1,3},{2,0},{3,1},{4,6},{5,7},{6,4},{7,5},{8,10},{9,11},{10,... | collective-permute-start | bytes 147464 | tf_op jit(solution)/shard_map/ppermute | solution.py:26
  53.6 2.4 %collective-permute-done.13 = bf16[96,256]{1,0:T(8,128)(2,1)S(1)} collective-permute-done((bf16[96,256]{1,0:T(8,128)(2,1)S(1)}, bf16[96,256]{1,0:T(8,128)(2,1)S(1)}, u32[]{:S(2)}, u32[]{:S(2)}) %collective-permute-start.13) | collective-permute-done | bytes 49184 | tf_op jit(solution)/shard_map/ppermute | solution.py:26
  56.2 0.3 target.1
  56.6 0.5 collective-permute-start.15
  57.0 1.0 %copy.18 = bf16[24,12,16,128]{3,2,1,0:T(8,128)(2,1)} copy(bf16[24,12,16,128]{3,2,1,0:T(8,128)(2,1)S(1)} %bitcast.5) | data formatting | bytes 2359296
  58.0 0.7 %add_add_fusion = f32[96,256]{1,0:T(8,128)} fusion(bf16[96,256]{1,0:T(8,128)(2,1)S(1)} %collective-permute-done.15, bf16[96,256]{1,0:T(8,128)(2,1)S(1)} %target.1, bf16[96,256]{1,0:T(8,128)(2,1)S(1)} %collective-permute-done.14, bf16[96,256]{1,0:T(8,128)(2,1)S(1)} %add_convert_fusion), kind=kLoop, calls=%fused_computation | loop fusion | flops 172032 | bytes 294912 | tf_op jit(solution)/shard_map/add | solution.py:490
  (42 shorter events, 1.1 us)
Async XLA Ops:
  0.6 7.6 %collective-permute-start.7 = (s32[1,126]{1,0:T(1,128)}, s32[1,126]{1,0:T(1,128)S(1)}, u32[]{:S(2)}, u32[]{:S(2)}) collective-permute-start(s32[1,126]{1,0:T(1,128)} %fetch_ref.1), channel_id=1, source_target_pairs={{0,4},{4,0},{8,12},{12,8},{16,20},{20,16},{24,28},{28,24},{1,5},{5... | collective-permute-start | bytes 1520 | tf_op jit(solution)/shard_map/ppermute | solution.py:26
  3.7 7.1 %collective-permute-start.9 = (s32[1,126]{1,0:T(1,128)}, s32[1,126]{1,0:T(1,128)S(1)}, u32[]{:S(2)}, u32[]{:S(2)}) collective-permute-start(s32[1,126]{1,0:T(1,128)} %fetch_ref.1), channel_id=1, source_target_pairs={{0,12},{4,8},{8,4},{12,0},{16,28},{20,24},{24,20},{28,16},{1,13},{... | collective-permute-start | bytes 1520 | tf_op jit(solution)/shard_map/ppermute | solution.py:26
  5.2 5.6 %collective-permute-start.8 = (s32[1,126]{1,0:T(1,128)}, s32[1,126]{1,0:T(1,128)S(1)}, u32[]{:S(2)}, u32[]{:S(2)}) collective-permute-start(s32[1,126]{1,0:T(1,128)} %fetch_ref.1), channel_id=1, source_target_pairs={{0,8},{4,12},{8,0},{12,4},{16,24},{20,28},{24,16},{28,20},{1,9},{5... | collective-permute-start | bytes 1520 | tf_op jit(solution)/shard_map/ppermute | solution.py:26
  5.2 11.8 %collective-permute-start.1 = (bf16[24,16,128]{2,1,0:T(8,128)(2,1)}, bf16[24,16,128]{2,1,0:T(8,128)(2,1)S(1)}, u32[]{:S(2)}, u32[]{:S(2)}) collective-permute-start(bf16[24,16,128]{2,1,0:T(8,128)(2,1)} %param.5), channel_id=1, source_target_pairs={{0,1},{1,0},{2,3},{3,2},{4,5},{5,4},{6,7},{7,6},{8,9},{9,8},{10,11... | collective-permute-start | bytes 294920 | tf_op jit(solution)/shard_map/ppermute | solution.py:26
  5.2 11.6 %collective-permute-start = (bf16[24,16,128]{2,1,0:T(8,128)(2,1)}, bf16[24,16,128]{2,1,0:T(8,128)(2,1)S(1)}, u32[]{:S(2)}, u32[]{:S(2)}) collective-permute-start(bf16[24,16,128]{2,1,0:T(8,128)(2,1)} %param.5), channel_id=1, source_target_pairs={{0,2},{1,3},{2,0},{3,1},{4,6},{5,7},{6,4},{7,5},{8,10},{9,11},{10,... | collective-permute-start | bytes 294920 | tf_op jit(solution)/shard_map/ppermute | solution.py:26
  7.2 20.9 %copy-start.1 = (s32[24,12]{0,1:T(8,128)S(1)}, s32[24,12]{0,1:T(8,128)}, u32[]{:S(2)}) copy-start(s32[24,12]{0,1:T(8,128)} %param.6) | copy-start | bytes 3460
  7.2 21.1 %copy-start = (s32[1,126]{1,0:T(1,128)S(1)}, s32[1,126]{1,0:T(1,128)}, u32[]{:S(2)}) copy-start(s32[1,126]{1,0:T(1,128)} %fetch_ref.1) | copy-start | bytes 1516
  8.2 8.2 %collective-permute-start.3 = (bf16[24,16,128]{2,1,0:T(8,128)(2,1)}, bf16[24,16,128]{2,1,0:T(8,128)(2,1)S(1)}, u32[]{:S(2)}, u32[]{:S(2)}) collective-permute-start(bf16[24,16,128]{2,1,0:T(8,128)(2,1)} %param.5), channel_id=1, source_target_pairs={{0,16},{4,20},{8,24},{12,28},{16,0},{20,4},{24,8},{28,12},{1,17},{... | collective-permute-start | bytes 294920 | tf_op jit(solution)/shard_map/ppermute | solution.py:26
  16.4 5.3 %collective-permute-start.5 = (bf16[24,16,128]{2,1,0:T(8,128)(2,1)S(1)}, bf16[24,16,128]{2,1,0:T(8,128)(2,1)S(1)}, u32[]{:S(2)}, u32[]{:S(2)}) collective-permute-start(bf16[24,16,128]{2,1,0:T(8,128)(2,1)S(1)} %collective-permute-done.3), channel_id=1, source_target_pairs={{0,1},{1,0},{2,3},{3,2},{4,5},{5,4},{6,7},{7,6},{8,9},{9,8},{10,11... | collective-permute-start | bytes 294920 | tf_op jit(solution)/shard_map/ppermute | solution.py:26
  16.4 5.2 %collective-permute-start.4 = (bf16[24,16,128]{2,1,0:T(8,128)(2,1)S(1)}, bf16[24,16,128]{2,1,0:T(8,128)(2,1)S(1)}, u32[]{:S(2)}, u32[]{:S(2)}) collective-permute-start(bf16[24,16,128]{2,1,0:T(8,128)(2,1)S(1)} %collective-permute-done.3), channel_id=1, source_target_pairs={{0,2},{1,3},{2,0},{3,1},{4,6},{5,7},{6,4},{7,5},{8,10},{9,11},{10,... | collective-permute-start | bytes 294920 | tf_op jit(solution)/shard_map/ppermute | solution.py:26
  16.8 4.8 %collective-permute-start.2 = (bf16[24,16,128]{2,1,0:T(8,128)(2,1)S(1)}, bf16[24,16,128]{2,1,0:T(8,128)(2,1)S(1)}, u32[]{:S(2)}, u32[]{:S(2)}) collective-permute-start(bf16[24,16,128]{2,1,0:T(8,128)(2,1)S(1)} %collective-permute-done), channel_id=1, source_target_pairs={{0,1},{1,0},{2,3},{3,2},{4,5},{5,4},{6,7},{7,6},{8,9},{9,8},{10,11... | collective-permute-start | bytes 294920 | tf_op jit(solution)/shard_map/ppermute | solution.py:26
  21.6 1.3 %collective-permute-start.6 = (bf16[24,16,128]{2,1,0:T(8,128)(2,1)S(1)}, bf16[24,16,128]{2,1,0:T(8,128)(2,1)S(1)}, u32[]{:S(2)}, u32[]{:S(2)}) collective-permute-start(bf16[24,16,128]{2,1,0:T(8,128)(2,1)S(1)} %collective-permute-done.4), channel_id=1, source_target_pairs={{0,1},{1,0},{2,3},{3,2},{4,5},{5,4},{6,7},{7,6},{8,9},{9,8},{10,11... | collective-permute-start | bytes 294920 | tf_op jit(solution)/shard_map/ppermute | solution.py:26
  24.6 12.0 %collective-permute-start.10 = (bf16[36,16,128]{2,1,0:T(8,128)(2,1)}, bf16[36,16,128]{2,1,0:T(8,128)(2,1)S(1)}, u32[]{:S(2)}, u32[]{:S(2)}) collective-permute-start(bf16[36,16,128]{2,1,0:T(8,128)(2,1)} %get-tuple-element.33), channel_id=1, source_target_pairs={{0,4},{4,0},{8,12},{12,8},{16,20},{20,16},{24,28},{28,24},{1,5},{5... | collective-permute-start | bytes 442376 | tf_op jit(solution)/shard_map/ppermute | solution.py:26
  26.1 10.5 %collective-permute-start.11 = (bf16[36,16,128]{2,1,0:T(8,128)(2,1)}, bf16[36,16,128]{2,1,0:T(8,128)(2,1)S(1)}, u32[]{:S(2)}, u32[]{:S(2)}) collective-permute-start(bf16[36,16,128]{2,1,0:T(8,128)(2,1)} %get-tuple-element.34), channel_id=1, source_target_pairs={{0,8},{4,12},{8,0},{12,4},{16,24},{20,28},{24,16},{28,20},{1,9},{5... | collective-permute-start | bytes 442376 | tf_op jit(solution)/shard_map/ppermute | solution.py:26
  26.9 9.7 %collective-permute-start.12 = (bf16[36,16,128]{2,1,0:T(8,128)(2,1)}, bf16[36,16,128]{2,1,0:T(8,128)(2,1)}, u32[]{:S(2)}, u32[]{:S(2)}) collective-permute-start(bf16[36,16,128]{2,1,0:T(8,128)(2,1)} %get-tuple-element.35), channel_id=1, source_target_pairs={{0,12},{4,8},{8,4},{12,0},{16,28},{20,24},{24,20},{28,16},{1,13},{... | collective-permute-start | bytes 442376 | tf_op jit(solution)/shard_map/ppermute | solution.py:26
  42.3 13.9 %all-to-all-start = ((bf16[16,24,256]{2,1,0:T(8,128)(2,1)}), bf16[16,24,256]{2,1,0:T(8,128)(2,1)S(1)}, u32[]{:S(2)}, u32[]{:S(2)}) async-start(bf16[16,24,256]{2,1,0:T(8,128)(2,1)} %bitcast.4), calls=%async_computation | async-start | bytes 393216 | tf_op jit(solution)/shard_map/all_to_all | solution.py:460
  51.6 4.4 %collective-permute-start.13 = (bf16[96,256]{1,0:T(8,128)(2,1)S(1)}, bf16[96,256]{1,0:T(8,128)(2,1)S(1)}, u32[]{:S(2)}, u32[]{:S(2)}) collective-permute-start(bf16[96,256]{1,0:T(8,128)(2,1)S(1)} %terms.1), channel_id=1, source_target_pairs={{0,2},{1,3},{2,0},{3,1},{4,6},{5,7},{6,4},{7,5},{8,10},{9,11},{10,... | collective-permute-start | bytes 147464 | tf_op jit(solution)/shard_map/ppermute | solution.py:26
  56.0 2.0 %collective-permute-start.14 = (bf16[96,256]{1,0:T(8,128)(2,1)S(1)}, bf16[96,256]{1,0:T(8,128)(2,1)S(1)}, u32[]{:S(2)}, u32[]{:S(2)}) collective-permute-start(bf16[96,256]{1,0:T(8,128)(2,1)S(1)} %add_convert_fusion), channel_id=1, source_target_pairs={{0,1},{1,0},{2,3},{3,2},{4,5},{5,4},{6,7},{7,6},{8,9},{9,8},{10,11... | collective-permute-start | bytes 147464 | tf_op jit(solution)/shard_map/ppermute | solution.py:26
  56.6 1.5 %collective-permute-start.15 = (bf16[96,256]{1,0:T(8,128)(2,1)S(1)}, bf16[96,256]{1,0:T(8,128)(2,1)S(1)}, u32[]{:S(2)}, u32[]{:S(2)}) collective-permute-start(bf16[96,256]{1,0:T(8,128)(2,1)S(1)} %target.1), channel_id=1, source_target_pairs={{0,1},{1,0},{2,3},{3,2},{4,5},{5,4},{6,7},{7,6},{8,9},{9,8},{10,11... | collective-permute-start | bytes 147464 | tf_op jit(solution)/shard_map/ppermute | solution.py:26

commit v5 on v4

--- a/solution.py
+++ b/solution.py
@@ -18,6 +18,7 @@
 VMEM = pl.BlockSpec(memory_space=pltpu.VMEM)
 SMEM = pl.BlockSpec(memory_space=pltpu.SMEM)
 PARAMS = pltpu.CompilerParams(vmem_limit_bytes=8 << 20)
+GHOST_PARAMS = pltpu.CompilerParams(vmem_limit_bytes=8 << 20)
 NT = (((1,), (1,)), ((), ()))
 
 
@@ -88,7 +89,7 @@
         source < 0,
         table_place(cols, lane, tile_dev, bits),
         jnp.where(source == 0, group_size + entry_int, 2 * group_size),
-    )
+    )[0]
     row_ref[...] = jnp.where(source < 0, cols, -1)
 
     kind = lax.broadcasted_iota(jnp.int32, (8, total), 0)
@@ -119,10 +120,10 @@
         chosen = jnp.where(wanted == rank[which : which + 1], 1.0, 0.0).astype(jnp.bfloat16)
         listed = lax.dot_general(carried, chosen, NT, preferred_element_type=jnp.float32)
         listed = listed.astype(jnp.int32)
-        (far_slot_ref, slot_ref)[which][...] = listed[0:1] * slots + listed[1:2]
+        (far_slot_ref, slot_ref)[which][...] = (listed[0:1] * slots + listed[1:2])[0]
         if which:
-            entry_ref[...] = listed[2:3] + (listed[5:6] - 1) * (2 * per_peer)
-            tile_ref[...] = listed[0:1]
+            entry_ref[...] = (listed[2:3] + (listed[5:6] - 1) * (2 * per_peer))[0]
+            tile_ref[...] = listed[0]
         row = listed[4:5] if which == 0 else listed[3:4] * rows + listed[4:5]
         target_ref[which : which + 1, :] = jnp.where(slot < count, row, -1)
 
@@ -309,17 +310,14 @@
         row = pl.multiple_of(step * batch, batch)
         terms_ref[pl.ds(row, batch), :] = terms_of(parts, spread, lane_block)
 
-    @pl.when(count > 0)
-    def _():
-        begin(0)
-
-        @pl.loop(1, steps)
-        def _(step):
-            finish(step - 1)
-            begin(step)
-
-        finish(steps - 1)
-
+    begin(0)
+
+    @pl.loop(1, steps)
+    def _(step):
+        finish(step - 1)
+        begin(step)
+
+    finish(steps - 1)
     result = summed(groups * rows, target_ref[1:2, :], terms_ref[0:total, :], tile_rows)
     result = result.reshape(groups, rows, width)
     row_place = lax.broadcasted_iota(jnp.int32, (groups, rows, width), 1)
@@ -381,7 +379,7 @@
     here = jnp.stack([me, lane]).astype(jnp.int32)
     picks = pl.pallas_call(
         functools.partial(pick_kernel, per_peer, half),
-        out_shape=[pltpu.VMEM((2 * per_peer, mode_count, tile_rows), modes.dtype)] * (half - 1),
+        out_shape=[jax.ShapeDtypeStruct((2 * per_peer, mode_count, tile_rows), modes.dtype)] * (half - 1),
         in_specs=[SMEM, SMEM, SMEM, VMEM],
         out_specs=[VMEM] * (half - 1),
         name="pick",
@@ -396,7 +394,9 @@
     place, own_row, far_slot, slot, entry, tile, counts, target, index_rows = pl.pallas_call(
         functools.partial(prep_kernel, slot_count, tile_dev, per_peer, rows, half, tuple(bits)),
         out_shape=[
-            *[jax.ShapeDtypeStruct((1, slot_total), jnp.int32)] * 6,
+            jax.ShapeDtypeStruct((slot_total,), jnp.int32),
+            jax.ShapeDtypeStruct((1, slot_total), jnp.int32),
+            *[jax.ShapeDtypeStruct((slot_total,), jnp.int32)] * 4,
             jax.ShapeDtypeStruct((8, LANES), jnp.int32),
             jax.ShapeDtypeStruct((2, slot_total), jnp.int32),
             jax.ShapeDtypeStruct((sub_count, 1, width), jnp.float32),
@@ -425,7 +425,7 @@
         scratch_shapes=[terms_scratch, pltpu.SemaphoreType.DMA((tile_dev // 4,))],
         name="own",
         compiler_params=PARAMS,
-    )(place.reshape(slot_total), far_slot.reshape(slot_total), counts, target, table, tiles)
+    )(place, far_slot, counts, target, table, tiles)
 
     prolong = pltpu.with_memory_space_constraint(prolong, pltpu.VMEM)
     product = pltpu.with_memory_space_constraint(product, pltpu.VMEM)
@@ -446,9 +446,9 @@
             terms_scratch,
         ],
         name="ghost",
-        compiler_params=PARAMS,
+        compiler_params=GHOST_PARAMS,
     )(
-        here, slot.reshape(slot_total), entry.reshape(slot_total), tile.reshape(slot_total), counts,
+        here, slot, entry, tile, counts,
         target, index_rows, far_sums, tiles, weight, prolong, *received,
     )
     finished = pltpu.with_memory_space_constraint(prolong, pltpu.VMEM)

time: 59 us -> 58.8 us (level)
  no operation moved by 1% of the time
where the time goes in v5:
time: 58.8 us; the launch traced here: 58.6 us
  starting transfers between devices  21.7 us (37%)
  Pallas kernels  19.4 us (33%)
  waiting for transfers between devices  13.6 us (23%)
  local copies, waits for them, and re-layouts  2.33 us (4%)
  between operations  0.8 us (1%)
  other arithmetic  0.79 us (1%)
    ppermute x16, starting transfers between devices, xor_permute(): return lax.ppermute(x, axis, [(i, i ^ bit) for i in range(count)])  15.9 us
    ppermute x16, waiting for transfers between devices, xor_permute(): return lax.ppermute(x, axis, [(i, i ^ bit) for i in range(count)])  13.5 us
    pallas_call x1, Pallas kernels, shards(): pl.pallas_call(functools.partial(own_kernel, slot_count), out_shape=[pltp...  7.09 us
    all_to_all x1, starting transfers between devices, shards(): lax.all_to_all(outgoing.reshape(sub_count * blk_half, rows, width), ('sub...  5.8 us
    pallas_call x1, Pallas kernels, shards(): pl.pallas_call(functools.partial(ghost_kernel, per_peer, half), out_shape...  5.67 us
    pallas_call x1, Pallas kernels, shards(): pl.pallas_call(terms_kernel, out_shape=jax.ShapeDtypeStruct((group_size,...  3.44 us
    unnamed x14, local copies, waits for them, and re-layouts  2.13 us
    pallas_call x1, Pallas kernels, shards(): pl.pallas_call(functools.partial(pick_kernel, per_peer, half), out_shape=...  1.72 us
  transfers between devices with their start and end apart: 17, of which 5 were waited for; matrix products, arithmetic and copies ran while one was open for 4% of the time, Pallas kernels for 20%

profile of v5, /device:TPU:0, one launch (start us, length us, event | category | flops | bytes accessed | tf_op | source)
XLA Modules:
  0.0 58.6 jit_solution(4007084232224030440)
XLA Ops:
  0.6 3.0 %collective-permute-start.7 = (s32[1,126]{1,0:T(1,128)}, s32[1,126]{1,0:T(1,128)S(1)}, u32[]{:S(2)}, u32[]{:S(2)}) collective-permute-start(s32[1,126]{1,0:T(1,128)} %fetch_ref.1), channel_id=1, source_target_pairs={{0,4},{4,0},{8,12},{12,8},{16,20},{20,16},{24,28},{28,24},{1,5},{5... | collective-permute-start | bytes 1520 | tf_op jit(solution)/shard_map/ppermute | solution.py:27
  3.7 1.5 %collective-permute-start.9 = (s32[1,126]{1,0:T(1,128)}, s32[1,126]{1,0:T(1,128)S(1)}, u32[]{:S(2)}, u32[]{:S(2)}) collective-permute-start(s32[1,126]{1,0:T(1,128)} %fetch_ref.1), channel_id=1, source_target_pairs={{0,12},{4,8},{8,4},{12,0},{16,28},{20,24},{24,20},{28,16},{1,13},{... | collective-permute-start | bytes 1520 | tf_op jit(solution)/shard_map/ppermute | solution.py:27
  5.2 1.9 %collective-permute-start = (bf16[24,16,128]{2,1,0:T(8,128)(2,1)}, bf16[24,16,128]{2,1,0:T(8,128)(2,1)S(1)}, u32[]{:S(2)}, u32[]{:S(2)}) collective-permute-start(bf16[24,16,128]{2,1,0:T(8,128)(2,1)} %param.5), channel_id=1, source_target_pairs={{0,2},{1,3},{2,0},{3,1},{4,6},{5,7},{6,4},{7,5},{8,10},{9,11},{10,... | collective-permute-start | bytes 294920 | tf_op jit(solution)/shard_map/ppermute | solution.py:27
  7.2 0.9 %constant_dynamic-update-slice_fusion.8 = bf16[193,16,128]{2,1,0:T(8,128)(2,1)S(1)} fusion(bf16[24,16,128]{2,1,0:T(8,128)(2,1)} %param.5), kind=kLoop, calls=%fused_computation.10 | loop fusion | bytes 196608
  8.2 2.6 %collective-permute-start.3 = (bf16[24,16,128]{2,1,0:T(8,128)(2,1)}, bf16[24,16,128]{2,1,0:T(8,128)(2,1)S(1)}, u32[]{:S(2)}, u32[]{:S(2)}) collective-permute-start(bf16[24,16,128]{2,1,0:T(8,128)(2,1)} %param.5), channel_id=1, source_target_pairs={{0,16},{4,20},{8,24},{12,28},{16,0},{20,4},{24,8},{28,12},{1,17},{... | collective-permute-start | bytes 294920 | tf_op jit(solution)/shard_map/ppermute | solution.py:27
  10.9 5.4 %collective-permute-done.3 = bf16[24,16,128]{2,1,0:T(8,128)(2,1)S(1)} collective-permute-done((bf16[24,16,128]{2,1,0:T(8,128)(2,1)}, bf16[24,16,128]{2,1,0:T(8,128)(2,1)S(1)}, u32[]{:S(2)}, u32[]{:S(2)}) %collective-permute-start.3) | collective-permute-done | bytes 98336 | tf_op jit(solution)/shard_map/ppermute | solution.py:27
  16.4 0.5 collective-permute-start.4
  17.1 4.5 %collective-permute-done.4 = bf16[24,16,128]{2,1,0:T(8,128)(2,1)S(1)} collective-permute-done((bf16[24,16,128]{2,1,0:T(8,128)(2,1)S(1)}, bf16[24,16,128]{2,1,0:T(8,128)(2,1)S(1)}, u32[]{:S(2)}, u32[]{:S(2)}) %collective-permute-start.4) | collective-permute-done | bytes 98336 | tf_op jit(solution)/shard_map/ppermute | solution.py:27
  21.7 1.2 %collective-permute-done.6 = bf16[24,16,128]{2,1,0:T(8,128)(2,1)S(1)} collective-permute-done((bf16[24,16,128]{2,1,0:T(8,128)(2,1)S(1)}, bf16[24,16,128]{2,1,0:T(8,128)(2,1)S(1)}, u32[]{:S(2)}, u32[]{:S(2)}) %collective-permute-start.6) | collective-permute-done | bytes 98336 | tf_op jit(solution)/shard_map/ppermute | solution.py:27
  22.9 1.7 %pick.1 = (bf16[36,16,128]{2,1,0:T(8,128)(2,1)}, bf16[36,16,128]{2,1,0:T(8,128)(2,1)}, bf16[36,16,128]{2,1,0:T(8,128)(2,1)}) custom-call(s32[2]{0:T(128)S(1)} %pad_add_fusion.1.here, s32[3,7]{1,0:T(4,128)S(1)} %slice.3.owner_ref, s32[3,126]{1,0:T(4,128)S(1)} %get-tuple-element.40.place_ref, bf16[193,16,128]{2,1,0:T(8,128)(2,1)S(1)} %constant_dynamic-update-slice_fusion.table_ref), custom_call_target="tpu_custom_call" | custom-call | tf_op jit(solution)/shard_map/pick/pallas_call | solution.py:380
  24.6 1.5 %collective-permute-start.10 = (bf16[36,16,128]{2,1,0:T(8,128)(2,1)}, bf16[36,16,128]{2,1,0:T(8,128)(2,1)S(1)}, u32[]{:S(2)}, u32[]{:S(2)}) collective-permute-start(bf16[36,16,128]{2,1,0:T(8,128)(2,1)} %get-tuple-element.33), channel_id=1, source_target_pairs={{0,4},{4,0},{8,12},{12,8},{16,20},{20,16},{24,28},{28,24},{1,5},{5... | collective-permute-start | bytes 442376 | tf_op jit(solution)/shard_map/ppermute | solution.py:27
  26.1 0.8 %collective-permute-start.11 = (bf16[36,16,128]{2,1,0:T(8,128)(2,1)}, bf16[36,16,128]{2,1,0:T(8,128)(2,1)S(1)}, u32[]{:S(2)}, u32[]{:S(2)}) collective-permute-start(bf16[36,16,128]{2,1,0:T(8,128)(2,1)} %get-tuple-element.34), channel_id=1, source_target_pairs={{0,8},{4,12},{8,0},{12,4},{16,24},{20,28},{24,16},{28,20},{1,9},{5... | collective-permute-start | bytes 442376 | tf_op jit(solution)/shard_map/ppermute | solution.py:27
  26.9 1.2 %collective-permute-start.12 = (bf16[36,16,128]{2,1,0:T(8,128)(2,1)}, bf16[36,16,128]{2,1,0:T(8,128)(2,1)}, u32[]{:S(2)}, u32[]{:S(2)}) collective-permute-start(bf16[36,16,128]{2,1,0:T(8,128)(2,1)} %get-tuple-element.35), channel_id=1, source_target_pairs={{0,12},{4,8},{8,4},{12,0},{16,28},{20,24},{24,20},{28,16},{1,13},{... | collective-permute-start | bytes 442376 | tf_op jit(solution)/shard_map/ppermute | solution.py:27
  28.3 1.1 %prep.1 = (s32[288]{0:T(512)S(1)}, s32[1,288]{1,0:T(1,128)S(1)}, s32[288]{0:T(512)S(1)}, s32[288]{0:T(512)S(1)}, s32[288]{0:T(512)S(1)}, /*index=5*/s32[288]{0:T...) custom-call(s32[2]{0:T(128)S(1)} %pad_add_fusion.1.here, s32[1,288]{1,0:T(1,128)S(1)} %reshape.16.cols_ref, ...), custom_call_target="tpu_custom_call" | custom-call | tf_op jit(solution)/shard_map/prep/pallas_call | solution.py:394
  29.4 7.1 %own.1 = (bf16[288,16,128]{2,1,0:T(8,128)(2,1)S(1)}, f32[24,1,128]{2,1,0:T(1,128)S(1)}, bf16[288,16,128]{2,1,0:T(8,128)(2,1)S(1)}, f32[24,256]{1,0:T(8,128)S(1)}, bf16[288,128,128]{2,1,0:T(8,128)(2,1)S(1)}) custom-call(s32[288]{0:T(512)S(1)} %get-tuple-element.27.place, s32[288]{0:T(512)S(1)} %get-tuple-element.28.far_slot, ...), custom_call_target="tpu_custom_call" | custom-call | tf_op jit(solution)/shard_map/own/pallas_call | solution.py:414
  36.5 5.7 %ghost.1 = (bf16[288,16,128]{2,1,0:T(8,128)(2,1)S(1)}, bf16[8,2,24,256]{3,2,1,0:T(8,128)(2,1)}) custom-call(s32[2]{0:T(128)S(1)} %pad_add_fusion.1.here, s32[288]{0:T(512)S(1)} %get-tuple-element.21.slots, s32[288]{0:T(512)S(1)} %get-tuple-element.22.entries, s32[288]{0:T(512)S(1)} %get-tuple-element.23.tiles, ...), custom_call_target="tpu_custom_call", output_to_operand_aliasing={{0}: (10, {})} | custom-call | tf_op jit(solution)/shard_map/ghost/pallas_call | solution.py:433
  42.2 5.8 %all-to-all-start = ((bf16[16,24,256]{2,1,0:T(8,128)(2,1)}), bf16[16,24,256]{2,1,0:T(8,128)(2,1)S(1)}, u32[]{:S(2)}, u32[]{:S(2)}) async-start(bf16[16,24,256]{2,1,0:T(8,128)(2,1)} %bitcast.4), calls=%async_computation | async-start | bytes 393216 | tf_op jit(solution)/shard_map/all_to_all | solution.py:460
  48.0 3.4 %terms.1 = bf16[96,256]{1,0:T(8,128)(2,1)S(1)} custom-call(s32[1,288]{1,0:T(1,128)S(1)} %get-tuple-element.37.row_ref, bf16[288,16,128]{2,1,0:T(8,128)(2,1)S(1)} %get-tuple-element.36.prolong_ref, bf16[288,16,128]{2,1,0:T(8,128)(2,1)S(1)} %get-tuple-element.38.product_ref), custom_call_target="tpu_custom_call" | custom-call | tf_op jit(solution)/shard_map/terms/pallas_call | solution.py:465
  51.5 2.0 %collective-permute-start.13 = (bf16[96,256]{1,0:T(8,128)(2,1)S(1)}, bf16[96,256]{1,0:T(8,128)(2,1)S(1)}, u32[]{:S(2)}, u32[]{:S(2)}) collective-permute-start(bf16[96,256]{1,0:T(8,128)(2,1)S(1)} %terms.1), channel_id=1, source_target_pairs={{0,2},{1,3},{2,0},{3,1},{4,6},{5,7},{6,4},{7,5},{8,10},{9,11},{10,... | collective-permute-start | bytes 147464 | tf_op jit(solution)/shard_map/ppermute | solution.py:27
  53.4 2.4 %collective-permute-done.13 = bf16[96,256]{1,0:T(8,128)(2,1)S(1)} collective-permute-done((bf16[96,256]{1,0:T(8,128)(2,1)S(1)}, bf16[96,256]{1,0:T(8,128)(2,1)S(1)}, u32[]{:S(2)}, u32[]{:S(2)}) %collective-permute-start.13) | collective-permute-done | bytes 49184 | tf_op jit(solution)/shard_map/ppermute | solution.py:27
  56.1 0.3 target.1
  56.4 0.5 collective-permute-start.15
  56.9 1.0 %copy.18 = bf16[24,12,16,128]{3,2,1,0:T(8,128)(2,1)} copy(bf16[24,12,16,128]{3,2,1,0:T(8,128)(2,1)S(1)} %bitcast.5) | data formatting | bytes 2359296
  57.9 0.7 %add_add_fusion = f32[96,256]{1,0:T(8,128)} fusion(bf16[96,256]{1,0:T(8,128)(2,1)S(1)} %collective-permute-done.15, bf16[96,256]{1,0:T(8,128)(2,1)S(1)} %target.1, bf16[96,256]{1,0:T(8,128)(2,1)S(1)} %collective-permute-done.14, bf16[96,256]{1,0:T(8,128)(2,1)S(1)} %add_convert_fusion), kind=kLoop, calls=%fused_computation | loop fusion | flops 172032 | bytes 294912 | tf_op jit(solution)/shard_map/add | solution.py:490
  (37 shorter events, 1.0 us)
Async XLA Ops:
  0.6 7.6 %collective-permute-start.7 = (s32[1,126]{1,0:T(1,128)}, s32[1,126]{1,0:T(1,128)S(1)}, u32[]{:S(2)}, u32[]{:S(2)}) collective-permute-start(s32[1,126]{1,0:T(1,128)} %fetch_ref.1), channel_id=1, source_target_pairs={{0,4},{4,0},{8,12},{12,8},{16,20},{20,16},{24,28},{28,24},{1,5},{5... | collective-permute-start | bytes 1520 | tf_op jit(solution)/shard_map/ppermute | solution.py:27
  3.7 7.1 %collective-permute-start.9 = (s32[1,126]{1,0:T(1,128)}, s32[1,126]{1,0:T(1,128)S(1)}, u32[]{:S(2)}, u32[]{:S(2)}) collective-permute-start(s32[1,126]{1,0:T(1,128)} %fetch_ref.1), channel_id=1, source_target_pairs={{0,12},{4,8},{8,4},{12,0},{16,28},{20,24},{24,20},{28,16},{1,13},{... | collective-permute-start | bytes 1520 | tf_op jit(solution)/shard_map/ppermute | solution.py:27
  5.2 5.6 %collective-permute-start.8 = (s32[1,126]{1,0:T(1,128)}, s32[1,126]{1,0:T(1,128)S(1)}, u32[]{:S(2)}, u32[]{:S(2)}) collective-permute-start(s32[1,126]{1,0:T(1,128)} %fetch_ref.1), channel_id=1, source_target_pairs={{0,8},{4,12},{8,0},{12,4},{16,24},{20,28},{24,16},{28,20},{1,9},{5... | collective-permute-start | bytes 1520 | tf_op jit(solution)/shard_map/ppermute | solution.py:27
  5.2 11.8 %collective-permute-start.1 = (bf16[24,16,128]{2,1,0:T(8,128)(2,1)}, bf16[24,16,128]{2,1,0:T(8,128)(2,1)S(1)}, u32[]{:S(2)}, u32[]{:S(2)}) collective-permute-start(bf16[24,16,128]{2,1,0:T(8,128)(2,1)} %param.5), channel_id=1, source_target_pairs={{0,1},{1,0},{2,3},{3,2},{4,5},{5,4},{6,7},{7,6},{8,9},{9,8},{10,11... | collective-permute-start | bytes 294920 | tf_op jit(solution)/shard_map/ppermute | solution.py:27
  5.2 11.6 %collective-permute-start = (bf16[24,16,128]{2,1,0:T(8,128)(2,1)}, bf16[24,16,128]{2,1,0:T(8,128)(2,1)S(1)}, u32[]{:S(2)}, u32[]{:S(2)}) collective-permute-start(bf16[24,16,128]{2,1,0:T(8,128)(2,1)} %param.5), channel_id=1, source_target_pairs={{0,2},{1,3},{2,0},{3,1},{4,6},{5,7},{6,4},{7,5},{8,10},{9,11},{10,... | collective-permute-start | bytes 294920 | tf_op jit(solution)/shard_map/ppermute | solution.py:27
  7.2 20.9 %copy-start.1 = (s32[24,12]{0,1:T(8,128)S(1)}, s32[24,12]{0,1:T(8,128)}, u32[]{:S(2)}) copy-start(s32[24,12]{0,1:T(8,128)} %param.6) | copy-start | bytes 3460
  7.2 21.1 %copy-start = (s32[1,126]{1,0:T(1,128)S(1)}, s32[1,126]{1,0:T(1,128)}, u32[]{:S(2)}) copy-start(s32[1,126]{1,0:T(1,128)} %fetch_ref.1) | copy-start | bytes 1516
  8.2 8.2 %collective-permute-start.3 = (bf16[24,16,128]{2,1,0:T(8,128)(2,1)}, bf16[24,16,128]{2,1,0:T(8,128)(2,1)S(1)}, u32[]{:S(2)}, u32[]{:S(2)}) collective-permute-start(bf16[24,16,128]{2,1,0:T(8,128)(2,1)} %param.5), channel_id=1, source_target_pairs={{0,16},{4,20},{8,24},{12,28},{16,0},{20,4},{24,8},{28,12},{1,17},{... | collective-permute-start | bytes 294920 | tf_op jit(solution)/shard_map/ppermute | solution.py:27
  16.4 5.3 %collective-permute-start.5 = (bf16[24,16,128]{2,1,0:T(8,128)(2,1)S(1)}, bf16[24,16,128]{2,1,0:T(8,128)(2,1)S(1)}, u32[]{:S(2)}, u32[]{:S(2)}) collective-permute-start(bf16[24,16,128]{2,1,0:T(8,128)(2,1)S(1)} %collective-permute-done.3), channel_id=1, source_target_pairs={{0,1},{1,0},{2,3},{3,2},{4,5},{5,4},{6,7},{7,6},{8,9},{9,8},{10,11... | collective-permute-start | bytes 294920 | tf_op jit(solution)/shard_map/ppermute | solution.py:27
  16.4 5.2 %collective-permute-start.4 = (bf16[24,16,128]{2,1,0:T(8,128)(2,1)S(1)}, bf16[24,16,128]{2,1,0:T(8,128)(2,1)S(1)}, u32[]{:S(2)}, u32[]{:S(2)}) collective-permute-start(bf16[24,16,128]{2,1,0:T(8,128)(2,1)S(1)} %collective-permute-done.3), channel_id=1, source_target_pairs={{0,2},{1,3},{2,0},{3,1},{4,6},{5,7},{6,4},{7,5},{8,10},{9,11},{10,... | collective-permute-start | bytes 294920 | tf_op jit(solution)/shard_map/ppermute | solution.py:27
  16.8 4.8 %collective-permute-start.2 = (bf16[24,16,128]{2,1,0:T(8,128)(2,1)S(1)}, bf16[24,16,128]{2,1,0:T(8,128)(2,1)S(1)}, u32[]{:S(2)}, u32[]{:S(2)}) collective-permute-start(bf16[24,16,128]{2,1,0:T(8,128)(2,1)S(1)} %collective-permute-done), channel_id=1, source_target_pairs={{0,1},{1,0},{2,3},{3,2},{4,5},{5,4},{6,7},{7,6},{8,9},{9,8},{10,11... | collective-permute-start | bytes 294920 | tf_op jit(solution)/shard_map/ppermute | solution.py:27
  21.6 1.3 %collective-permute-start.6 = (bf16[24,16,128]{2,1,0:T(8,128)(2,1)S(1)}, bf16[24,16,128]{2,1,0:T(8,128)(2,1)S(1)}, u32[]{:S(2)}, u32[]{:S(2)}) collective-permute-start(bf16[24,16,128]{2,1,0:T(8,128)(2,1)S(1)} %collective-permute-done.4), channel_id=1, source_target_pairs={{0,1},{1,0},{2,3},{3,2},{4,5},{5,4},{6,7},{7,6},{8,9},{9,8},{10,11... | collective-permute-start | bytes 294920 | tf_op jit(solution)/shard_map/ppermute | solution.py:27
  24.6 11.9 %collective-permute-start.10 = (bf16[36,16,128]{2,1,0:T(8,128)(2,1)}, bf16[36,16,128]{2,1,0:T(8,128)(2,1)S(1)}, u32[]{:S(2)}, u32[]{:S(2)}) collective-permute-start(bf16[36,16,128]{2,1,0:T(8,128)(2,1)} %get-tuple-element.33), channel_id=1, source_target_pairs={{0,4},{4,0},{8,12},{12,8},{16,20},{20,16},{24,28},{28,24},{1,5},{5... | collective-permute-start | bytes 442376 | tf_op jit(solution)/shard_map/ppermute | solution.py:27
  26.1 10.4 %collective-permute-start.11 = (bf16[36,16,128]{2,1,0:T(8,128)(2,1)}, bf16[36,16,128]{2,1,0:T(8,128)(2,1)S(1)}, u32[]{:S(2)}, u32[]{:S(2)}) collective-permute-start(bf16[36,16,128]{2,1,0:T(8,128)(2,1)} %get-tuple-element.34), channel_id=1, source_target_pairs={{0,8},{4,12},{8,0},{12,4},{16,24},{20,28},{24,16},{28,20},{1,9},{5... | collective-permute-start | bytes 442376 | tf_op jit(solution)/shard_map/ppermute | solution.py:27
  26.9 9.6 %collective-permute-start.12 = (bf16[36,16,128]{2,1,0:T(8,128)(2,1)}, bf16[36,16,128]{2,1,0:T(8,128)(2,1)}, u32[]{:S(2)}, u32[]{:S(2)}) collective-permute-start(bf16[36,16,128]{2,1,0:T(8,128)(2,1)} %get-tuple-element.35), channel_id=1, source_target_pairs={{0,12},{4,8},{8,4},{12,0},{16,28},{20,24},{24,20},{28,16},{1,13},{... | collective-permute-start | bytes 442376 | tf_op jit(solution)/shard_map/ppermute | solution.py:27
  42.2 13.9 %all-to-all-start = ((bf16[16,24,256]{2,1,0:T(8,128)(2,1)}), bf16[16,24,256]{2,1,0:T(8,128)(2,1)S(1)}, u32[]{:S(2)}, u32[]{:S(2)}) async-start(bf16[16,24,256]{2,1,0:T(8,128)(2,1)} %bitcast.4), calls=%async_computation | async-start | bytes 393216 | tf_op jit(solution)/shard_map/all_to_all | solution.py:460
  51.5 4.4 %collective-permute-start.13 = (bf16[96,256]{1,0:T(8,128)(2,1)S(1)}, bf16[96,256]{1,0:T(8,128)(2,1)S(1)}, u32[]{:S(2)}, u32[]{:S(2)}) collective-permute-start(bf16[96,256]{1,0:T(8,128)(2,1)S(1)} %terms.1), channel_id=1, source_target_pairs={{0,2},{1,3},{2,0},{3,1},{4,6},{5,7},{6,4},{7,5},{8,10},{9,11},{10,... | collective-permute-start | bytes 147464 | tf_op jit(solution)/shard_map/ppermute | solution.py:27
  55.9 2.0 %collective-permute-start.14 = (bf16[96,256]{1,0:T(8,128)(2,1)S(1)}, bf16[96,256]{1,0:T(8,128)(2,1)S(1)}, u32[]{:S(2)}, u32[]{:S(2)}) collective-permute-start(bf16[96,256]{1,0:T(8,128)(2,1)S(1)} %add_convert_fusion), channel_id=1, source_target_pairs={{0,1},{1,0},{2,3},{3,2},{4,5},{5,4},{6,7},{7,6},{8,9},{9,8},{10,11... | collective-permute-start | bytes 147464 | tf_op jit(solution)/shard_map/ppermute | solution.py:27
  56.4 1.5 %collective-permute-start.15 = (bf16[96,256]{1,0:T(8,128)(2,1)S(1)}, bf16[96,256]{1,0:T(8,128)(2,1)S(1)}, u32[]{:S(2)}, u32[]{:S(2)}) collective-permute-start(bf16[96,256]{1,0:T(8,128)(2,1)S(1)} %target.1), channel_id=1, source_target_pairs={{0,1},{1,0},{2,3},{3,2},{4,5},{5,4},{6,7},{7,6},{8,9},{9,8},{10,11... | collective-permute-start | bytes 147464 | tf_op jit(solution)/shard_map/ppermute | solution.py:27

commit v6 on v5

--- a/solution.py
+++ b/solution.py
@@ -57,7 +57,7 @@
 
 def prep_kernel(
     slots, tile_dev, per_peer, rows, half, bits, here,
-    cols_ref, fetch_ref, place_ref, row_ref, far_slot_ref, slot_ref, entry_ref, tile_ref, counts_ref,
+    cols_ref, fetch_ref, place_ref, row_ref, far_slot_ref, slot_ref, own_slot_ref, entry_ref, tile_ref, counts_ref,
     target_ref, index_ref,
 ):
     me, lane = here[0], here[1]
@@ -90,10 +90,9 @@
         table_place(cols, lane, tile_dev, bits),
         jnp.where(source == 0, group_size + entry_int, 2 * group_size),
     )[0]
-    row_ref[...] = jnp.where(source < 0, cols, -1)
 
     kind = lax.broadcasted_iota(jnp.int32, (8, total), 0)
-    chosen = jnp.where(source > 0, 1, source)
+    chosen = jnp.where(source > 0, 1, jnp.where(source == 0, 0, 2))
     by_kind = jnp.where(kind == chosen, 1.0, 0.0)
     before = lax.broadcasted_iota(jnp.int32, (total, total), 0) < lax.broadcasted_iota(
         jnp.int32, (total, total), 1
@@ -109,23 +108,27 @@
     carried = jnp.concatenate(
         [
             tile.astype(jnp.float32), (slot - tile * slots).astype(jnp.float32), entry, owner,
-            member, low,
+            member, low, cols.astype(jnp.float32),
         ],
         axis=0,
     ).astype(jnp.bfloat16)
     at = lax.broadcasted_iota(jnp.int32, (total, total), 0)
-    for which in range(2):
+    for which in range(3):
         count = counts[which : which + 1]
         wanted = jnp.where(at < count, at, 0)
         chosen = jnp.where(wanted == rank[which : which + 1], 1.0, 0.0).astype(jnp.bfloat16)
         listed = lax.dot_general(carried, chosen, NT, preferred_element_type=jnp.float32)
         listed = listed.astype(jnp.int32)
-        (far_slot_ref, slot_ref)[which][...] = (listed[0:1] * slots + listed[1:2])[0]
-        if which:
+        (far_slot_ref, slot_ref, own_slot_ref)[which][...] = (listed[0:1] * slots + listed[1:2])[0]
+        if which == 1:
             entry_ref[...] = (listed[2:3] + (listed[5:6] - 1) * (2 * per_peer))[0]
             tile_ref[...] = listed[0]
-        row = listed[4:5] if which == 0 else listed[3:4] * rows + listed[4:5]
-        target_ref[which : which + 1, :] = jnp.where(slot < count, row, -1)
+        row = (listed[4:5], listed[3:4] * rows + listed[4:5], listed[6:7])[which]
+        row = jnp.where(slot < count, row, -1)
+        if which == 2:
+            row_ref[...] = row
+        else:
+            target_ref[which : which + 1, :] = row
 
     index_ref[...] = jnp.full(index_ref.shape, -1.0, jnp.float32)
     groups = fetch_ref.shape[1] // per_peer
@@ -135,6 +138,7 @@
             jnp.where(ghost_lane == p * per_peer, divided(fetched, group_size), 0)
         )
         index_ref[group, :, 0:per_peer] = part
+        index_ref[group, :, per_peer : 2 * per_peer] = part
 
 
 def terms_of(parts, spread, lane_block):
@@ -204,8 +208,8 @@
 
 
 def own_kernel(
-    slots, place, far_slot, counts_ref, target_ref, table_ref, a_hbm,
-    prolong_ref, weight_ref, product_ref, far_ref, a_ref, terms_ref, arrived,
+    slots, pitch, half, place, far_slot, counts_ref, here, target_ref, index_ref, table_ref, a_hbm,
+    prolong_ref, weight_ref, product_ref, first_ref, second_ref, extra_ref, rest_ref, a_ref, terms_ref, arrived,
 ):
     tile_dev = weight_ref.shape[0]
     mode_count, tile_rows = table_ref.shape[1:]
@@ -224,6 +228,29 @@
     @pl.loop(0, steps)
     def _(step):
         fetch(step).start()
+
+    total = tile_dev * slots
+    terms_ref[...] = jnp.zeros_like(terms_ref)
+    rest_ref[...] = jnp.zeros_like(rest_ref)
+    groups = index_ref.shape[0]
+    height, extra = extra_ref.shape
+    rows = height // groups
+    far_rows = -(-pitch // 8) * 8
+    place_row = lax.broadcasted_iota(jnp.int32, (height, total), 0)
+    goal = target_ref[1:2, :]
+    first_ref[...] = jnp.where(place_row == goal, 1.0, 0.0).astype(jnp.bfloat16)
+    goal = jnp.where(goal >= 0, goal + pitch, -1)
+    second_ref[...] = jnp.where(place_row == goal, 1.0, 0.0).astype(jnp.bfloat16)
+    row = lax.broadcasted_iota(jnp.int32, (height, extra), 0)
+    lane = lax.broadcasted_iota(jnp.int32, (height, extra), 1)
+    far_row = (here[0] ^ half) * rows
+    chosen = (lane < groups) & (row == lane * rows + 2 * pitch)
+    for part in range(2):
+        at = lane - groups - part * far_rows
+        chosen = chosen | ((at >= 0) & (at < pitch) & (row == far_row + part * pitch + at))
+    extra_ref[...] = jnp.where(chosen, 1.0, 0.0).astype(jnp.bfloat16)
+    for group in range(groups):
+        rest_ref[group : group + 1, :] = index_ref[group][:, 0:LANES] * tile_rows
 
     @pl.loop(0, steps)
     def _(step):
@@ -246,7 +273,6 @@
                     product_ref[slot + d] = product.astype(jnp.bfloat16)
 
     spread, lane_block = term_constants(batch, mode_count)
-    terms_ref[...] = jnp.zeros_like(terms_ref)
 
     @pl.loop(0, (counts_ref[0, 0] + batch - 1) // batch)
     def _(step):
@@ -255,27 +281,30 @@
         row = pl.multiple_of(step * batch, batch)
         terms_ref[pl.ds(row, batch), :] = terms_of(parts, spread, lane_block)
 
-    total = tile_dev * slots
-    far_ref[...] = summed(far_ref.shape[0], target_ref[0:1, :], terms_ref[0:total, :], tile_rows)
-
-
-def terms_kernel(row_ref, prolong_ref, product_ref, sums_ref, terms_ref):
+    sums = summed(far_rows, target_ref[0:1, :], terms_ref[0:total, :], 1)
+    rest_ref[groups : groups + far_rows, :] = sums[:, :LANES]
+    rest_ref[groups + far_rows : groups + 2 * far_rows, :] = sums[:, LANES:]
+
+
+def terms_kernel(slots, counts_ref, row_ref, prolong_ref, product_ref, sums_ref, terms_ref):
     total, mode_count, tile_rows = prolong_ref.shape
-    per_step = 6 * BATCH
-    spread, lane_block = term_constants(per_step, mode_count)
-
-    @pl.loop(0, total // per_step)
+    batch = 6 * BATCH
+    spread, lane_block = term_constants(batch, mode_count)
+    terms_ref[...] = jnp.zeros_like(terms_ref)
+
+    @pl.loop(0, (counts_ref[2, 0] + batch - 1) // batch)
     def _(step):
-        first = step * per_step
-        parts = [(prolong_ref[first + k], product_ref[first + k]) for k in range(per_step)]
-        terms_ref[pl.ds(pl.multiple_of(first, BATCH), per_step), :] = terms_of(parts, spread, lane_block)
-
-    sums = summed(sums_ref.shape[0], row_ref[...], terms_ref[...], tile_rows)
+        first = step * batch
+        slot = [slots[jnp.minimum(first + i, total - 1)] for i in range(batch)]
+        parts = [(prolong_ref[f], product_ref[f]) for f in slot]
+        terms_ref[pl.ds(pl.multiple_of(first, BATCH), batch), :] = terms_of(parts, spread, lane_block)
+
+    sums = summed(sums_ref.shape[0], row_ref[...], terms_ref[0:total, :], tile_rows)
     sums_ref[...] = sums.astype(jnp.bfloat16)
 
 
 def ghost_kernel(
-    pitch, half, here, slots, entries, tiles, counts_ref, target_ref, index_ref, far_ref, a_ref, weight_ref,
+    half, slots, entries, tiles, counts_ref, first_ref, second_ref, extra_ref, rest_ref, a_ref, weight_ref,
     old_ref, *refs,
 ):
     received = refs[: half - 1]
@@ -318,12 +347,13 @@
         begin(step)
 
     finish(steps - 1)
-    result = summed(groups * rows, target_ref[1:2, :], terms_ref[0:total, :], tile_rows)
-    result = result.reshape(groups, rows, width)
-    row_place = lax.broadcasted_iota(jnp.int32, (groups, rows, width), 1)
-    group_place = lax.broadcasted_iota(jnp.int32, (groups, rows, width), 0)
-    result = jnp.where(group_place == (here[0] ^ half), far_ref[...][None], result)
-    result = jnp.where(row_place == pitch, index_ref[...], result).astype(jnp.bfloat16)
+    terms = terms_ref[0:total, :].astype(jnp.bfloat16)
+    result = jnp.dot(first_ref[...], terms[:, :LANES], preferred_element_type=jnp.float32)
+    result = result + jnp.dot(second_ref[...], terms[:, LANES:], preferred_element_type=jnp.float32)
+    result = result + jnp.dot(
+        extra_ref[...], rest_ref[...].astype(jnp.bfloat16), preferred_element_type=jnp.float32
+    )
+    result = (result * (1.0 / tile_rows)).reshape(groups, rows, width).astype(jnp.bfloat16)
     for copy in range(copies):
         out_ref[:, copy] = result
 
@@ -332,13 +362,18 @@
     senders, rows, width = incoming_ref.shape
     group_size = out_ref.shape[0]
     tile = lax.broadcasted_iota(jnp.int32, (group_size, rows), 0)
-    total = jnp.zeros((group_size, width), jnp.float32)
+    lane = lax.broadcasted_iota(jnp.int32, (group_size, rows), 1)
+    totals = [jnp.zeros((group_size, width), jnp.float32) for _ in range(2)]
     for sender in range(senders):
         value = incoming_ref[sender]
-        wanted = value[pitch : pitch + 1, :rows].astype(jnp.float32).astype(jnp.int32)
-        one_hot = (tile == wanted).astype(jnp.bfloat16)
-        total = total + jnp.dot(one_hot, value, preferred_element_type=jnp.float32)
-    out_ref[...] = total.astype(jnp.bfloat16)
+        wanted = value[2 * pitch : 2 * pitch + 1, :rows].astype(jnp.float32).astype(jnp.int32)
+        match = tile == wanted
+        for part in range(2):
+            here = match & (lane >= part * pitch) & (lane < (part + 1) * pitch)
+            one_hot = jnp.where(here, 1.0, 0.0).astype(jnp.bfloat16)
+            totals[part] = totals[part] + jnp.dot(one_hot, value, preferred_element_type=jnp.float32)
+    for part, total in enumerate(totals):
+        out_ref[:, part * width : (part + 1) * width] = total.astype(jnp.bfloat16)
 
 
 def shards(a_tiles, modes, col_tiles, fetch_list):
@@ -389,54 +424,57 @@
     for peer in range(1, half):
         received.append(xor_permute(picks[peer - 1], "sub", peer))
 
-    rows = -(-(per_peer + 1) // 8) * 8
+    rows = -(-(2 * per_peer + 1) // 8) * 8
     columns = col_tiles.reshape(1, slot_total)
-    place, own_row, far_slot, slot, entry, tile, counts, target, index_rows = pl.pallas_call(
+    place, own_row, far_slot, slot, own_slot, entry, tile, counts, target, index_rows = pl.pallas_call(
         functools.partial(prep_kernel, slot_count, tile_dev, per_peer, rows, half, tuple(bits)),
         out_shape=[
             jax.ShapeDtypeStruct((slot_total,), jnp.int32),
             jax.ShapeDtypeStruct((1, slot_total), jnp.int32),
-            *[jax.ShapeDtypeStruct((slot_total,), jnp.int32)] * 4,
+            *[jax.ShapeDtypeStruct((slot_total,), jnp.int32)] * 5,
             jax.ShapeDtypeStruct((8, LANES), jnp.int32),
             jax.ShapeDtypeStruct((2, slot_total), jnp.int32),
             jax.ShapeDtypeStruct((sub_count, 1, width), jnp.float32),
         ],
         in_specs=[SMEM, VMEM, VMEM],
-        out_specs=[VMEM] * 9,
+        out_specs=[VMEM] * 10,
         name="prep",
         compiler_params=PARAMS,
     )(here, columns, fetch_list)
 
     tiles = a_tiles.reshape(slot_total, tile_rows, tile_rows)
     tiles = pltpu.with_memory_space_constraint(tiles, pltpu.HBM)
+    extra = -(-(sub_count + 2 * (-(-per_peer // 8) * 8)) // 32) * 32
     terms_scratch = pltpu.VMEM((slot_total + 2 * BATCH, width), jnp.float32)
     vectors = (slot_total, mode_count, tile_rows)
-    prolong, weight, product, far_sums, tiles = pl.pallas_call(
-        functools.partial(own_kernel, slot_count),
+    prolong, weight, product, first, second, added, rest, tiles = pl.pallas_call(
+        functools.partial(own_kernel, slot_count, per_peer, half),
         out_shape=[
             pltpu.VMEM(vectors, jnp.bfloat16),
             jax.ShapeDtypeStruct((tile_dev, 1, tile_rows), jnp.float32),
             pltpu.VMEM(vectors, jnp.bfloat16),
-            jax.ShapeDtypeStruct((rows, width), jnp.float32),
+            *[jax.ShapeDtypeStruct((sub_count * rows, slot_total), jnp.bfloat16)] * 2,
+            jax.ShapeDtypeStruct((sub_count * rows, extra), jnp.bfloat16),
+            jax.ShapeDtypeStruct((extra, LANES), jnp.float32),
             pltpu.VMEM((slot_total, tile_rows, tile_rows), jnp.bfloat16),
         ],
-        in_specs=[SMEM, SMEM, SMEM, VMEM, VMEM, pl.BlockSpec(memory_space=pltpu.HBM)],
-        out_specs=[VMEM] * 5,
+        in_specs=[SMEM] * 4 + [VMEM] * 3 + [pl.BlockSpec(memory_space=pltpu.HBM)],
+        out_specs=[VMEM] * 8,
         scratch_shapes=[terms_scratch, pltpu.SemaphoreType.DMA((tile_dev // 4,))],
         name="own",
         compiler_params=PARAMS,
-    )(place, far_slot, counts, target, table, tiles)
+    )(place, far_slot, counts, here, target, index_rows, table, tiles)
 
     prolong = pltpu.with_memory_space_constraint(prolong, pltpu.VMEM)
     product = pltpu.with_memory_space_constraint(product, pltpu.VMEM)
     tiles = pltpu.with_memory_space_constraint(tiles, pltpu.VMEM)
     prolong, outgoing = pl.pallas_call(
-        functools.partial(ghost_kernel, per_peer, half),
+        functools.partial(ghost_kernel, half),
         out_shape=[
             pltpu.VMEM(vectors, jnp.bfloat16),
-            jax.ShapeDtypeStruct((sub_count, blk_half, rows, width), jnp.bfloat16),
+            jax.ShapeDtypeStruct((sub_count, blk_half, rows, LANES), jnp.bfloat16),
         ],
-        in_specs=[SMEM] * 5 + [VMEM] * (6 + half - 1),
+        in_specs=[SMEM] * 4 + [VMEM] * (7 + half - 1),
         out_specs=[VMEM, VMEM],
         input_output_aliases={10: 0},
         scratch_shapes=[
@@ -448,8 +486,7 @@
         name="ghost",
         compiler_params=GHOST_PARAMS,
     )(
-        here, slot, entry, tile, counts,
-        target, index_rows, far_sums, tiles, weight, prolong, *received,
+        slot, entry, tile, counts, first, second, added, rest, tiles, weight, prolong, *received,
     )
     finished = pltpu.with_memory_space_constraint(prolong, pltpu.VMEM)
 
@@ -458,19 +495,19 @@
         for core in range(2)
     ]
     incoming = lax.all_to_all(
-        outgoing.reshape(sub_count * blk_half, rows, width),
+        outgoing.reshape(sub_count * blk_half, rows, LANES),
         ("sub", "blk"), split_axis=0, concat_axis=0, axis_index_groups=groups, tiled=True,
     )
 
     own_total = pl.pallas_call(
         terms_kernel,
         out_shape=jax.ShapeDtypeStruct((group_size, width), jnp.bfloat16),
-        in_specs=[VMEM] * 3,
+        in_specs=[SMEM] * 2 + [VMEM] * 3,
         out_specs=VMEM,
-        scratch_shapes=[pltpu.VMEM((slot_total, width), jnp.float32)],
+        scratch_shapes=[pltpu.VMEM((slot_total + 6 * BATCH, width), jnp.float32)],
         name="terms",
         compiler_params=PARAMS,
-    )(own_row, finished, product)
+    )(own_slot, counts, own_row, finished, product)
     bit = blk_half
     while bit:
         other = xor_permute(own_total, "blk", bit)

time: 58.8 us -> 58.7 us (level)
  waiting for transfers between devices: 13.6 us -> 14.2 us
  transfers between devices with their start and end apart: 17 -> 17, of which waited for: 5 -> 6; matrix products, arithmetic and copies ran while one was open for 4% -> 4% of each run, Pallas kernels for 20% -> 20%
where the time goes in v6:
time: 58.7 us; the launch traced here: 58.4 us
  starting transfers between devices  21.3 us (36%)
  Pallas kernels  19.1 us (33%)
  waiting for transfers between devices  14.2 us (24%)
  local copies, waits for them, and re-layouts  2.33 us (4%)
  between operations  0.8 us (1%)
  other arithmetic  0.79 us (1%)
    ppermute x16, starting transfers between devices, xor_permute(): return lax.ppermute(x, axis, [(i, i ^ bit) for i in range(count)])  15.5 us
    ppermute x16, waiting for transfers between devices, xor_permute(): return lax.ppermute(x, axis, [(i, i ^ bit) for i in range(count)])  13.7 us
    pallas_call x1, Pallas kernels, shards(): pl.pallas_call(functools.partial(own_kernel, slot_count, per_peer, half),...  7.11 us
    all_to_all x1, starting transfers between devices, shards(): lax.all_to_all(outgoing.reshape(sub_count * blk_half, rows, LANES), ('sub...  5.8 us
    pallas_call x1, Pallas kernels, shards(): pl.pallas_call(functools.partial(ghost_kernel, half), out_shape=[pltpu.VM...  5.74 us
    pallas_call x1, Pallas kernels, shards(): pl.pallas_call(terms_kernel, out_shape=jax.ShapeDtypeStruct((group_size,...  2.97 us
    unnamed x14, local copies, waits for them, and re-layouts  2.13 us
    pallas_call x1, Pallas kernels, shards(): pl.pallas_call(functools.partial(pick_kernel, per_peer, half), out_shape=...  1.72 us
  transfers between devices with their start and end apart: 17, of which 6 were waited for; matrix products, arithmetic and copies ran while one was open for 4% of the time, Pallas kernels for 20%

profile of v6, /device:TPU:0, one launch (start us, length us, event | category | flops | bytes accessed | tf_op | source)
XLA Modules:
  0.0 58.4 jit_solution(13499131623621223616)
XLA Ops:
  0.6 3.0 %collective-permute-start.7 = (s32[1,126]{1,0:T(1,128)}, s32[1,126]{1,0:T(1,128)S(1)}, u32[]{:S(2)}, u32[]{:S(2)}) collective-permute-start(s32[1,126]{1,0:T(1,128)} %fetch_ref.1), channel_id=1, source_target_pairs={{0,4},{4,0},{8,12},{12,8},{16,20},{20,16},{24,28},{28,24},{1,5},{5... | collective-permute-start | bytes 1520 | tf_op jit(solution)/shard_map/ppermute | solution.py:27
  3.7 1.5 %collective-permute-start.9 = (s32[1,126]{1,0:T(1,128)}, s32[1,126]{1,0:T(1,128)S(1)}, u32[]{:S(2)}, u32[]{:S(2)}) collective-permute-start(s32[1,126]{1,0:T(1,128)} %fetch_ref.1), channel_id=1, source_target_pairs={{0,12},{4,8},{8,4},{12,0},{16,28},{20,24},{24,20},{28,16},{1,13},{... | collective-permute-start | bytes 1520 | tf_op jit(solution)/shard_map/ppermute | solution.py:27
  5.2 1.9 %collective-permute-start = (bf16[24,16,128]{2,1,0:T(8,128)(2,1)}, bf16[24,16,128]{2,1,0:T(8,128)(2,1)S(1)}, u32[]{:S(2)}, u32[]{:S(2)}) collective-permute-start(bf16[24,16,128]{2,1,0:T(8,128)(2,1)} %param.5), channel_id=1, source_target_pairs={{0,2},{1,3},{2,0},{3,1},{4,6},{5,7},{6,4},{7,5},{8,10},{9,11},{10,... | collective-permute-start | bytes 294920 | tf_op jit(solution)/shard_map/ppermute | solution.py:27
  7.2 0.9 %constant_dynamic-update-slice_fusion.8 = bf16[193,16,128]{2,1,0:T(8,128)(2,1)S(1)} fusion(bf16[24,16,128]{2,1,0:T(8,128)(2,1)} %param.5), kind=kLoop, calls=%fused_computation.10 | loop fusion | bytes 196608
  8.2 2.6 %collective-permute-start.3 = (bf16[24,16,128]{2,1,0:T(8,128)(2,1)}, bf16[24,16,128]{2,1,0:T(8,128)(2,1)S(1)}, u32[]{:S(2)}, u32[]{:S(2)}) collective-permute-start(bf16[24,16,128]{2,1,0:T(8,128)(2,1)} %param.5), channel_id=1, source_target_pairs={{0,16},{4,20},{8,24},{12,28},{16,0},{20,4},{24,8},{28,12},{1,17},{... | collective-permute-start | bytes 294920 | tf_op jit(solution)/shard_map/ppermute | solution.py:27
  10.9 5.4 %collective-permute-done.3 = bf16[24,16,128]{2,1,0:T(8,128)(2,1)S(1)} collective-permute-done((bf16[24,16,128]{2,1,0:T(8,128)(2,1)}, bf16[24,16,128]{2,1,0:T(8,128)(2,1)S(1)}, u32[]{:S(2)}, u32[]{:S(2)}) %collective-permute-start.3) | collective-permute-done | bytes 98336 | tf_op jit(solution)/shard_map/ppermute | solution.py:27
  16.4 0.5 collective-permute-start.4
  17.1 4.5 %collective-permute-done.4 = bf16[24,16,128]{2,1,0:T(8,128)(2,1)S(1)} collective-permute-done((bf16[24,16,128]{2,1,0:T(8,128)(2,1)S(1)}, bf16[24,16,128]{2,1,0:T(8,128)(2,1)S(1)}, u32[]{:S(2)}, u32[]{:S(2)}) %collective-permute-start.4) | collective-permute-done | bytes 98336 | tf_op jit(solution)/shard_map/ppermute | solution.py:27
  21.7 1.2 %collective-permute-done.6 = bf16[24,16,128]{2,1,0:T(8,128)(2,1)S(1)} collective-permute-done((bf16[24,16,128]{2,1,0:T(8,128)(2,1)S(1)}, bf16[24,16,128]{2,1,0:T(8,128)(2,1)S(1)}, u32[]{:S(2)}, u32[]{:S(2)}) %collective-permute-start.6) | collective-permute-done | bytes 98336 | tf_op jit(solution)/shard_map/ppermute | solution.py:27
  22.9 1.7 %pick.1 = (bf16[36,16,128]{2,1,0:T(8,128)(2,1)}, bf16[36,16,128]{2,1,0:T(8,128)(2,1)}, bf16[36,16,128]{2,1,0:T(8,128)(2,1)}) custom-call(s32[2]{0:T(128)S(1)} %pad_add_fusion.1.here, s32[3,7]{1,0:T(4,128)S(1)} %slice.3.owner_ref, s32[3,126]{1,0:T(4,128)S(1)} %get-tuple-element.48.place_ref, bf16[193,16,128]{2,1,0:T(8,128)(2,1)S(1)} %constant_dynamic-update-slice_fusion.table_ref), custom_call_target="tpu_custom_call" | custom-call | tf_op jit(solution)/shard_map/pick/pallas_call | solution.py:415
  24.6 1.5 %collective-permute-start.10 = (bf16[36,16,128]{2,1,0:T(8,128)(2,1)}, bf16[36,16,128]{2,1,0:T(8,128)(2,1)S(1)}, u32[]{:S(2)}, u32[]{:S(2)}) collective-permute-start(bf16[36,16,128]{2,1,0:T(8,128)(2,1)} %get-tuple-element.40), channel_id=1, source_target_pairs={{0,4},{4,0},{8,12},{12,8},{16,20},{20,16},{24,28},{28,24},{1,5},{5... | collective-permute-start | bytes 442376 | tf_op jit(solution)/shard_map/ppermute | solution.py:27
  26.1 0.8 %collective-permute-start.11 = (bf16[36,16,128]{2,1,0:T(8,128)(2,1)}, bf16[36,16,128]{2,1,0:T(8,128)(2,1)S(1)}, u32[]{:S(2)}, u32[]{:S(2)}) collective-permute-start(bf16[36,16,128]{2,1,0:T(8,128)(2,1)} %get-tuple-element.41), channel_id=1, source_target_pairs={{0,8},{4,12},{8,0},{12,4},{16,24},{20,28},{24,16},{28,20},{1,9},{5... | collective-permute-start | bytes 442376 | tf_op jit(solution)/shard_map/ppermute | solution.py:27
  26.9 1.2 %collective-permute-start.12 = (bf16[36,16,128]{2,1,0:T(8,128)(2,1)}, bf16[36,16,128]{2,1,0:T(8,128)(2,1)}, u32[]{:S(2)}, u32[]{:S(2)}) collective-permute-start(bf16[36,16,128]{2,1,0:T(8,128)(2,1)} %get-tuple-element.42), channel_id=1, source_target_pairs={{0,12},{4,8},{8,4},{12,0},{16,28},{20,24},{24,20},{28,16},{1,13},{... | collective-permute-start | bytes 442376 | tf_op jit(solution)/shard_map/ppermute | solution.py:27
  28.3 1.2 %prep.1 = (s32[288]{0:T(512)S(1)}, s32[1,288]{1,0:T(1,128)S(1)}, s32[288]{0:T(512)S(1)}, s32[288]{0:T(512)S(1)}, s32[288]{0:T(512)S(1)}, /*index=5*/s32[288]{0:T...) custom-call(s32[2]{0:T(128)S(1)} %pad_add_fusion.1.here, ...), custom_call_target="tpu_custom_call" | custom-call | tf_op jit(solution)/shard_map/prep/pallas_call | solution.py:429
  29.5 7.1 %own.1 = (bf16[288,16,128]{2,1,0:T(8,128)(2,1)S(1)}, f32[24,1,128]{2,1,0:T(1,128)S(1)}, bf16[288,16,128]{2,1,0:T(8,128)(2,1)S(1)}, bf16[320,288]{1,0:T(8,128)(2,...) custom-call(s32[288]{0:T(512)S(1)} %get-tuple-element.29.place, ...), custom_call_target="tpu_custom_call" | custom-call | tf_op jit(solution)/shard_map/own/pallas_call | solution.py:450
  36.6 5.7 %ghost.1 = (bf16[288,16,128]{2,1,0:T(8,128)(2,1)S(1)}, bf16[8,2,40,128]{3,2,1,0:T(8,128)(2,1)}) custom-call(s32[288]{0:T(512)S(1)} %get-tuple-element.25.slots, s32[288]{0:T(512)S(1)} %get-tuple-element.26.entries, s32[288]{0:T(512)S(1)} %get-tuple-element.27.tiles, s32[8,128]{1,0:T(8,128)S(1)} %get-tuple-element.28.counts_ref, ...), custom_call_target="tpu_custom_call", output_to_operand_aliasing={{0}: (10, {})} | custom-call | tf_op jit(solution)/shard_map/ghost/pallas_call | solution.py:471
  42.4 5.8 %all-to-all-start = ((bf16[16,40,128]{2,1,0:T(8,128)(2,1)}), bf16[16,40,128]{2,1,0:T(8,128)(2,1)S(1)}, u32[]{:S(2)}, u32[]{:S(2)}) async-start(bf16[16,40,128]{2,1,0:T(8,128)(2,1)} %bitcast.4), calls=%async_computation | async-start | bytes 327680 | tf_op jit(solution)/shard_map/all_to_all | solution.py:497
  48.2 3.0 %terms.1 = bf16[96,256]{1,0:T(8,128)(2,1)S(1)} custom-call(s32[288]{0:T(512)S(1)} %get-tuple-element.44.slots, s32[8,128]{1,0:T(8,128)S(1)} %get-tuple-element.28.counts_ref, s32[1,288]{1,0:T(1,128)S(1)} %get-tuple-element.45.row_ref, bf16[288,16,128]{2,1,0:T(8,128)(2,1)S(1)} %get-tuple-element.43.prolong_ref, ...), custom_call_target="tpu_custom_call" | custom-call | tf_op jit(solution)/shard_map/terms/pallas_call | solution.py:502
  51.2 2.0 %collective-permute-start.13 = (bf16[96,256]{1,0:T(8,128)(2,1)S(1)}, bf16[96,256]{1,0:T(8,128)(2,1)S(1)}, u32[]{:S(2)}, u32[]{:S(2)}) collective-permute-start(bf16[96,256]{1,0:T(8,128)(2,1)S(1)} %terms.1), channel_id=1, source_target_pairs={{0,2},{1,3},{2,0},{3,1},{4,6},{5,7},{6,4},{7,5},{8,10},{9,11},{10,... | collective-permute-start | bytes 147464 | tf_op jit(solution)/shard_map/ppermute | solution.py:27
  53.1 2.4 %collective-permute-done.13 = bf16[96,256]{1,0:T(8,128)(2,1)S(1)} collective-permute-done((bf16[96,256]{1,0:T(8,128)(2,1)S(1)}, bf16[96,256]{1,0:T(8,128)(2,1)S(1)}, u32[]{:S(2)}, u32[]{:S(2)}) %collective-permute-start.13) | collective-permute-done | bytes 49184 | tf_op jit(solution)/shard_map/ppermute | solution.py:27
  55.6 0.5 all-to-all-done.incoming_ref
  56.1 0.3 target.1
  56.5 1.0 %copy.18 = bf16[24,12,16,128]{3,2,1,0:T(8,128)(2,1)} copy(bf16[24,12,16,128]{3,2,1,0:T(8,128)(2,1)S(1)} %bitcast.5) | data formatting | bytes 2359296
  57.8 0.7 %add_add_fusion = f32[96,256]{1,0:T(8,128)} fusion(bf16[96,256]{1,0:T(8,128)(2,1)S(1)} %collective-permute-done.15, bf16[96,256]{1,0:T(8,128)(2,1)S(1)} %target.1, bf16[96,256]{1,0:T(8,128)(2,1)S(1)} %collective-permute-done.14, bf16[96,256]{1,0:T(8,128)(2,1)S(1)} %add_convert_fusion), kind=kLoop, calls=%fused_computation | loop fusion | flops 172032 | bytes 294912 | tf_op jit(solution)/shard_map/add | solution.py:527
  (37 shorter events, 1.2 us)
Async XLA Ops:
  0.6 7.6 %collective-permute-start.7 = (s32[1,126]{1,0:T(1,128)}, s32[1,126]{1,0:T(1,128)S(1)}, u32[]{:S(2)}, u32[]{:S(2)}) collective-permute-start(s32[1,126]{1,0:T(1,128)} %fetch_ref.1), channel_id=1, source_target_pairs={{0,4},{4,0},{8,12},{12,8},{16,20},{20,16},{24,28},{28,24},{1,5},{5... | collective-permute-start | bytes 1520 | tf_op jit(solution)/shard_map/ppermute | solution.py:27
  3.7 7.1 %collective-permute-start.9 = (s32[1,126]{1,0:T(1,128)}, s32[1,126]{1,0:T(1,128)S(1)}, u32[]{:S(2)}, u32[]{:S(2)}) collective-permute-start(s32[1,126]{1,0:T(1,128)} %fetch_ref.1), channel_id=1, source_target_pairs={{0,12},{4,8},{8,4},{12,0},{16,28},{20,24},{24,20},{28,16},{1,13},{... | collective-permute-start | bytes 1520 | tf_op jit(solution)/shard_map/ppermute | solution.py:27
  5.2 5.6 %collective-permute-start.8 = (s32[1,126]{1,0:T(1,128)}, s32[1,126]{1,0:T(1,128)S(1)}, u32[]{:S(2)}, u32[]{:S(2)}) collective-permute-start(s32[1,126]{1,0:T(1,128)} %fetch_ref.1), channel_id=1, source_target_pairs={{0,8},{4,12},{8,0},{12,4},{16,24},{20,28},{24,16},{28,20},{1,9},{5... | collective-permute-start | bytes 1520 | tf_op jit(solution)/shard_map/ppermute | solution.py:27
  5.2 11.8 %collective-permute-start.1 = (bf16[24,16,128]{2,1,0:T(8,128)(2,1)}, bf16[24,16,128]{2,1,0:T(8,128)(2,1)S(1)}, u32[]{:S(2)}, u32[]{:S(2)}) collective-permute-start(bf16[24,16,128]{2,1,0:T(8,128)(2,1)} %param.5), channel_id=1, source_target_pairs={{0,1},{1,0},{2,3},{3,2},{4,5},{5,4},{6,7},{7,6},{8,9},{9,8},{10,11... | collective-permute-start | bytes 294920 | tf_op jit(solution)/shard_map/ppermute | solution.py:27
  5.2 11.6 %collective-permute-start = (bf16[24,16,128]{2,1,0:T(8,128)(2,1)}, bf16[24,16,128]{2,1,0:T(8,128)(2,1)S(1)}, u32[]{:S(2)}, u32[]{:S(2)}) collective-permute-start(bf16[24,16,128]{2,1,0:T(8,128)(2,1)} %param.5), channel_id=1, source_target_pairs={{0,2},{1,3},{2,0},{3,1},{4,6},{5,7},{6,4},{7,5},{8,10},{9,11},{10,... | collective-permute-start | bytes 294920 | tf_op jit(solution)/shard_map/ppermute | solution.py:27
  7.2 20.9 %copy-start.1 = (s32[24,12]{0,1:T(8,128)S(1)}, s32[24,12]{0,1:T(8,128)}, u32[]{:S(2)}) copy-start(s32[24,12]{0,1:T(8,128)} %param.6) | copy-start | bytes 3460
  7.2 21.1 %copy-start = (s32[1,126]{1,0:T(1,128)S(1)}, s32[1,126]{1,0:T(1,128)}, u32[]{:S(2)}) copy-start(s32[1,126]{1,0:T(1,128)} %fetch_ref.1) | copy-start | bytes 1516
  8.2 8.2 %collective-permute-start.3 = (bf16[24,16,128]{2,1,0:T(8,128)(2,1)}, bf16[24,16,128]{2,1,0:T(8,128)(2,1)S(1)}, u32[]{:S(2)}, u32[]{:S(2)}) collective-permute-start(bf16[24,16,128]{2,1,0:T(8,128)(2,1)} %param.5), channel_id=1, source_target_pairs={{0,16},{4,20},{8,24},{12,28},{16,0},{20,4},{24,8},{28,12},{1,17},{... | collective-permute-start | bytes 294920 | tf_op jit(solution)/shard_map/ppermute | solution.py:27
  16.4 5.3 %collective-permute-start.5 = (bf16[24,16,128]{2,1,0:T(8,128)(2,1)S(1)}, bf16[24,16,128]{2,1,0:T(8,128)(2,1)S(1)}, u32[]{:S(2)}, u32[]{:S(2)}) collective-permute-start(bf16[24,16,128]{2,1,0:T(8,128)(2,1)S(1)} %collective-permute-done.3), channel_id=1, source_target_pairs={{0,1},{1,0},{2,3},{3,2},{4,5},{5,4},{6,7},{7,6},{8,9},{9,8},{10,11... | collective-permute-start | bytes 294920 | tf_op jit(solution)/shard_map/ppermute | solution.py:27
  16.4 5.2 %collective-permute-start.4 = (bf16[24,16,128]{2,1,0:T(8,128)(2,1)S(1)}, bf16[24,16,128]{2,1,0:T(8,128)(2,1)S(1)}, u32[]{:S(2)}, u32[]{:S(2)}) collective-permute-start(bf16[24,16,128]{2,1,0:T(8,128)(2,1)S(1)} %collective-permute-done.3), channel_id=1, source_target_pairs={{0,2},{1,3},{2,0},{3,1},{4,6},{5,7},{6,4},{7,5},{8,10},{9,11},{10,... | collective-permute-start | bytes 294920 | tf_op jit(solution)/shard_map/ppermute | solution.py:27
  16.8 4.8 %collective-permute-start.2 = (bf16[24,16,128]{2,1,0:T(8,128)(2,1)S(1)}, bf16[24,16,128]{2,1,0:T(8,128)(2,1)S(1)}, u32[]{:S(2)}, u32[]{:S(2)}) collective-permute-start(bf16[24,16,128]{2,1,0:T(8,128)(2,1)S(1)} %collective-permute-done), channel_id=1, source_target_pairs={{0,1},{1,0},{2,3},{3,2},{4,5},{5,4},{6,7},{7,6},{8,9},{9,8},{10,11... | collective-permute-start | bytes 294920 | tf_op jit(solution)/shard_map/ppermute | solution.py:27
  21.6 1.3 %collective-permute-start.6 = (bf16[24,16,128]{2,1,0:T(8,128)(2,1)S(1)}, bf16[24,16,128]{2,1,0:T(8,128)(2,1)S(1)}, u32[]{:S(2)}, u32[]{:S(2)}) collective-permute-start(bf16[24,16,128]{2,1,0:T(8,128)(2,1)S(1)} %collective-permute-done.4), channel_id=1, source_target_pairs={{0,1},{1,0},{2,3},{3,2},{4,5},{5,4},{6,7},{7,6},{8,9},{9,8},{10,11... | collective-permute-start | bytes 294920 | tf_op jit(solution)/shard_map/ppermute | solution.py:27
  24.6 12.0 %collective-permute-start.10 = (bf16[36,16,128]{2,1,0:T(8,128)(2,1)}, bf16[36,16,128]{2,1,0:T(8,128)(2,1)S(1)}, u32[]{:S(2)}, u32[]{:S(2)}) collective-permute-start(bf16[36,16,128]{2,1,0:T(8,128)(2,1)} %get-tuple-element.40), channel_id=1, source_target_pairs={{0,4},{4,0},{8,12},{12,8},{16,20},{20,16},{24,28},{28,24},{1,5},{5... | collective-permute-start | bytes 442376 | tf_op jit(solution)/shard_map/ppermute | solution.py:27
  26.1 10.5 %collective-permute-start.11 = (bf16[36,16,128]{2,1,0:T(8,128)(2,1)}, bf16[36,16,128]{2,1,0:T(8,128)(2,1)S(1)}, u32[]{:S(2)}, u32[]{:S(2)}) collective-permute-start(bf16[36,16,128]{2,1,0:T(8,128)(2,1)} %get-tuple-element.41), channel_id=1, source_target_pairs={{0,8},{4,12},{8,0},{12,4},{16,24},{20,28},{24,16},{28,20},{1,9},{5... | collective-permute-start | bytes 442376 | tf_op jit(solution)/shard_map/ppermute | solution.py:27
  26.9 9.7 %collective-permute-start.12 = (bf16[36,16,128]{2,1,0:T(8,128)(2,1)}, bf16[36,16,128]{2,1,0:T(8,128)(2,1)}, u32[]{:S(2)}, u32[]{:S(2)}) collective-permute-start(bf16[36,16,128]{2,1,0:T(8,128)(2,1)} %get-tuple-element.42), channel_id=1, source_target_pairs={{0,12},{4,8},{8,4},{12,0},{16,28},{20,24},{24,20},{28,16},{1,13},{... | collective-permute-start | bytes 442376 | tf_op jit(solution)/shard_map/ppermute | solution.py:27
  42.4 13.7 %all-to-all-start = ((bf16[16,40,128]{2,1,0:T(8,128)(2,1)}), bf16[16,40,128]{2,1,0:T(8,128)(2,1)S(1)}, u32[]{:S(2)}, u32[]{:S(2)}) async-start(bf16[16,40,128]{2,1,0:T(8,128)(2,1)} %bitcast.4), calls=%async_computation | async-start | bytes 327680 | tf_op jit(solution)/shard_map/all_to_all | solution.py:497
  51.2 4.4 %collective-permute-start.13 = (bf16[96,256]{1,0:T(8,128)(2,1)S(1)}, bf16[96,256]{1,0:T(8,128)(2,1)S(1)}, u32[]{:S(2)}, u32[]{:S(2)}) collective-permute-start(bf16[96,256]{1,0:T(8,128)(2,1)S(1)} %terms.1), channel_id=1, source_target_pairs={{0,2},{1,3},{2,0},{3,1},{4,6},{5,7},{6,4},{7,5},{8,10},{9,11},{10,... | collective-permute-start | bytes 147464 | tf_op jit(solution)/shard_map/ppermute | solution.py:27
  55.5 2.0 %collective-permute-start.14 = (bf16[96,256]{1,0:T(8,128)(2,1)S(1)}, bf16[96,256]{1,0:T(8,128)(2,1)S(1)}, u32[]{:S(2)}, u32[]{:S(2)}) collective-permute-start(bf16[96,256]{1,0:T(8,128)(2,1)S(1)} %add_convert_fusion), channel_id=1, source_target_pairs={{0,1},{1,0},{2,3},{3,2},{4,5},{5,4},{6,7},{7,6},{8,9},{9,8},{10,11... | collective-permute-start | bytes 147464 | tf_op jit(solution)/shard_map/ppermute | solution.py:27
  56.5 1.3 %collective-permute-start.15 = (bf16[96,256]{1,0:T(8,128)(2,1)S(1)}, bf16[96,256]{1,0:T(8,128)(2,1)S(1)}, u32[]{:S(2)}, u32[]{:S(2)}) collective-permute-start(bf16[96,256]{1,0:T(8,128)(2,1)S(1)} %target.1), channel_id=1, source_target_pairs={{0,1},{1,0},{2,3},{3,2},{4,5},{5,4},{6,7},{7,6},{8,9},{9,8},{10,11... | collective-permute-start | bytes 147464 | tf_op jit(solution)/shard_map/ppermute | solution.py:27

commit v7 on v6

--- a/solution.py
+++ b/solution.py
@@ -288,14 +288,17 @@
 
 def terms_kernel(slots, counts_ref, row_ref, prolong_ref, product_ref, sums_ref, terms_ref):
     total, mode_count, tile_rows = prolong_ref.shape
-    batch = 6 * BATCH
+    batch = 7 * BATCH
     spread, lane_block = term_constants(batch, mode_count)
     terms_ref[...] = jnp.zeros_like(terms_ref)
 
     @pl.loop(0, (counts_ref[2, 0] + batch - 1) // batch)
     def _(step):
         first = step * batch
-        slot = [slots[jnp.minimum(first + i, total - 1)] for i in range(batch)]
+        at = [first + i for i in range(batch)]
+        if total % batch:
+            at = [jnp.minimum(i, total - 1) for i in at]
+        slot = [slots[i] for i in at]
         parts = [(prolong_ref[f], product_ref[f]) for f in slot]
         terms_ref[pl.ds(pl.multiple_of(first, BATCH), batch), :] = terms_of(parts, spread, lane_block)
 
@@ -504,7 +507,7 @@
         out_shape=jax.ShapeDtypeStruct((group_size, width), jnp.bfloat16),
         in_specs=[SMEM] * 2 + [VMEM] * 3,
         out_specs=VMEM,
-        scratch_shapes=[pltpu.VMEM((slot_total + 6 * BATCH, width), jnp.float32)],
+        scratch_shapes=[pltpu.VMEM((slot_total + 7 * BATCH, width), jnp.float32)],
         name="terms",
         compiler_params=PARAMS,
     )(own_slot, counts, own_row, finished, product)

time: 58.7 us -> 58.7 us (level)
    all_to_all x1, waiting for transfers between devices: 0.48 us -> 1.18 us  [shards(): lax.all_to_all(outgoing.reshape(sub_count * blk_half, rows, LANES), ('sub...]
  transfers between devices with their start and end apart: 17 -> 17, of which waited for: 6 -> 6; matrix products, arithmetic and copies ran while one was open for 4% -> 4% of each run, Pallas kernels for 20% -> 19%
where the time goes in v7:
time: 58.7 us; the launch traced here: 58.4 us
  starting transfers between devices  21.3 us (36%)
  Pallas kernels  18.6 us (32%)
  waiting for transfers between devices  14.7 us (25%)
  local copies, waits for them, and re-layouts  2.34 us (4%)
  between operations  0.81 us (1%)
  other arithmetic  0.79 us (1%)
    ppermute x16, starting transfers between devices, xor_permute(): return lax.ppermute(x, axis, [(i, i ^ bit) for i in range(count)])  15.5 us
    ppermute x16, waiting for transfers between devices, xor_permute(): return lax.ppermute(x, axis, [(i, i ^ bit) for i in range(count)])  13.5 us
    pallas_call x1, Pallas kernels, shards(): pl.pallas_call(functools.partial(own_kernel, slot_count, per_peer, half),...  7.11 us
    all_to_all x1, starting transfers between devices, shards(): lax.all_to_all(outgoing.reshape(sub_count * blk_half, rows, LANES), ('sub...  5.8 us
    pallas_call x1, Pallas kernels, shards(): pl.pallas_call(functools.partial(ghost_kernel, half), out_shape=[pltpu.VM...  5.74 us
    pallas_call x1, Pallas kernels, shards(): pl.pallas_call(terms_kernel, out_shape=jax.ShapeDtypeStruct((group_size,...  2.49 us
    unnamed x14, local copies, waits for them, and re-layouts  2.14 us
    pallas_call x1, Pallas kernels, shards(): pl.pallas_call(functools.partial(pick_kernel, per_peer, half), out_shape=...  1.72 us
  transfers between devices with their start and end apart: 17, of which 6 were waited for; matrix products, arithmetic and copies ran while one was open for 4% of the time, Pallas kernels for 19%

profile of v7, /device:TPU:0, one launch (start us, length us, event | category | flops | bytes accessed | tf_op | source)
XLA Modules:
  0.0 58.4 jit_solution(17411707889432049075)
XLA Ops:
  0.6 3.0 %collective-permute-start.7 = (s32[1,126]{1,0:T(1,128)}, s32[1,126]{1,0:T(1,128)S(1)}, u32[]{:S(2)}, u32[]{:S(2)}) collective-permute-start(s32[1,126]{1,0:T(1,128)} %fetch_ref.1), channel_id=1, source_target_pairs={{0,4},{4,0},{8,12},{12,8},{16,20},{20,16},{24,28},{28,24},{1,5},{5... | collective-permute-start | bytes 1520 | tf_op jit(solution)/shard_map/ppermute | solution.py:27
  3.7 1.5 %collective-permute-start.9 = (s32[1,126]{1,0:T(1,128)}, s32[1,126]{1,0:T(1,128)S(1)}, u32[]{:S(2)}, u32[]{:S(2)}) collective-permute-start(s32[1,126]{1,0:T(1,128)} %fetch_ref.1), channel_id=1, source_target_pairs={{0,12},{4,8},{8,4},{12,0},{16,28},{20,24},{24,20},{28,16},{1,13},{... | collective-permute-start | bytes 1520 | tf_op jit(solution)/shard_map/ppermute | solution.py:27
  5.2 1.9 %collective-permute-start = (bf16[24,16,128]{2,1,0:T(8,128)(2,1)}, bf16[24,16,128]{2,1,0:T(8,128)(2,1)S(1)}, u32[]{:S(2)}, u32[]{:S(2)}) collective-permute-start(bf16[24,16,128]{2,1,0:T(8,128)(2,1)} %param.5), channel_id=1, source_target_pairs={{0,2},{1,3},{2,0},{3,1},{4,6},{5,7},{6,4},{7,5},{8,10},{9,11},{10,... | collective-permute-start | bytes 294920 | tf_op jit(solution)/shard_map/ppermute | solution.py:27
  7.2 0.9 %constant_dynamic-update-slice_fusion.8 = bf16[193,16,128]{2,1,0:T(8,128)(2,1)S(1)} fusion(bf16[24,16,128]{2,1,0:T(8,128)(2,1)} %param.5), kind=kLoop, calls=%fused_computation.10 | loop fusion | bytes 196608
  8.2 2.6 %collective-permute-start.3 = (bf16[24,16,128]{2,1,0:T(8,128)(2,1)}, bf16[24,16,128]{2,1,0:T(8,128)(2,1)S(1)}, u32[]{:S(2)}, u32[]{:S(2)}) collective-permute-start(bf16[24,16,128]{2,1,0:T(8,128)(2,1)} %param.5), channel_id=1, source_target_pairs={{0,16},{4,20},{8,24},{12,28},{16,0},{20,4},{24,8},{28,12},{1,17},{... | collective-permute-start | bytes 294920 | tf_op jit(solution)/shard_map/ppermute | solution.py:27
  10.9 5.4 %collective-permute-done.3 = bf16[24,16,128]{2,1,0:T(8,128)(2,1)S(1)} collective-permute-done((bf16[24,16,128]{2,1,0:T(8,128)(2,1)}, bf16[24,16,128]{2,1,0:T(8,128)(2,1)S(1)}, u32[]{:S(2)}, u32[]{:S(2)}) %collective-permute-start.3) | collective-permute-done | bytes 98336 | tf_op jit(solution)/shard_map/ppermute | solution.py:27
  16.4 0.5 collective-permute-start.4
  17.1 4.5 %collective-permute-done.4 = bf16[24,16,128]{2,1,0:T(8,128)(2,1)S(1)} collective-permute-done((bf16[24,16,128]{2,1,0:T(8,128)(2,1)S(1)}, bf16[24,16,128]{2,1,0:T(8,128)(2,1)S(1)}, u32[]{:S(2)}, u32[]{:S(2)}) %collective-permute-start.4) | collective-permute-done | bytes 98336 | tf_op jit(solution)/shard_map/ppermute | solution.py:27
  21.7 1.2 %collective-permute-done.6 = bf16[24,16,128]{2,1,0:T(8,128)(2,1)S(1)} collective-permute-done((bf16[24,16,128]{2,1,0:T(8,128)(2,1)S(1)}, bf16[24,16,128]{2,1,0:T(8,128)(2,1)S(1)}, u32[]{:S(2)}, u32[]{:S(2)}) %collective-permute-start.6) | collective-permute-done | bytes 98336 | tf_op jit(solution)/shard_map/ppermute | solution.py:27
  22.9 1.7 %pick.1 = (bf16[36,16,128]{2,1,0:T(8,128)(2,1)}, bf16[36,16,128]{2,1,0:T(8,128)(2,1)}, bf16[36,16,128]{2,1,0:T(8,128)(2,1)}) custom-call(s32[2]{0:T(128)S(1)} %pad_add_fusion.1.here, s32[3,7]{1,0:T(4,128)S(1)} %slice.3.owner_ref, s32[3,126]{1,0:T(4,128)S(1)} %get-tuple-element.48.place_ref, bf16[193,16,128]{2,1,0:T(8,128)(2,1)S(1)} %constant_dynamic-update-slice_fusion.table_ref), custom_call_target="tpu_custom_call" | custom-call | tf_op jit(solution)/shard_map/pick/pallas_call | solution.py:418
  24.6 1.5 %collective-permute-start.10 = (bf16[36,16,128]{2,1,0:T(8,128)(2,1)}, bf16[36,16,128]{2,1,0:T(8,128)(2,1)S(1)}, u32[]{:S(2)}, u32[]{:S(2)}) collective-permute-start(bf16[36,16,128]{2,1,0:T(8,128)(2,1)} %get-tuple-element.40), channel_id=1, source_target_pairs={{0,4},{4,0},{8,12},{12,8},{16,20},{20,16},{24,28},{28,24},{1,5},{5... | collective-permute-start | bytes 442376 | tf_op jit(solution)/shard_map/ppermute | solution.py:27
  26.1 0.8 %collective-permute-start.11 = (bf16[36,16,128]{2,1,0:T(8,128)(2,1)}, bf16[36,16,128]{2,1,0:T(8,128)(2,1)S(1)}, u32[]{:S(2)}, u32[]{:S(2)}) collective-permute-start(bf16[36,16,128]{2,1,0:T(8,128)(2,1)} %get-tuple-element.41), channel_id=1, source_target_pairs={{0,8},{4,12},{8,0},{12,4},{16,24},{20,28},{24,16},{28,20},{1,9},{5... | collective-permute-start | bytes 442376 | tf_op jit(solution)/shard_map/ppermute | solution.py:27
  26.9 1.2 %collective-permute-start.12 = (bf16[36,16,128]{2,1,0:T(8,128)(2,1)}, bf16[36,16,128]{2,1,0:T(8,128)(2,1)}, u32[]{:S(2)}, u32[]{:S(2)}) collective-permute-start(bf16[36,16,128]{2,1,0:T(8,128)(2,1)} %get-tuple-element.42), channel_id=1, source_target_pairs={{0,12},{4,8},{8,4},{12,0},{16,28},{20,24},{24,20},{28,16},{1,13},{... | collective-permute-start | bytes 442376 | tf_op jit(solution)/shard_map/ppermute | solution.py:27
  28.3 1.2 %prep.1 = (s32[288]{0:T(512)S(1)}, s32[1,288]{1,0:T(1,128)S(1)}, s32[288]{0:T(512)S(1)}, s32[288]{0:T(512)S(1)}, s32[288]{0:T(512)S(1)}, /*index=5*/s32[288]{0:T...) custom-call(s32[2]{0:T(128)S(1)} %pad_add_fusion.1.here, ...), custom_call_target="tpu_custom_call" | custom-call | tf_op jit(solution)/shard_map/prep/pallas_call | solution.py:432
  29.5 7.1 %own.1 = (bf16[288,16,128]{2,1,0:T(8,128)(2,1)S(1)}, f32[24,1,128]{2,1,0:T(1,128)S(1)}, bf16[288,16,128]{2,1,0:T(8,128)(2,1)S(1)}, bf16[320,288]{1,0:T(8,128)(2,...) custom-call(s32[288]{0:T(512)S(1)} %get-tuple-element.29.place, ...), custom_call_target="tpu_custom_call" | custom-call | tf_op jit(solution)/shard_map/own/pallas_call | solution.py:453
  36.6 5.7 %ghost.1 = (bf16[288,16,128]{2,1,0:T(8,128)(2,1)S(1)}, bf16[8,2,40,128]{3,2,1,0:T(8,128)(2,1)}) custom-call(s32[288]{0:T(512)S(1)} %get-tuple-element.25.slots, s32[288]{0:T(512)S(1)} %get-tuple-element.26.entries, s32[288]{0:T(512)S(1)} %get-tuple-element.27.tiles, s32[8,128]{1,0:T(8,128)S(1)} %get-tuple-element.28.counts_ref, ...), custom_call_target="tpu_custom_call", output_to_operand_aliasing={{0}: (10, {})} | custom-call | tf_op jit(solution)/shard_map/ghost/pallas_call | solution.py:474
  42.4 5.8 %all-to-all-start = ((bf16[16,40,128]{2,1,0:T(8,128)(2,1)}), bf16[16,40,128]{2,1,0:T(8,128)(2,1)S(1)}, u32[]{:S(2)}, u32[]{:S(2)}) async-start(bf16[16,40,128]{2,1,0:T(8,128)(2,1)} %bitcast.4), calls=%async_computation | async-start | bytes 327680 | tf_op jit(solution)/shard_map/all_to_all | solution.py:500
  48.2 2.5 %terms.1 = bf16[96,256]{1,0:T(8,128)(2,1)S(1)} custom-call(s32[288]{0:T(512)S(1)} %get-tuple-element.44.slots, s32[8,128]{1,0:T(8,128)S(1)} %get-tuple-element.28.counts_ref, s32[1,288]{1,0:T(1,128)S(1)} %get-tuple-element.45.row_ref, bf16[288,16,128]{2,1,0:T(8,128)(2,1)S(1)} %get-tuple-element.43.prolong_ref, ...), custom_call_target="tpu_custom_call" | custom-call | tf_op jit(solution)/shard_map/terms/pallas_call | solution.py:505
  50.7 2.0 %collective-permute-start.13 = (bf16[96,256]{1,0:T(8,128)(2,1)S(1)}, bf16[96,256]{1,0:T(8,128)(2,1)S(1)}, u32[]{:S(2)}, u32[]{:S(2)}) collective-permute-start(bf16[96,256]{1,0:T(8,128)(2,1)S(1)} %terms.1), channel_id=1, source_target_pairs={{0,2},{1,3},{2,0},{3,1},{4,6},{5,7},{6,4},{7,5},{8,10},{9,11},{10,... | collective-permute-start | bytes 147464 | tf_op jit(solution)/shard_map/ppermute | solution.py:27
  52.7 2.2 %collective-permute-done.13 = bf16[96,256]{1,0:T(8,128)(2,1)S(1)} collective-permute-done((bf16[96,256]{1,0:T(8,128)(2,1)S(1)}, bf16[96,256]{1,0:T(8,128)(2,1)S(1)}, u32[]{:S(2)}, u32[]{:S(2)}) %collective-permute-start.13) | collective-permute-done | bytes 49184 | tf_op jit(solution)/shard_map/ppermute | solution.py:27
  54.9 1.2 %all-to-all-done.incoming_ref = bf16[16,40,128]{2,1,0:T(8,128)(2,1)S(1)} async-done(((bf16[16,40,128]{2,1,0:T(8,128)(2,1)}), bf16[16,40,128]{2,1,0:T(8,128)(2,1)S(1)}, u32[]{:S(2)}, u32[]{:S(2)}) %all-to-all-start) | async-done | bytes 163872 | tf_op jit(solution)/shard_map/all_to_all | solution.py:500
  56.1 0.3 target.1
  56.5 1.0 %copy.18 = bf16[24,12,16,128]{3,2,1,0:T(8,128)(2,1)} copy(bf16[24,12,16,128]{3,2,1,0:T(8,128)(2,1)S(1)} %bitcast.5) | data formatting | bytes 2359296
  57.8 0.7 %add_add_fusion = f32[96,256]{1,0:T(8,128)} fusion(bf16[96,256]{1,0:T(8,128)(2,1)S(1)} %collective-permute-done.15, bf16[96,256]{1,0:T(8,128)(2,1)S(1)} %target.1, bf16[96,256]{1,0:T(8,128)(2,1)S(1)} %collective-permute-done.14, bf16[96,256]{1,0:T(8,128)(2,1)S(1)} %add_convert_fusion), kind=kLoop, calls=%fused_computation | loop fusion | flops 172032 | bytes 294912 | tf_op jit(solution)/shard_map/add | solution.py:530
  (37 shorter events, 1.2 us)
Async XLA Ops:
  0.6 7.6 %collective-permute-start.7 = (s32[1,126]{1,0:T(1,128)}, s32[1,126]{1,0:T(1,128)S(1)}, u32[]{:S(2)}, u32[]{:S(2)}) collective-permute-start(s32[1,126]{1,0:T(1,128)} %fetch_ref.1), channel_id=1, source_target_pairs={{0,4},{4,0},{8,12},{12,8},{16,20},{20,16},{24,28},{28,24},{1,5},{5... | collective-permute-start | bytes 1520 | tf_op jit(solution)/shard_map/ppermute | solution.py:27
  3.7 7.1 %collective-permute-start.9 = (s32[1,126]{1,0:T(1,128)}, s32[1,126]{1,0:T(1,128)S(1)}, u32[]{:S(2)}, u32[]{:S(2)}) collective-permute-start(s32[1,126]{1,0:T(1,128)} %fetch_ref.1), channel_id=1, source_target_pairs={{0,12},{4,8},{8,4},{12,0},{16,28},{20,24},{24,20},{28,16},{1,13},{... | collective-permute-start | bytes 1520 | tf_op jit(solution)/shard_map/ppermute | solution.py:27
  5.2 5.6 %collective-permute-start.8 = (s32[1,126]{1,0:T(1,128)}, s32[1,126]{1,0:T(1,128)S(1)}, u32[]{:S(2)}, u32[]{:S(2)}) collective-permute-start(s32[1,126]{1,0:T(1,128)} %fetch_ref.1), channel_id=1, source_target_pairs={{0,8},{4,12},{8,0},{12,4},{16,24},{20,28},{24,16},{28,20},{1,9},{5... | collective-permute-start | bytes 1520 | tf_op jit(solution)/shard_map/ppermute | solution.py:27
  5.2 11.8 %collective-permute-start.1 = (bf16[24,16,128]{2,1,0:T(8,128)(2,1)}, bf16[24,16,128]{2,1,0:T(8,128)(2,1)S(1)}, u32[]{:S(2)}, u32[]{:S(2)}) collective-permute-start(bf16[24,16,128]{2,1,0:T(8,128)(2,1)} %param.5), channel_id=1, source_target_pairs={{0,1},{1,0},{2,3},{3,2},{4,5},{5,4},{6,7},{7,6},{8,9},{9,8},{10,11... | collective-permute-start | bytes 294920 | tf_op jit(solution)/shard_map/ppermute | solution.py:27
  5.2 11.6 %collective-permute-start = (bf16[24,16,128]{2,1,0:T(8,128)(2,1)}, bf16[24,16,128]{2,1,0:T(8,128)(2,1)S(1)}, u32[]{:S(2)}, u32[]{:S(2)}) collective-permute-start(bf16[24,16,128]{2,1,0:T(8,128)(2,1)} %param.5), channel_id=1, source_target_pairs={{0,2},{1,3},{2,0},{3,1},{4,6},{5,7},{6,4},{7,5},{8,10},{9,11},{10,... | collective-permute-start | bytes 294920 | tf_op jit(solution)/shard_map/ppermute | solution.py:27
  7.2 20.9 %copy-start.1 = (s32[24,12]{0,1:T(8,128)S(1)}, s32[24,12]{0,1:T(8,128)}, u32[]{:S(2)}) copy-start(s32[24,12]{0,1:T(8,128)} %param.6) | copy-start | bytes 3460
  7.2 21.1 %copy-start = (s32[1,126]{1,0:T(1,128)S(1)}, s32[1,126]{1,0:T(1,128)}, u32[]{:S(2)}) copy-start(s32[1,126]{1,0:T(1,128)} %fetch_ref.1) | copy-start | bytes 1516
  8.2 8.2 %collective-permute-start.3 = (bf16[24,16,128]{2,1,0:T(8,128)(2,1)}, bf16[24,16,128]{2,1,0:T(8,128)(2,1)S(1)}, u32[]{:S(2)}, u32[]{:S(2)}) collective-permute-start(bf16[24,16,128]{2,1,0:T(8,128)(2,1)} %param.5), channel_id=1, source_target_pairs={{0,16},{4,20},{8,24},{12,28},{16,0},{20,4},{24,8},{28,12},{1,17},{... | collective-permute-start | bytes 294920 | tf_op jit(solution)/shard_map/ppermute | solution.py:27
  16.4 5.3 %collective-permute-start.5 = (bf16[24,16,128]{2,1,0:T(8,128)(2,1)S(1)}, bf16[24,16,128]{2,1,0:T(8,128)(2,1)S(1)}, u32[]{:S(2)}, u32[]{:S(2)}) collective-permute-start(bf16[24,16,128]{2,1,0:T(8,128)(2,1)S(1)} %collective-permute-done.3), channel_id=1, source_target_pairs={{0,1},{1,0},{2,3},{3,2},{4,5},{5,4},{6,7},{7,6},{8,9},{9,8},{10,11... | collective-permute-start | bytes 294920 | tf_op jit(solution)/shard_map/ppermute | solution.py:27
  16.4 5.2 %collective-permute-start.4 = (bf16[24,16,128]{2,1,0:T(8,128)(2,1)S(1)}, bf16[24,16,128]{2,1,0:T(8,128)(2,1)S(1)}, u32[]{:S(2)}, u32[]{:S(2)}) collective-permute-start(bf16[24,16,128]{2,1,0:T(8,128)(2,1)S(1)} %collective-permute-done.3), channel_id=1, source_target_pairs={{0,2},{1,3},{2,0},{3,1},{4,6},{5,7},{6,4},{7,5},{8,10},{9,11},{10,... | collective-permute-start | bytes 294920 | tf_op jit(solution)/shard_map/ppermute | solution.py:27
  16.8 4.8 %collective-permute-start.2 = (bf16[24,16,128]{2,1,0:T(8,128)(2,1)S(1)}, bf16[24,16,128]{2,1,0:T(8,128)(2,1)S(1)}, u32[]{:S(2)}, u32[]{:S(2)}) collective-permute-start(bf16[24,16,128]{2,1,0:T(8,128)(2,1)S(1)} %collective-permute-done), channel_id=1, source_target_pairs={{0,1},{1,0},{2,3},{3,2},{4,5},{5,4},{6,7},{7,6},{8,9},{9,8},{10,11... | collective-permute-start | bytes 294920 | tf_op jit(solution)/shard_map/ppermute | solution.py:27
  21.6 1.3 %collective-permute-start.6 = (bf16[24,16,128]{2,1,0:T(8,128)(2,1)S(1)}, bf16[24,16,128]{2,1,0:T(8,128)(2,1)S(1)}, u32[]{:S(2)}, u32[]{:S(2)}) collective-permute-start(bf16[24,16,128]{2,1,0:T(8,128)(2,1)S(1)} %collective-permute-done.4), channel_id=1, source_target_pairs={{0,1},{1,0},{2,3},{3,2},{4,5},{5,4},{6,7},{7,6},{8,9},{9,8},{10,11... | collective-permute-start | bytes 294920 | tf_op jit(solution)/shard_map/ppermute | solution.py:27
  24.6 12.0 %collective-permute-start.10 = (bf16[36,16,128]{2,1,0:T(8,128)(2,1)}, bf16[36,16,128]{2,1,0:T(8,128)(2,1)S(1)}, u32[]{:S(2)}, u32[]{:S(2)}) collective-permute-start(bf16[36,16,128]{2,1,0:T(8,128)(2,1)} %get-tuple-element.40), channel_id=1, source_target_pairs={{0,4},{4,0},{8,12},{12,8},{16,20},{20,16},{24,28},{28,24},{1,5},{5... | collective-permute-start | bytes 442376 | tf_op jit(solution)/shard_map/ppermute | solution.py:27
  26.1 10.5 %collective-permute-start.11 = (bf16[36,16,128]{2,1,0:T(8,128)(2,1)}, bf16[36,16,128]{2,1,0:T(8,128)(2,1)S(1)}, u32[]{:S(2)}, u32[]{:S(2)}) collective-permute-start(bf16[36,16,128]{2,1,0:T(8,128)(2,1)} %get-tuple-element.41), channel_id=1, source_target_pairs={{0,8},{4,12},{8,0},{12,4},{16,24},{20,28},{24,16},{28,20},{1,9},{5... | collective-permute-start | bytes 442376 | tf_op jit(solution)/shard_map/ppermute | solution.py:27
  26.9 9.7 %collective-permute-start.12 = (bf16[36,16,128]{2,1,0:T(8,128)(2,1)}, bf16[36,16,128]{2,1,0:T(8,128)(2,1)}, u32[]{:S(2)}, u32[]{:S(2)}) collective-permute-start(bf16[36,16,128]{2,1,0:T(8,128)(2,1)} %get-tuple-element.42), channel_id=1, source_target_pairs={{0,12},{4,8},{8,4},{12,0},{16,28},{20,24},{24,20},{28,16},{1,13},{... | collective-permute-start | bytes 442376 | tf_op jit(solution)/shard_map/ppermute | solution.py:27
  42.4 13.7 %all-to-all-start = ((bf16[16,40,128]{2,1,0:T(8,128)(2,1)}), bf16[16,40,128]{2,1,0:T(8,128)(2,1)S(1)}, u32[]{:S(2)}, u32[]{:S(2)}) async-start(bf16[16,40,128]{2,1,0:T(8,128)(2,1)} %bitcast.4), calls=%async_computation | async-start | bytes 327680 | tf_op jit(solution)/shard_map/all_to_all | solution.py:500
  50.7 4.2 %collective-permute-start.13 = (bf16[96,256]{1,0:T(8,128)(2,1)S(1)}, bf16[96,256]{1,0:T(8,128)(2,1)S(1)}, u32[]{:S(2)}, u32[]{:S(2)}) collective-permute-start(bf16[96,256]{1,0:T(8,128)(2,1)S(1)} %terms.1), channel_id=1, source_target_pairs={{0,2},{1,3},{2,0},{3,1},{4,6},{5,7},{6,4},{7,5},{8,10},{9,11},{10,... | collective-permute-start | bytes 147464 | tf_op jit(solution)/shard_map/ppermute | solution.py:27
  54.8 2.7 %collective-permute-start.14 = (bf16[96,256]{1,0:T(8,128)(2,1)S(1)}, bf16[96,256]{1,0:T(8,128)(2,1)S(1)}, u32[]{:S(2)}, u32[]{:S(2)}) collective-permute-start(bf16[96,256]{1,0:T(8,128)(2,1)S(1)} %add_convert_fusion), channel_id=1, source_target_pairs={{0,1},{1,0},{2,3},{3,2},{4,5},{5,4},{6,7},{7,6},{8,9},{9,8},{10,11... | collective-permute-start | bytes 147464 | tf_op jit(solution)/shard_map/ppermute | solution.py:27
  56.5 1.3 %collective-permute-start.15 = (bf16[96,256]{1,0:T(8,128)(2,1)S(1)}, bf16[96,256]{1,0:T(8,128)(2,1)S(1)}, u32[]{:S(2)}, u32[]{:S(2)}) collective-permute-start(bf16[96,256]{1,0:T(8,128)(2,1)S(1)} %target.1), channel_id=1, source_target_pairs={{0,1},{1,0},{2,3},{3,2},{4,5},{5,4},{6,7},{7,6},{8,9},{9,8},{10,11... | collective-permute-start | bytes 147464 | tf_op jit(solution)/shard_map/ppermute | solution.py:27
